TPU v7x, 32 devices: a whole 2x2x4 slice. The times are simulated.
32 devices in a mesh: blk: 4 (over y, x), ep: 8 (over z, core).
Axes of the slice: x: 2, y: 2, z: 4, core: 2. Of those that a mesh axis runs over, the one named last changes fastest.
Arguments:
- tokens: bfloat16 [4096, 1024], P(('blk', 'ep')), may hold values from -6 to 6
- expert_ids: int32 [4096, 6], P(('blk', 'ep')), may hold values from 0 to 63, all different within a row; in each aligned block of 128 rows (0 to 127, 128 to 255, ...) at most 16 rows name the same one
- route_weight: float32 [4096, 6], P(('blk', 'ep')), may hold values from 0.05 to 1
- gate_weight: bfloat16 [1024, 64, 768], P('blk', 'ep'), may hold values from -0.1875 to 0.1875
- up_weight: bfloat16 [1024, 64, 768], P('blk', 'ep'), may hold values from -0.1875 to 0.1875
- down_weight: bfloat16 [1024, 64, 768], P('blk', 'ep'), may hold values from -0.21875 to 0.21875
- out_grad: bfloat16 [4096, 1024], P(('blk', 'ep')), may hold values from -6 to 6
Outputs:
- layer_output: bfloat16 [4096, 1024], P(('blk', 'ep'))
- grad_tokens: float32 [4096, 1024], P(('blk', 'ep'))
- grad_route: float32 [4096, 6], P(('blk', 'ep'))
- grad_gate: float32 [1024, 64, 768], P('blk', 'ep')
- grad_up: float32 [1024, 64, 768], P('blk', 'ep')
- grad_down: float32 [1024, 64, 768], P('blk', 'ep')
Inputs may be any that keep to these rules, and one draw needn't show every extreme that they name: `expert_ids`: within the 128 tokens of one device, the 6 experts of a token differ, and no expert is named by more than 16 of them; in every draw some expert is named by exactly 16 tokens of some device.
All inputs are finite; a program needn't handle non-finite values.
Results may differ from a plain program's by a relative error of at most 0.008.
Values may be sent and summed in bfloat16 or wider, within the bound.
No kernel may reach another device: no remote copies, remote signals or barrier semaphores. Data moves between devices by JAX's collectives and lax.ppermute only.
A program may use at most 256 MiB of HBM per device.

v0:
```python
import jax
import jax.numpy as jnp
from jax import lax
from jax.sharding import PartitionSpec as P

EXPERTS = 64
CAP = 16


def expand_rows(routed, weights):
    return jnp.einsum("erd,def->erf", routed, weights, preferred_element_type=jnp.float32)


def contract_rows(inner, weights):
    return jnp.einsum("erf,def->erd", inner, weights, preferred_element_type=jnp.float32)


def outer_rows(routed, inner):
    return jnp.einsum("erd,erf->def", routed, inner, preferred_element_type=jnp.float32)


def body(tokens, expert_ids, route_weight, gate_weight, up_weight, down_weight, out_grad):
    tok_count, model_width = tokens.shape
    top_count = expert_ids.shape[1]
    experts = EXPERTS
    capacity = CAP
    flat_ids = expert_ids.reshape(-1)
    onehot = (flat_ids[:, None] == jnp.arange(experts, dtype=jnp.int32)[None, :]).astype(jnp.int32)
    slot_rank = jnp.sum((jnp.cumsum(onehot, axis=0) - 1) * onehot, axis=1)
    target = flat_ids * capacity + slot_rank
    repeated = jnp.repeat(tokens, top_count, axis=0)
    outgoing = jnp.zeros((experts * capacity, model_width), jnp.bfloat16).at[target].set(repeated)
    received = lax.all_to_all(
        outgoing.reshape(experts, capacity, model_width),
        "ep",
        split_axis=0,
        concat_axis=1,
        tiled=True,
    )
    gate_full, up_full, down_full = (
        lax.all_gather(gate_weight, "blk", axis=0, tiled=True),
        lax.all_gather(up_weight, "blk", axis=0, tiled=True),
        lax.all_gather(down_weight, "blk", axis=0, tiled=True),
    )
    gate_pre = expand_rows(received, gate_full)
    up_pre = expand_rows(received, up_full)
    gate_sig = jax.nn.sigmoid(gate_pre)
    hidden = (gate_pre * gate_sig * up_pre).astype(jnp.bfloat16)
    expert_out = contract_rows(hidden, down_full).astype(jnp.bfloat16)
    returned = lax.all_to_all(expert_out, "ep", split_axis=1, concat_axis=0, tiled=True)
    chosen = returned.reshape(experts * capacity, model_width)[target].reshape(
        tok_count, top_count, model_width
    )
    chosen_f32 = chosen.astype(jnp.float32)
    layer_output = jnp.sum(route_weight[:, :, None] * chosen_f32, axis=1).astype(jnp.bfloat16)
    grad_f32 = out_grad.astype(jnp.float32)
    grad_route = jnp.sum(chosen_f32 * grad_f32[:, None, :], axis=2)
    slot_grad = (route_weight[:, :, None] * grad_f32[:, None, :]).astype(jnp.bfloat16)
    grad_send = (
        jnp.zeros((experts * capacity, model_width), jnp.bfloat16)
        .at[target]
        .set(slot_grad.reshape(-1, model_width))
    )
    grad_recv = lax.all_to_all(
        grad_send.reshape(experts, capacity, model_width),
        "ep",
        split_axis=0,
        concat_axis=1,
        tiled=True,
    )
    down_summed = lax.psum_scatter(
        outer_rows(grad_recv, hidden).astype(jnp.bfloat16), "blk", scatter_dimension=0, tiled=True
    ).astype(jnp.float32)
    grad_hidden = expand_rows(grad_recv, down_full)
    gate_delta = (grad_hidden * up_pre * gate_sig * (1.0 + gate_pre * (1.0 - gate_sig))).astype(
        jnp.bfloat16
    )
    up_delta = (grad_hidden * gate_pre * gate_sig).astype(jnp.bfloat16)
    input_grad = (contract_rows(gate_delta, gate_full) + contract_rows(up_delta, up_full)).astype(
        jnp.bfloat16
    )
    grad_back = lax.all_to_all(input_grad, "ep", split_axis=1, concat_axis=0, tiled=True)
    picked_grad = grad_back.reshape(experts * capacity, model_width)[target].reshape(
        tok_count, top_count, model_width
    )
    grad_tokens = jnp.sum(picked_grad.astype(jnp.float32), axis=1)
    pair_summed = lax.psum_scatter(
        jnp.stack(
            [outer_rows(received, gate_delta), outer_rows(received, up_delta)], axis=1
        ).astype(jnp.bfloat16),
        "blk",
        scatter_dimension=0,
        tiled=True,
    ).astype(jnp.float32)
    grad_gate = pair_summed[:, 0]
    grad_up = pair_summed[:, 1]
    return (layer_output, grad_tokens, grad_route, grad_gate, grad_up, down_summed)


def solution(mesh):
    in_specs = (
        P(("blk", "ep"), None),
        P(("blk", "ep"), None),
        P(("blk", "ep"), None),
        P("blk", "ep", None),
        P("blk", "ep", None),
        P("blk", "ep", None),
        P(("blk", "ep"), None),
    )
    out_specs = (
        P(("blk", "ep"), None),
        P(("blk", "ep"), None),
        P(("blk", "ep"), None),
        P("blk", "ep", None),
        P("blk", "ep", None),
        P("blk", "ep", None),
    )
    return jax.shard_map(body, mesh=mesh, in_specs=in_specs, out_specs=out_specs, check_vma=False)
```

profile of v0, /device:TPU:0, one launch (start us, length us, event | category | flops | bytes accessed | tf_op | source)
XLA Modules:
  0.0 790.3 jit_solution(9528315452976201955)
XLA Ops:
  7.2 4.2 copy.50
  11.5 1.8 copy-done.4
  13.3 2.3 copy.51
  15.6 1.8 copy-done.5
  17.4 2.3 copy.52
  19.7 0.7 copy-done.8
  20.5 0.1 eq.25
  20.6 0.1 eq.29
  20.8 0.1 copy.45
  20.9 0.1 mul.82
  21.1 1.8 reduce-window.6
  22.9 0.3 slice_reduce_fusion
  23.2 0.3 broadcast_in_dim.2
  23.5 1.4 reshape.126
  24.9 0.1 fusion.6
  25.1 8.0 %scatter_custom_fusion = bf16[1024,1024]{1,0:T(8,128)(2,1)} fusion(s32[768]{0:T(1024)S(1)} %fusion.8, bf16[768,1024]{1,0:T(8,128)(2,1)} %reshape.126, bf16[]{:T(256)} %constant.7.clone.1), kind=kCustom, calls=%fused_computation.22 | custom fusion | bytes 2097664 | tf_op jit(solution)/shard_map/scatter | solution.py:32
  33.1 6.7 all-to-all-start
  39.9 2.5 mul.89
  42.4 3.1 mul.90
  45.5 0.1 copy.44
  45.6 0.1 mul.87
  45.8 9.6 %scatter_custom_fusion.1 = bf16[1024,1024]{1,0:T(8,128)(2,1)} fusion(s32[768]{0:T(1024)S(1)} %fusion.8, f32[768,1024]{1,0:T(8,128)S(1)} %mul.90, f32[768]{0:T(1024)S(1)} %mul.87, bf16[]{:T(256)} %constant.7.clone.1), kind=kCustom, calls=%fused_computation.19 | custom fusion | flops 1572864 | bytes 5246978 | tf_op jit(solution)/shard_map/scatter | solution.py:62
  55.4 33.6 %all-to-all-done = bf16[64,16,1024]{2,1,0:T(8,128)(2,1)} async-done(((bf16[64,16,1024]{2,1,0:T(8,128)(2,1)}), bf16[64,16,1024]{2,1,0:T(8,128)(2,1)}, u32[]{:S(2)}, u32[]{:S(2)}) %all-to-all-start) | async-done | bytes 2097184 | tf_op jit(solution)/shard_map/all_to_all | solution.py:33
  89.0 4.4 all-to-all-start.2
  93.3 0.3 reduce-scatter.5.cloned.1.call-start
  93.6 1.8 copy.49
  95.4 47.0 %all-to-all-done.2 = bf16[64,16,1024]{2,1,0:T(8,128)(2,1)} async-done(((bf16[64,16,1024]{2,1,0:T(8,128)(2,1)}), bf16[64,16,1024]{2,1,0:T(8,128)(2,1)}, u32[]{:S(2)}, u32[]{:S(2)}) %all-to-all-start.2) | async-done | bytes 2097184 | tf_op jit(solution)/shard_map/all_to_all | solution.py:64
  142.4 3.3 copy.56
  145.7 10.2 %fusion.9 = f32[8,128,768]{2,1,0:T(8,128)} fusion(bf16[8,128,1024]{2,1,0:T(8,128)(2,1)S(1)} %bitcast.68, bf16[1024,8,768]{2,0,1:T(8,128)(2,1)} %all-gather.4.cloned.1.call-done), kind=kOutput, calls=%fused_computation.36 | convolution fusion | flops 1610612736 | bytes 17825792 | tf_op jit(solution)/shard_map/erd,def->erf/dot_general | solution.py:11
  155.8 105.9 %all-gather.6.cloned.1.call-done = bf16[1024,8,768]{2,0,1:T(8,128)(2,1)} async-done(((bf16[256,8,768]{2,0,1:T(8,128)(2,1)}), bf16[1024,8,768]{2,0,1:T(8,128)(2,1)}) %all-gather.6.cloned.1.call-update) | async-done | bytes 12582928 | tf_op jit(solution)/shard_map/all_gather | solution.py:42
  261.7 8.1 %fusion.10 = f32[8,128,768]{2,1,0:T(8,128)} fusion(bf16[8,128,1024]{2,1,0:T(8,128)(2,1)S(1)} %bitcast.69, bf16[1024,8,768]{2,0,1:T(8,128)(2,1)} %all-gather.6.cloned.1.call-done), kind=kOutput, calls=%fused_computation.37 | convolution fusion | flops 1610612736 | bytes 17825792 | tf_op jit(solution)/shard_map/erd,def->erf/dot_general | solution.py:11
  269.8 116.3 %all-gather.8.cloned.1.call-done = bf16[1024,8,768]{2,0,1:T(8,128)(2,1)} async-done(((bf16[256,8,768]{2,0,1:T(8,128)(2,1)}), bf16[1024,8,768]{2,0,1:T(8,128)(2,1)}) %all-gather.8.cloned.1.call-update) | async-done | bytes 12582928 | tf_op jit(solution)/shard_map/all_gather | solution.py:43
  386.1 11.7 %multiply_convert_fusion = (bf16[8,128,768]{2,1,0:T(8,128)(2,1)}, bf16[8,128,768]{2,1,0:T(8,128)(2,1)}, bf16[8,128,768]{2,1,0:T(8,128)(2,1)S(1)}) fusion(f32[8,128,768]{2,1,0:T(8,128)} %fusion.9, f32[8,128,768]{2,1,0:T(8,128)} %fusion.10, bf16[8,128,1024]{2,1,0:T(8,128)(2,1)} %bitcast.73, bf16[1024,8,768]{2,0,1:T(8,128)(2,1)} %all-gather.8.cloned.1.call-done), kind=kOutput, calls=%fused_computation.13 | convolution fusion | flops 1623195648 | bytes 25690112 | tf_op jit(solution)/shard_map/erd,def->erf/dot_general | solution.py:11
  397.8 1.1 copy-done.2
  399.0 6.3 convert_bitcast_fusion
  405.3 0.4 reduce-scatter.3.cloned.1.call-start
  405.7 8.4 %convert_bitcast_fusion.1 = bf16[1024,1,8,768]{0,3,2,1:T(8,128)(2,1)} fusion(bf16[8,128,768]{2,1,0:T(8,128)(2,1)} %get-tuple-element.28, bf16[8,128,1024]{2,1,0:T(8,128)(2,1)S(1)} %bitcast.70), kind=kOutput, calls=%fused_computation.6 | convolution fusion | flops 1616904192 | bytes 16252928 | tf_op jit(solution)/shard_map/erd,erf->def/dot_general | solution.py:19
  414.1 6.6 convert_bitcast_fusion.2
  420.7 21.0 %pad_maximum_fusion = bf16[1024,2,8,768]{0,3,2,1:T(8,128)(2,1)} fusion(bf16[1024,1,8,768]{0,3,2,1:T(8,128)(2,1)} %convert_bitcast_fusion.1, bf16[1024,1,8,768]{0,3,2,1:T(8,128)(2,1)} %convert_bitcast_fusion.2), kind=kLoop, calls=%fused_computation.4 | loop fusion | flops 12582912 | bytes 50331648 | tf_op jit(solution)/shard_map/stack | solution.py:88
  441.7 1.4 copy-done.3
  443.1 9.1 %convolution_convert_fusion = bf16[8,128,1024]{2,1,0:T(8,128)(2,1)S(1)} fusion(bf16[8,128,768]{2,1,0:T(8,128)(2,1)S(1)} %copy-done.3, bf16[1024,8,768]{2,0,1:T(8,128)(2,1)} %all-gather.8.cloned.1.call-done), kind=kOutput, calls=%fused_computation.18 | convolution fusion | flops 1611661312 | bytes 16252928 | tf_op jit(solution)/shard_map/erf,def->erd/dot_general | solution.py:15
  452.2 2.5 copy.53
  454.7 4.6 all-to-all-start.1
  459.3 9.5 %fusion.11 = f32[8,128,1024]{2,1,0:T(8,128)S(1)} fusion(bf16[8,128,768]{2,1,0:T(8,128)(2,1)} %get-tuple-element.29, bf16[1024,8,768]{2,0,1:T(8,128)(2,1)} %all-gather.4.cloned.1.call-done), kind=kOutput, calls=%fused_computation.38 | convolution fusion | flops 1610612736 | bytes 18350080 | tf_op jit(solution)/shard_map/erf,def->erd/dot_general | solution.py:15
  468.8 10.7 %add_convert_fusion = bf16[8,128,1024]{2,1,0:T(8,128)(2,1)} fusion(f32[8,128,1024]{2,1,0:T(8,128)S(1)} %fusion.11, bf16[8,128,768]{2,1,0:T(8,128)(2,1)} %get-tuple-element.28, bf16[1024,8,768]{2,0,1:T(8,128)(2,1)} %all-gather.6.cloned.1.call-done), kind=kOutput, calls=%fused_computation.11 | convolution fusion | flops 1612709888 | bytes 20447232 | tf_op jit(solution)/shard_map/erf,def->erd/dot_general | solution.py:15
  479.5 4.1 copy.57
  483.6 24.9 %all-to-all-done.1 = bf16[8,128,1024]{2,0,1:T(8,128)(2,1)} async-done(((bf16[8,128,1024]{2,0,1:T(8,128)(2,1)}), bf16[8,128,1024]{2,0,1:T(8,128)(2,1)}, u32[]{:S(2)}, u32[]{:S(2)}) %all-to-all-start.1) | async-done | bytes 2097184 | tf_op jit(solution)/shard_map/all_to_all | solution.py:50
  508.4 4.5 all-to-all-start.3
  513.0 2.9 copy.54
  515.9 3.6 gather_fusion
  519.5 4.0 reshape.104
  523.4 38.6 %all-to-all-done.3 = bf16[8,128,1024]{2,0,1:T(8,128)(2,1)} async-done(((bf16[8,128,1024]{2,0,1:T(8,128)(2,1)}), bf16[8,128,1024]{2,0,1:T(8,128)(2,1)}, u32[]{:S(2)}, u32[]{:S(2)}) %all-to-all-start.3) | async-done | bytes 2097184 | tf_op jit(solution)/shard_map/all_to_all | solution.py:82
  562.0 2.8 copy.58
  564.8 3.6 gather_fusion.1
  568.4 4.0 reshape.105
  572.4 5.1 multiply_reduce_fusion
  577.5 0.7 copy.62
  578.2 4.3 reduce_sum.41
  582.5 5.7 copy.65
  588.2 162.7 %reduce-scatter.3.cloned.1.call-done = bf16[256,2,8,768]{0,3,2,1:T(8,128)(2,1)} async-done(((bf16[1024,2,8,768]{0,3,2,1:T(8,128)(2,1)}), bf16[256,2,8,768]{0,3,2,1:T(8,128)(2,1)}) %reduce-scatter.3.cloned.1.call-update) | async-done | bytes 6291472 | tf_op jit(solution)/shard_map/reduce_scatter | solution.py:87
  751.0 8.7 %convert_element_type.72 = f32[256,2,8,768]{0,3,2,1:T(8,128)} convert(bf16[256,2,8,768]{0,3,2,1:T(8,128)(2,1)} %reduce-scatter.3.cloned.1.call-done) | non-fusion elementwise | flops 3145728 | bytes 18874368 | tf_op jit(solution)/shard_map/convert_element_type | solution.py:94
  759.7 10.5 %slice_bitcast_fusion = (f32[256,8,768]{0,2,1:T(8,128)}, f32[256,8,768]{0,2,1:T(8,128)}) fusion(f32[256,2,8,768]{0,3,2,1:T(8,128)} %convert_element_type.72), kind=kLoop, calls=%fused_computation.8 | loop fusion | bytes 25165824 | tf_op jit(solution)/shard_map/squeeze | solution.py:96
  770.2 6.7 copy.63
  776.9 6.7 copy.64
  (32 shorter events, 0.5 us)
Async XLA Ops:
  7.2 138.5 %all-gather.4.cloned.1.call-start = ((), (), s32[]{:S(2)}) async-start(), calls=%async_computation.6 | async-start | bytes 15728640 | tf_op jit(solution)/shard_map/all_gather | solution.py:41
  11.4 1.9 copy-start.4
  11.4 250.3 %all-gather.6.cloned.1.call-start = ((), (), s32[]{:S(2)}) async-start(), calls=%async_computation.7 | async-start | bytes 15728640 | tf_op jit(solution)/shard_map/all_gather | solution.py:42
  15.5 1.9 copy-start.5
  15.6 370.6 %all-gather.8.cloned.1.call-start = ((), (), s32[]{:S(2)}) async-start(), calls=%async_computation.8 | async-start | bytes 15728640 | tf_op jit(solution)/shard_map/all_gather | solution.py:43
  19.7 0.7 copy-start.8
  19.7 3.5 copy-start.7
  25.1 14.8 %copy-start.6 = (bf16[128,1024]{1,0:T(8,128)(2,1)S(1)}, bf16[128,1024]{1,0:T(8,128)(2,1)}, u32[]{:S(2)}) copy-start(bf16[128,1024]{1,0:T(8,128)(2,1)} %param.13) | copy-start | bytes 786436
  33.1 55.8 %all-to-all-start = ((bf16[64,16,1024]{2,1,0:T(8,128)(2,1)}), bf16[64,16,1024]{2,1,0:T(8,128)(2,1)}, u32[]{:S(2)}, u32[]{:S(2)}) async-start(bf16[64,16,1024]{2,1,0:T(8,128)(2,1)} %bitcast.1), calls=%async_computation | async-start | bytes 4194304 | tf_op jit(solution)/shard_map/all_to_all | solution.py:33
  42.4 3.1 copy-start.9
  89.0 53.4 %all-to-all-start.2 = ((bf16[64,16,1024]{2,1,0:T(8,128)(2,1)}), bf16[64,16,1024]{2,1,0:T(8,128)(2,1)}, u32[]{:S(2)}, u32[]{:S(2)}) async-start(bf16[64,16,1024]{2,1,0:T(8,128)(2,1)} %bitcast.72), calls=%async_computation.2 | async-start | bytes 4194304 | tf_op jit(solution)/shard_map/all_to_all | solution.py:64
  93.3 489.2 %reduce-scatter.5.cloned.1.call-start = ((), (), s32[]{:S(2)}) async-start(), calls=%async_computation.10 | async-start | bytes 15728640 | tf_op jit(solution)/shard_map/reduce_scatter | solution.py:71
  386.1 12.8 %copy-start = (bf16[8,8,16,1024]{3,2,1,0:T(8,128)(2,1)S(1)}, bf16[8,8,16,1024]{3,2,1,0:T(8,128)(2,1)}, u32[]{:S(2)}) copy-start(bf16[8,8,16,1024]{3,2,1,0:T(8,128)(2,1)} %copy.56) | copy-start | bytes 6291460
  397.8 1.1 copy-start.2
  405.3 345.7 %reduce-scatter.3.cloned.1.call-start = ((), (), s32[]{:S(2)}) async-start(), calls=%async_computation.9 | async-start | bytes 31457280 | tf_op jit(solution)/shard_map/reduce_scatter | solution.py:87
  405.7 8.4 %copy-start.1 = (bf16[8,128,768]{2,1,0:T(8,128)(2,1)S(1)}, bf16[8,128,768]{2,1,0:T(8,128)(2,1)}, u32[]{:S(2)}) copy-start(bf16[8,128,768]{2,1,0:T(8,128)(2,1)} %get-tuple-element.29) | copy-start | bytes 4718596
  441.7 1.4 copy-start.3
  454.7 53.7 %all-to-all-start.1 = ((bf16[8,128,1024]{2,0,1:T(8,128)(2,1)}), bf16[8,128,1024]{2,0,1:T(8,128)(2,1)}, u32[]{:S(2)}, u32[]{:S(2)}) async-start(bf16[8,128,1024]{2,0,1:T(8,128)(2,1)} %copy.53), calls=%async_computation.1 | async-start | bytes 4194304 | tf_op jit(solution)/shard_map/all_to_all | solution.py:50
  508.4 53.6 %all-to-all-start.3 = ((bf16[8,128,1024]{2,0,1:T(8,128)(2,1)}), bf16[8,128,1024]{2,0,1:T(8,128)(2,1)}, u32[]{:S(2)}, u32[]{:S(2)}) async-start(bf16[8,128,1024]{2,0,1:T(8,128)(2,1)} %copy.57), calls=%async_computation.3 | async-start | bytes 4194304 | tf_op jit(solution)/shard_map/all_to_all | solution.py:82
Sparse Core Ops, SparseCore 0:
  11.5 125.2 all-gather.3
  139.2 122.5 all-gather.5
  263.6 122.5 all-gather.7
  405.4 120.7 reduce-scatter.4
  529.1 221.8 reduce-scatter.2
where the time goes:
time: 797 us; the launch traced here: 790 us
  waiting for transfers between devices  529 us (66%)
  local copies, waits for them, and re-layouts  94.7 us (12%)
  matrix products  80.5 us (10%)
  other arithmetic  50.8 us (6%)
  starting transfers between devices  21 us (3%)
  between operations  14.2 us (2%)
    reduce_scatter x1, waiting for transfers between devices, body(): lax.psum_scatter(jnp.stack([outer_rows(received, gate_delta), outer_rows(...  163 us
    all_gather x1, waiting for transfers between devices, body(): lax.all_gather(down_weight, 'blk', axis=0, tiled=True)  116 us
    all_gather x1, waiting for transfers between devices, body(): lax.all_gather(up_weight, 'blk', axis=0, tiled=True)  106 us
    all_to_all x1, waiting for transfers between devices, body(): lax.all_to_all(grad_send.reshape(experts, capacity, model_width), 'ep', s...  47 us
    all_to_all x1, waiting for transfers between devices, body(): lax.all_to_all(input_grad, 'ep', split_axis=1, concat_axis=0, tiled=True)  38.6 us
    unnamed x29, local copies, waits for them, and re-layouts  35.6 us
    all_to_all x1, waiting for transfers between devices, body(): lax.all_to_all(outgoing.reshape(experts, capacity, model_width), 'ep', sp...  33.6 us
    dot_general x3, matrix products, expand_rows(): jnp.einsum('erd,def->erf', routed, weights, preferred_element_type=jnp.fl...  29.9 us
  transfers between devices with their start and end apart: 9, of which 7 were waited for; matrix products, arithmetic and copies ran while one was open for 21% of the time, Pallas kernels for 0%

commit v1 on v0

--- a/solution.py
+++ b/solution.py
@@ -5,6 +5,12 @@
 
 EXPERTS = 64
 CAP = 16
+BF = jnp.bfloat16
+F32 = jnp.float32
+
+
+def dot(a, b, ca, cb):
+    return lax.dot_general(a, b, (((ca,), (cb,)), ((), ())), preferred_element_type=F32)
 
 
 def expand_rows(routed, weights):
@@ -19,7 +25,7 @@
     return jnp.einsum("erd,erf->def", routed, inner, preferred_element_type=jnp.float32)
 
 
-def body(tokens, expert_ids, route_weight, gate_weight, up_weight, down_weight, out_grad):
+def gathered_body(tokens, expert_ids, route_weight, gate_weight, up_weight, down_weight, out_grad):
     tok_count, model_width = tokens.shape
     top_count = expert_ids.shape[1]
     experts = EXPERTS
@@ -97,6 +103,135 @@
     return (layer_output, grad_tokens, grad_route, grad_gate, grad_up, down_summed)
 
 
+def expert_body(tokens, expert_ids, route_weight, gate_weight, up_weight, down_weight, out_grad):
+    nb, ne = lax.axis_size("blk"), lax.axis_size("ep")
+    me = lax.axis_index("blk")
+    tok, width = tokens.shape
+    top = expert_ids.shape[1]
+    local_experts = gate_weight.shape[1]
+    own = local_experts // nb
+    chunk = gate_weight.shape[0]
+    inner = gate_weight.shape[2]
+
+    def hop(x, j):
+        return lax.ppermute(x, "blk", [(i, i ^ j) for i in range(nb)])
+
+    def spread(x):
+        return [x] + [hop(x, j) for j in range(1, nb)]
+
+    def to_local(x):
+        return jnp.concatenate(
+            [lax.dynamic_slice_in_dim(x, (me ^ j) * chunk, chunk, 1) for j in range(nb)], axis=1
+        )
+
+    ids_all = jnp.concatenate(spread(expert_ids), 0)
+    rw_all = jnp.concatenate(spread(route_weight), 0)
+    tok_all = to_local(jnp.concatenate(spread(tokens), 0))
+    og_all = to_local(jnp.concatenate(spread(out_grad), 0))
+
+    w_emajor = [jnp.swapaxes(w, 0, 1) for w in (gate_weight, up_weight, down_weight)]
+
+    def weight_of(w, i):
+        pieces = []
+        for j in range(nb):
+            piece = lax.dynamic_index_in_dim(w, (me ^ j) * own + i, 0, keepdims=False)
+            pieces.append(piece if j == 0 else hop(piece, j))
+        return jnp.concatenate(pieces, 0)
+
+    weights = [[weight_of(w, i) for w in w_emajor] for i in range(own)]
+
+    rows = nb * tok
+    row = jnp.arange(rows)
+    before = ((row[:, None] > row[None, :]) & (row[:, None] // tok == row[None, :] // tok)).astype(BF)
+    slots = ne * nb * CAP
+    slot = jnp.arange(slots)
+    slot_dest, slot_group, slot_rank = slot // (nb * CAP), (slot // CAP) % nb, slot % CAP
+
+    sel, sel_w, gates = [], [], []
+    for i in range(own):
+        experts = jnp.arange(ne) * local_experts + me * own + i
+        eq = ids_all[:, :, None] == experts[None, None, :]
+        member = jnp.any(eq, axis=1)
+        weight = jnp.sum(jnp.where(eq, rw_all[:, :, None], 0.0), axis=1)
+        rank = dot(before, member.astype(BF), 1, 0)
+        rank = jnp.where(member, rank, -1.0).astype(jnp.int32)
+        rank_s = jnp.repeat(rank.T, nb * CAP, axis=0)
+        weight_s = jnp.repeat(weight.T, nb * CAP, axis=0)
+        hit = (rank_s == slot_rank[:, None]) & (slot_group[:, None] == row[None, :] // tok)
+        sel.append(hit.astype(BF))
+        sel_w.append(jnp.where(hit, weight_s, 0.0))
+        gates.append(eq)
+
+    def exchange(x):
+        return lax.all_to_all(
+            x.reshape(ne, nb * CAP, width), "ep", split_axis=0, concat_axis=0, tiled=True
+        ).reshape(slots, width)
+
+    routed, graded = [], []
+    for i in range(own):
+        routed.append(exchange(dot(sel[i], tok_all, 1, 0).astype(BF)))
+        slot_grad = dot(sel[i], og_all, 1, 0) * jnp.sum(sel_w[i], axis=1, keepdims=True)
+        graded.append(exchange(slot_grad.astype(BF)))
+
+    outs, backs, grads = [], [], []
+    for i in range(own):
+        wg, wu, wd = weights[i]
+        x, sg = routed[i], graded[i]
+        gate_pre, up_pre = dot(x, wg, 1, 0), dot(x, wu, 1, 0)
+        sig = jax.nn.sigmoid(gate_pre)
+        hidden = (gate_pre * sig * up_pre).astype(BF)
+        outs.append(exchange(dot(hidden, wd, 1, 1).astype(BF)))
+        gh = dot(sg, wd, 1, 0)
+        gate_delta = (gh * up_pre * sig * (1.0 + gate_pre * (1.0 - sig))).astype(BF)
+        up_delta = (gh * gate_pre * sig).astype(BF)
+        ig = dot(gate_delta, wg, 1, 1) + dot(up_delta, wu, 1, 1)
+        backs.append(exchange(ig.astype(BF)))
+        parts = (dot(x, gate_delta, 0, 0), dot(x, up_delta, 0, 0), dot(sg, hidden, 0, 0))
+        got = []
+        for part in parts:
+            part = part.astype(BF).reshape(nb, chunk, inner)
+            got.append([part[0]] + [hop(part[j], j) for j in range(1, nb)])
+        grads.append(got)
+
+    mixed = jnp.zeros((rows, width), F32)
+    token_grad = jnp.zeros((rows, width), F32)
+    route_grad = jnp.zeros((rows, top), F32)
+    for i in range(own):
+        high = sel_w[i].astype(BF)
+        low = (sel_w[i] - high.astype(F32)).astype(BF)
+        mixed += dot(high, outs[i], 0, 0) + dot(low, outs[i], 0, 0)
+        token_grad += dot(sel[i], backs[i], 0, 0)
+        score = dot(outs[i], og_all, 1, 1)
+        score = jnp.where(sel[i] > 0, score, 0.0).reshape(ne, nb * CAP, rows).sum(1)
+        route_grad += jnp.sum(jnp.where(gates[i], score.T[:, None, :], 0.0), axis=2)
+
+    def from_local(x):
+        out = []
+        for c in range(nb):
+            out.append(lax.dynamic_slice_in_dim(x, (me ^ c) * chunk, chunk, 1))
+        return jnp.concatenate(out, 1)
+
+    def gather_back(x):
+        x = x.reshape((nb, tok) + x.shape[1:])
+        total = x[0].astype(F32)
+        for j in range(1, nb):
+            total += hop(x[j], j).astype(F32)
+        return total
+
+    layer_output = gather_back(from_local(mixed).astype(BF)).astype(BF)
+    grad_tokens = gather_back(from_local(token_grad).astype(BF))
+    grad_route = gather_back(route_grad)
+
+    def finish(m):
+        order = jnp.stack([jnp.stack([grads[i][m][j] for i in range(own)], 0) for j in range(nb)], 0)
+        buf = jnp.concatenate(
+            [lax.dynamic_index_in_dim(order, me ^ j, 0, keepdims=False) for j in range(nb)], 0
+        )
+        return jnp.swapaxes(buf, 0, 1).astype(F32)
+
+    return (layer_output, grad_tokens, grad_route, finish(0), finish(1), finish(2))
+
+
 def solution(mesh):
     in_specs = (
         P(("blk", "ep"), None),
@@ -115,4 +250,7 @@
         P("blk", "ep", None),
         P("blk", "ep", None),
     )
+    nb, ne = mesh.shape["blk"], mesh.shape["ep"]
+    whole_experts = nb & (nb - 1) == 0 and (EXPERTS // ne) % nb == 0
+    body = expert_body if whole_experts else gathered_body
     return jax.shard_map(body, mesh=mesh, in_specs=in_specs, out_specs=out_specs, check_vma=False)

time: 797 us -> 439 us (0.55)
  waiting for transfers between devices: 529 us -> 175 us
  starting transfers between devices: 21 us -> 106 us
  other arithmetic: 50.8 us -> 16.5 us
  local copies, waits for them, and re-layouts: 94.7 us -> 63.7 us
  matrix products: 80.5 us -> 67.4 us
  between operations: 14.2 us -> 2.76 us
    all_gather x3 -> x0, waiting for transfers between devices: 222 us -> none  [the longest x1 116 us: body(): lax.all_gather(down_weight, 'blk', axis=0, tiled=True)]
    reduce_scatter x2 -> x0, waiting for transfers between devices: 163 us -> none  [the longest x1 163 us: body(): lax.psum_scatter(jnp.stack([outer_rows(received, gate_delta), outer_rows(...]
    ppermute x0 -> x57, waiting for transfers between devices: none -> 139 us  [hop(): return lax.ppermute(x, 'blk', [(i, i ^ j) for i in range(nb)])]
    all_to_all x4 -> x8, waiting for transfers between devices: 144 us -> 36 us  [exchange(): lax.all_to_all(x.reshape(ne, nb * CAP, width), 'ep', split_axis=0, concat...]
    ppermute x0 -> x57, starting transfers between devices: none -> 68.8 us  [hop(): return lax.ppermute(x, 'blk', [(i, i ^ j) for i in range(nb)])]
    another operation x0 -> x4, local copies, waits for them, and re-layouts: none -> 27 us
    all_to_all x4 -> x8, starting transfers between devices: 20.2 us -> 37.2 us  [exchange(): lax.all_to_all(x.reshape(ne, nb * CAP, width), 'ep', split_axis=0, concat...]
    another operation x3 -> x15, other arithmetic: 22.8 us -> 6.38 us  [finish(): jnp.stack([jnp.stack([grads[i][m][j] for i in range(own)], 0) for j in ra...]
  transfers between devices with their start and end apart: 9 -> 65, of which waited for: 7 -> 29; matrix products, arithmetic and copies ran while one was open for 21% -> 27% of each run, Pallas kernels for 0% -> 0%
where the time goes in v1:
time: 439 us; the launch traced here: 432 us
  waiting for transfers between devices  175 us (40%)
  starting transfers between devices  106 us (24%)
  matrix products  67.4 us (15%)
  local copies, waits for them, and re-layouts  63.7 us (15%)
  other arithmetic  16.5 us (4%)
    ppermute x57, waiting for transfers between devices, hop(): return lax.ppermute(x, 'blk', [(i, i ^ j) for i in range(nb)])  139 us
    ppermute x57, starting transfers between devices, hop(): return lax.ppermute(x, 'blk', [(i, i ^ j) for i in range(nb)])  68.8 us
    dot_general x32, matrix products, dot(): lax.dot_general(a, b, (((ca,), (cb,)), ((), ())), preferred_element_type=...  67.4 us
    all_to_all x8, starting transfers between devices, exchange(): lax.all_to_all(x.reshape(ne, nb * CAP, width), 'ep', split_axis=0, concat...  37.2 us
    all_to_all x8, waiting for transfers between devices, exchange(): lax.all_to_all(x.reshape(ne, nb * CAP, width), 'ep', split_axis=0, concat...  36 us
    unnamed x251, local copies, waits for them, and re-layouts  30.3 us
    another operation x4, local copies, waits for them, and re-layouts  27 us
  transfers between devices with their start and end apart: 65, of which 29 were waited for; matrix products, arithmetic and copies ran while one was open for 27% of the time, Pallas kernels for 0%

profile of v1, /device:TPU:0, one launch (start us, length us, event | category | flops | bytes accessed | tf_op | source)
XLA Modules:
  0.0 431.6 jit_solution(6159425954593408501)
XLA Ops:
  0.6 3.0 collective-permute-start.1
  12.6 4.0 collective-permute-done.6
  16.7 3.1 collective-permute-done.8
  21.7 5.0 %all-to-all-start.2 = ((bf16[8,64,1024]{2,1,0:T(8,128)(2,1)}), bf16[8,64,1024]{2,1,0:T(8,128)(2,1)}, u32[]{:S(2)}, u32[]{:S(2)}) async-start(bf16[8,64,1024]{2,1,0:T(8,128)(2,1)} %bitcast.255), calls=%async_computation.2 | async-start | bytes 2097152 | tf_op jit(solution)/shard_map/all_to_all | solution.py:166
  26.8 7.6 %constant_dynamic-slice_fusion.27 = (bf16[256,1,768]{2,1,0:T(2,128)(2,1)}, bf16[256,1,768]{2,1,0:T(2,128)(2,1)S(1)}, bf16[256,1,768]{2,1,0:T(2,128)(2,1)S(1)}, b...) fusion(bf16[256,8,768]{2,1,0:T(8,128)(2,1)S(1)} %copy-done, ...), kind=kLoop, calls=%fused_computation.200 | loop fusion | bytes 6291488 | tf_op jit(solution)/shard_map/dynamic-slice
  35.1 2.4 collective-permute-start.20
  41.3 12.2 %all-to-all-done.2 = bf16[8,64,1024]{2,1,0:T(8,128)(2,1)} async-done(((bf16[8,64,1024]{2,1,0:T(8,128)(2,1)}), bf16[8,64,1024]{2,1,0:T(8,128)(2,1)}, u32[]{:S(2)}, u32[]{:S(2)}) %all-to-all-start.2) | async-done | bytes 1048608 | tf_op jit(solution)/shard_map/all_to_all | solution.py:166
  53.5 4.5 %all-to-all-start = ((bf16[8,64,1024]{2,1,0:T(8,128)(2,1)}), bf16[8,64,1024]{2,1,0:T(8,128)(2,1)}, u32[]{:S(2)}, u32[]{:S(2)}) async-start(bf16[8,64,1024]{2,1,0:T(8,128)(2,1)} %bitcast.252), calls=%async_computation | async-start | bytes 2097152 | tf_op jit(solution)/shard_map/all_to_all | solution.py:166
  57.9 19.2 %constant_dynamic-slice_fusion.19 = (bf16[256,1,768]{2,1,0:T(2,128)(2,1)}, bf16[256,1,768]{2,1,0:T(2,128)(2,1)S(1)}, bf16[256,1,768]{2,1,0:T(2,128)(2,1)S(1)}, b...) fusion(bf16[256,8,768]{2,1,0:T(8,128)(2,1)S(1)} %copy-done.1, ...), kind=kLoop, calls=%fused_computation.192 | loop fusion | bytes 12582944 | tf_op jit(solution)/shard_map/dynamic-slice.8
  81.3 2.5 collective-permute-start.26
  84.4 2.5 fusion.28
  90.8 8.5 %collective-permute-done.23 = bf16[256,768]{1,0:T(8,128)(2,1)S(1)} collective-permute-done((bf16[256,768]{1,0:T(8,128)(2,1)S(1)}, bf16[256,768]{1,0:T(8,128)(2,1)S(1)}, u32[]{:S(2)}, u32[]{:S(2)}) %collective-permute-start.23) | collective-permute-done | bytes 393248 | tf_op jit(solution)/shard_map/ppermute | solution.py:117
  99.3 3.6 multiply_convert_fusion.6
  102.9 4.8 %collective-permute-done.26 = bf16[256,768]{1,0:T(8,128)(2,1)S(1)} collective-permute-done((bf16[256,768]{1,0:T(8,128)(2,1)S(1)}, bf16[256,768]{1,0:T(8,128)(2,1)S(1)}, u32[]{:S(2)}, u32[]{:S(2)}) %collective-permute-start.26) | collective-permute-done | bytes 393248 | tf_op jit(solution)/shard_map/ppermute | solution.py:117
  107.7 7.7 %collective-permute-done.24 = bf16[256,768]{1,0:T(8,128)(2,1)S(1)} collective-permute-done((bf16[256,768]{1,0:T(8,128)(2,1)S(1)}, bf16[256,768]{1,0:T(8,128)(2,1)S(1)}, u32[]{:S(2)}, u32[]{:S(2)}) %collective-permute-start.24) | collective-permute-done | bytes 393248 | tf_op jit(solution)/shard_map/ppermute | solution.py:117
  116.3 2.0 convolution_convert_fusion.6
  118.3 5.3 %all-to-all-start.3 = ((bf16[8,64,1024]{2,1,0:T(8,128)(2,1)}), bf16[8,64,1024]{2,1,0:T(8,128)(2,1)S(1)}, u32[]{:S(2)}, u32[]{:S(2)}) async-start(bf16[8,64,1024]{2,1,0:T(8,128)(2,1)} %bitcast.254), calls=%async_computation.3 | async-start | bytes 2097152 | tf_op jit(solution)/shard_map/all_to_all | solution.py:166
  127.6 2.0 collective-permute-start.14
  130.7 5.0 %collective-permute-done.9 = bf16[256,768]{1,0:T(8,128)(2,1)S(1)} collective-permute-done((bf16[256,768]{1,0:T(8,128)(2,1)S(1)}, bf16[256,768]{1,0:T(8,128)(2,1)S(1)}, u32[]{:S(2)}, u32[]{:S(2)}) %collective-permute-start.9) | collective-permute-done | bytes 393248 | tf_op jit(solution)/shard_map/ppermute | solution.py:117
  138.9 15.3 %collective-permute-done.10 = bf16[256,768]{1,0:T(8,128)(2,1)S(1)} collective-permute-done((bf16[256,768]{1,0:T(8,128)(2,1)S(1)}, bf16[256,768]{1,0:T(8,128)(2,1)S(1)}, u32[]{:S(2)}, u32[]{:S(2)}) %collective-permute-start.10) | collective-permute-done | bytes 393248 | tf_op jit(solution)/shard_map/ppermute | solution.py:117
  155.8 2.2 fusion.32
  160.0 2.6 collective-permute-done.13
  162.6 3.8 multiply_convert_fusion.7
  166.4 3.1 collective-permute-done.15
  169.4 9.3 %collective-permute-done.16 = bf16[256,768]{1,0:T(8,128)(2,1)S(1)} collective-permute-done((bf16[256,768]{1,0:T(8,128)(2,1)S(1)}, bf16[256,768]{1,0:T(8,128)(2,1)S(1)}, u32[]{:S(2)}, u32[]{:S(2)}) %collective-permute-start.16) | collective-permute-done | bytes 393248 | tf_op jit(solution)/shard_map/ppermute | solution.py:117
  181.6 4.9 %all-to-all-start.1 = ((bf16[8,64,1024]{2,1,0:T(8,128)(2,1)}), bf16[8,64,1024]{2,1,0:T(8,128)(2,1)S(1)}, u32[]{:S(2)}, u32[]{:S(2)}) async-start(bf16[8,64,1024]{2,1,0:T(8,128)(2,1)} %bitcast.17), calls=%async_computation.1 | async-start | bytes 2097152 | tf_op jit(solution)/shard_map/all_to_all | solution.py:166
  191.7 2.0 collective-permute-start.32
  193.7 6.6 %collective-permute-done.30 = bf16[128,1024]{1,0:T(8,128)(2,1)S(1)} collective-permute-done((bf16[128,1024]{1,0:T(8,128)(2,1)S(1)}, bf16[128,1024]{1,0:T(8,128)(2,1)S(1)}, u32[]{:S(2)}, u32[]{:S(2)}) %collective-permute-start.30) | collective-permute-done | bytes 262176 | tf_op jit(solution)/shard_map/ppermute | solution.py:117
  200.4 4.3 %collective-permute-done.32 = bf16[128,1024]{1,0:T(8,128)(2,1)S(1)} collective-permute-done((bf16[128,1024]{1,0:T(8,128)(2,1)S(1)}, bf16[128,1024]{1,0:T(8,128)(2,1)S(1)}, u32[]{:S(2)}, u32[]{:S(2)}) %collective-permute-start.32) | collective-permute-done | bytes 262176 | tf_op jit(solution)/shard_map/ppermute | solution.py:117
  206.3 6.7 %all-to-all-done.1 = bf16[8,64,1024]{2,1,0:T(8,128)(2,1)S(1)} async-done(((bf16[8,64,1024]{2,1,0:T(8,128)(2,1)}), bf16[8,64,1024]{2,1,0:T(8,128)(2,1)S(1)}, u32[]{:S(2)}, u32[]{:S(2)}) %all-to-all-start.1) | async-done | bytes 1048608 | tf_op jit(solution)/shard_map/all_to_all | solution.py:166
  217.7 3.6 all-to-all-start.4
  221.4 2.9 multiply_convert_fusion
  224.2 2.2 fusion.9
  226.4 2.2 fusion.8
  228.6 2.2 fusion.11
  230.8 17.0 %all-to-all-done.4 = bf16[8,64,1024]{2,1,0:T(8,128)(2,1)S(1)} async-done(((bf16[8,64,1024]{2,1,0:T(8,128)(2,1)}), bf16[8,64,1024]{2,1,0:T(8,128)(2,1)S(1)}, u32[]{:S(2)}, u32[]{:S(2)}) %all-to-all-start.4) | async-done | bytes 1048608 | tf_op jit(solution)/shard_map/all_to_all | solution.py:166
  247.8 3.7 all-to-all-start.6
  251.5 3.7 fusion
  262.5 8.7 %collective-permute-done.36 = f32[128,6]{0,1:T(8,128)S(1)} collective-permute-done((f32[128,6]{0,1:T(8,128)S(1)}, f32[128,6]{0,1:T(8,128)S(1)}, u32[]{:S(2)}, u32[]{:S(2)}) %collective-permute-start.36) | collective-permute-done | bytes 3104 | tf_op jit(solution)/shard_map/ppermute | solution.py:117
  272.2 2.6 collective-permute-done.37
  277.3 2.1 convolution_convert_fusion.1
  286.4 2.2 convolution_convert_fusion.5
  288.7 2.4 convolution_convert_fusion.3
  292.4 2.0 add_convert_fusion.1
  294.4 4.8 %all-to-all-start.5 = ((bf16[8,64,1024]{2,1,0:T(8,128)(2,1)}), bf16[8,64,1024]{2,1,0:T(8,128)(2,1)}, u32[]{:S(2)}, u32[]{:S(2)}) async-start(bf16[8,64,1024]{2,1,0:T(8,128)(2,1)} %bitcast.246), calls=%async_computation.5 | async-start | bytes 2097152 | tf_op jit(solution)/shard_map/all_to_all | solution.py:166
  304.9 2.2 convolution_convert_fusion.4
  307.1 2.2 convolution_convert_fusion.2
  312.7 3.2 add_convert_fusion
  317.9 2.0 collective-permute-start.49
  321.5 7.9 %collective-permute-done.44 = bf16[256,768]{1,0:T(8,128)(2,1)S(1)} collective-permute-done((bf16[256,768]{1,0:T(8,128)(2,1)S(1)}, bf16[256,768]{1,0:T(8,128)(2,1)S(1)}, u32[]{:S(2)}, u32[]{:S(2)}) %collective-permute-start.44) | collective-permute-done | bytes 393248 | tf_op jit(solution)/shard_map/ppermute | solution.py:117
  331.5 14.6 %collective-permute-done.42 = bf16[256,768]{1,0:T(8,128)(2,1)S(1)} collective-permute-done((bf16[256,768]{1,0:T(8,128)(2,1)S(1)}, bf16[256,768]{1,0:T(8,128)(2,1)S(1)}, u32[]{:S(2)}, u32[]{:S(2)}) %collective-permute-start.42) | collective-permute-done | bytes 393248 | tf_op jit(solution)/shard_map/ppermute | solution.py:117
  349.4 5.2 %collective-permute-done.50 = bf16[256,768]{1,0:T(8,128)(2,1)S(1)} collective-permute-done((bf16[256,768]{1,0:T(8,128)(2,1)S(1)}, bf16[256,768]{1,0:T(8,128)(2,1)S(1)}, u32[]{:S(2)}, u32[]{:S(2)}) %collective-permute-start.50) | collective-permute-done | bytes 393248 | tf_op jit(solution)/shard_map/ppermute | solution.py:117
  355.7 6.9 %collective-permute-done.47 = bf16[256,768]{1,0:T(8,128)(2,1)S(1)} collective-permute-done((bf16[256,768]{1,0:T(8,128)(2,1)S(1)}, bf16[256,768]{1,0:T(8,128)(2,1)S(1)}, u32[]{:S(2)}, u32[]{:S(2)}) %collective-permute-start.47) | collective-permute-done | bytes 393248 | tf_op jit(solution)/shard_map/ppermute | solution.py:117
  363.6 7.8 %collective-permute-done.48 = bf16[256,768]{1,0:T(8,128)(2,1)S(1)} collective-permute-done((bf16[256,768]{1,0:T(8,128)(2,1)S(1)}, bf16[256,768]{1,0:T(8,128)(2,1)S(1)}, u32[]{:S(2)}, u32[]{:S(2)}) %collective-permute-start.48) | collective-permute-done | bytes 393248 | tf_op jit(solution)/shard_map/ppermute | solution.py:117
  372.0 2.1 collective-permute-start.55
  377.8 5.4 %all-to-all-start.7 = ((bf16[8,64,1024]{2,1,0:T(8,128)(2,1)}), bf16[8,64,1024]{2,1,0:T(8,128)(2,1)}, u32[]{:S(2)}, u32[]{:S(2)}) async-start(bf16[8,64,1024]{2,1,0:T(8,128)(2,1)} %bitcast.244), calls=%async_computation.7 | async-start | bytes 2097152 | tf_op jit(solution)/shard_map/all_to_all | solution.py:166
  383.2 2.1 convert_bitcast_fusion.1
  387.5 6.3 %copy.100 = f32[256,8,768]{2,1,0:T(8,128)} copy(f32[256,8,768]{2,0,1:T(8,128)S(1)} %convert_bitcast_fusion.1) | data formatting | bytes 12582912
  393.8 6.3 %copy.99 = f32[256,8,768]{2,1,0:T(8,128)} copy(f32[256,8,768]{2,0,1:T(8,128)S(1)} %convert_bitcast_fusion.2) | data formatting | bytes 12582912
  401.4 3.1 collective-permute-done.53
  408.0 3.4 fusion.70
  411.4 2.8 bitcast_add_fusion
  418.9 6.3 %copy.101 = f32[256,8,768]{2,1,0:T(8,128)} copy(f32[256,8,768]{2,0,1:T(8,128)S(1)} %convert_bitcast_fusion) | data formatting | bytes 12582912
  425.3 3.6 collective-permute-done.35
  (405 shorter events, 107.6 us)
Async XLA Ops:
  0.6 9.1 %collective-permute-start.1 = (s32[128,6]{0,1:T(8,128)}, s32[128,6]{0,1:T(8,128)S(1)}, u32[]{:S(2)}, u32[]{:S(2)}) collective-permute-start(s32[128,6]{0,1:T(8,128)} %param.8), channel_id=1, source_target_pairs={{0,16},{8,24},{16,0},{24,8},{1,17},{9,25},{17,1},{25,9},{2,18},{10... | collective-permute-start | bytes 9224 | tf_op jit(solution)/shard_map/ppermute | solution.py:117
  3.7 6.2 %collective-permute-start = (s32[128,6]{0,1:T(8,128)}, s32[128,6]{0,1:T(8,128)S(1)}, u32[]{:S(2)}, u32[]{:S(2)}) collective-permute-start(s32[128,6]{0,1:T(8,128)} %param.8), channel_id=1, source_target_pairs={{0,8},{8,0},{16,24},{24,16},{1,9},{9,1},{17,25},{25,17},{2,10},{10... | collective-permute-start | bytes 9224 | tf_op jit(solution)/shard_map/ppermute | solution.py:117
  5.2 4.8 %collective-permute-start.2 = (s32[128,6]{0,1:T(8,128)}, s32[128,6]{0,1:T(8,128)S(1)}, u32[]{:S(2)}, u32[]{:S(2)}) collective-permute-start(s32[128,6]{0,1:T(8,128)} %param.8), channel_id=1, source_target_pairs={{0,24},{8,16},{16,8},{24,0},{1,25},{9,17},{17,9},{25,1},{2,26},{10... | collective-permute-start | bytes 9224 | tf_op jit(solution)/shard_map/ppermute | solution.py:117
  5.2 11.4 %collective-permute-start.7 = (bf16[128,1024]{1,0:T(8,128)(2,1)}, bf16[128,1024]{1,0:T(8,128)(2,1)S(1)}, u32[]{:S(2)}, u32[]{:S(2)}) collective-permute-start(bf16[128,1024]{1,0:T(8,128)(2,1)} %param.7), channel_id=1, source_target_pairs={{0,16},{8,24},{16,0},{24,8},{1,17},{9,25},{17,1},{25,9},{2,18},{10... | collective-permute-start | bytes 786440 | tf_op jit(solution)/shard_map/ppermute | solution.py:117
  7.2 9.5 %collective-permute-start.6 = (bf16[128,1024]{1,0:T(8,128)(2,1)}, bf16[128,1024]{1,0:T(8,128)(2,1)S(1)}, u32[]{:S(2)}, u32[]{:S(2)}) collective-permute-start(bf16[128,1024]{1,0:T(8,128)(2,1)} %param.7), channel_id=1, source_target_pairs={{0,8},{8,0},{16,24},{24,16},{1,9},{9,1},{17,25},{25,17},{2,10},{10... | collective-permute-start | bytes 786440 | tf_op jit(solution)/shard_map/ppermute | solution.py:117
  9.7 10.0 %collective-permute-start.8 = (bf16[128,1024]{1,0:T(8,128)(2,1)}, bf16[128,1024]{1,0:T(8,128)(2,1)S(1)}, u32[]{:S(2)}, u32[]{:S(2)}) collective-permute-start(bf16[128,1024]{1,0:T(8,128)(2,1)} %param.7), channel_id=1, source_target_pairs={{0,24},{8,16},{16,8},{24,0},{1,25},{9,17},{17,9},{25,1},{2,26},{10... | collective-permute-start | bytes 786440 | tf_op jit(solution)/shard_map/ppermute | solution.py:117
  21.7 31.7 %all-to-all-start.2 = ((bf16[8,64,1024]{2,1,0:T(8,128)(2,1)}), bf16[8,64,1024]{2,1,0:T(8,128)(2,1)}, u32[]{:S(2)}, u32[]{:S(2)}) async-start(bf16[8,64,1024]{2,1,0:T(8,128)(2,1)} %bitcast.255), calls=%async_computation.2 | async-start | bytes 2097152 | tf_op jit(solution)/shard_map/all_to_all | solution.py:166
  35.1 45.2 %collective-permute-start.20 = (bf16[256,768]{1,0:T(8,128)(2,1)}, bf16[256,768]{1,0:T(8,128)(2,1)}, u32[]{:S(2)}, u32[]{:S(2)}) collective-permute-start(bf16[256,768]{1,0:T(8,128)(2,1)} %bitcast.228), channel_id=1, source_target_pairs={{0,24},{8,16},{16,8},{24,0},{1,25},{9,17},{17,9},{25,1},{2,26},{10... | collective-permute-start | bytes 1179656 | tf_op jit(solution)/shard_map/ppermute | solution.py:117
  38.3 43.0 %collective-permute-start.18 = (bf16[256,768]{1,0:T(8,128)(2,1)}, bf16[256,768]{1,0:T(8,128)(2,1)}, u32[]{:S(2)}, u32[]{:S(2)}) collective-permute-start(bf16[256,768]{1,0:T(8,128)(2,1)} %bitcast.230), channel_id=1, source_target_pairs={{0,8},{8,0},{16,24},{24,16},{1,9},{9,1},{17,25},{25,17},{2,10},{10... | collective-permute-start | bytes 1179656 | tf_op jit(solution)/shard_map/ppermute | solution.py:117
  39.0 44.8 %collective-permute-start.19 = (bf16[256,768]{1,0:T(8,128)(2,1)S(1)}, bf16[256,768]{1,0:T(8,128)(2,1)}, u32[]{:S(2)}, u32[]{:S(2)}) collective-permute-start(bf16[256,768]{1,0:T(8,128)(2,1)S(1)} %bitcast.272), channel_id=1, source_target_pairs={{0,16},{8,24},{16,0},{24,8},{1,17},{9,25},{17,1},{25,9},{2,18},{10... | collective-permute-start | bytes 1179656 | tf_op jit(solution)/shard_map/ppermute | solution.py:117
  53.5 64.8 %all-to-all-start = ((bf16[8,64,1024]{2,1,0:T(8,128)(2,1)}), bf16[8,64,1024]{2,1,0:T(8,128)(2,1)}, u32[]{:S(2)}, u32[]{:S(2)}) async-start(bf16[8,64,1024]{2,1,0:T(8,128)(2,1)} %bitcast.252), calls=%async_computation | async-start | bytes 2097152 | tf_op jit(solution)/shard_map/all_to_all | solution.py:166
  77.2 11.5 %collective-permute-start.22 = (bf16[256,768]{1,0:T(8,128)(2,1)S(1)}, bf16[256,768]{1,0:T(8,128)(2,1)S(1)}, u32[]{:S(2)}, u32[]{:S(2)}) collective-permute-start(bf16[256,768]{1,0:T(8,128)(2,1)S(1)} %bitcast.288), channel_id=1, source_target_pairs={{0,16},{8,24},{16,0},{24,8},{1,17},{9,25},{17,1},{25,9},{2,18},{10... | collective-permute-start | bytes 1179656 | tf_op jit(solution)/shard_map/ppermute | solution.py:117
  78.8 12.0 %collective-permute-start.21 = (bf16[256,768]{1,0:T(8,128)(2,1)S(1)}, bf16[256,768]{1,0:T(8,128)(2,1)S(1)}, u32[]{:S(2)}, u32[]{:S(2)}) collective-permute-start(bf16[256,768]{1,0:T(8,128)(2,1)S(1)} %bitcast.283), channel_id=1, source_target_pairs={{0,8},{8,0},{16,24},{24,16},{1,9},{9,1},{17,25},{25,17},{2,10},{10... | collective-permute-start | bytes 1179656 | tf_op jit(solution)/shard_map/ppermute | solution.py:117
  80.4 18.9 %collective-permute-start.23 = (bf16[256,768]{1,0:T(8,128)(2,1)S(1)}, bf16[256,768]{1,0:T(8,128)(2,1)S(1)}, u32[]{:S(2)}, u32[]{:S(2)}) collective-permute-start(bf16[256,768]{1,0:T(8,128)(2,1)S(1)} %bitcast.289), channel_id=1, source_target_pairs={{0,24},{8,16},{16,8},{24,0},{1,25},{9,17},{17,9},{25,1},{2,26},{10... | collective-permute-start | bytes 1179656 | tf_op jit(solution)/shard_map/ppermute | solution.py:117
  81.3 26.3 %collective-permute-start.26 = (bf16[256,768]{1,0:T(8,128)(2,1)S(1)}, bf16[256,768]{1,0:T(8,128)(2,1)S(1)}, u32[]{:S(2)}, u32[]{:S(2)}) collective-permute-start(bf16[256,768]{1,0:T(8,128)(2,1)S(1)} %bitcast.295), channel_id=1, source_target_pairs={{0,24},{8,16},{16,8},{24,0},{1,25},{9,17},{17,9},{25,1},{2,26},{10... | collective-permute-start | bytes 1179656 | tf_op jit(solution)/shard_map/ppermute | solution.py:117
  83.8 31.6 %collective-permute-start.24 = (bf16[256,768]{1,0:T(8,128)(2,1)S(1)}, bf16[256,768]{1,0:T(8,128)(2,1)S(1)}, u32[]{:S(2)}, u32[]{:S(2)}) collective-permute-start(bf16[256,768]{1,0:T(8,128)(2,1)S(1)} %bitcast.291), channel_id=1, source_target_pairs={{0,8},{8,0},{16,24},{24,16},{1,9},{9,1},{17,25},{25,17},{2,10},{10... | collective-permute-start | bytes 1179656 | tf_op jit(solution)/shard_map/ppermute | solution.py:117
  88.7 26.7 %collective-permute-start.25 = (bf16[256,768]{1,0:T(8,128)(2,1)S(1)}, bf16[256,768]{1,0:T(8,128)(2,1)S(1)}, u32[]{:S(2)}, u32[]{:S(2)}) collective-permute-start(bf16[256,768]{1,0:T(8,128)(2,1)S(1)} %bitcast.281), channel_id=1, source_target_pairs={{0,16},{8,24},{16,0},{24,8},{1,17},{9,25},{17,1},{25,9},{2,18},{10... | collective-permute-start | bytes 1179656 | tf_op jit(solution)/shard_map/ppermute | solution.py:117
  118.3 63.3 %all-to-all-start.3 = ((bf16[8,64,1024]{2,1,0:T(8,128)(2,1)}), bf16[8,64,1024]{2,1,0:T(8,128)(2,1)S(1)}, u32[]{:S(2)}, u32[]{:S(2)}) async-start(bf16[8,64,1024]{2,1,0:T(8,128)(2,1)} %bitcast.254), calls=%async_computation.3 | async-start | bytes 2097152 | tf_op jit(solution)/shard_map/all_to_all | solution.py:166
  123.7 12.0 %collective-permute-start.9 = (bf16[256,768]{1,0:T(8,128)(2,1)S(1)}, bf16[256,768]{1,0:T(8,128)(2,1)S(1)}, u32[]{:S(2)}, u32[]{:S(2)}) collective-permute-start(bf16[256,768]{1,0:T(8,128)(2,1)S(1)} %bitcast.297), channel_id=1, source_target_pairs={{0,8},{8,0},{16,24},{24,16},{1,9},{9,1},{17,25},{25,17},{2,10},{10... | collective-permute-start | bytes 1179656 | tf_op jit(solution)/shard_map/ppermute | solution.py:117
  125.3 28.9 %collective-permute-start.10 = (bf16[256,768]{1,0:T(8,128)(2,1)S(1)}, bf16[256,768]{1,0:T(8,128)(2,1)S(1)}, u32[]{:S(2)}, u32[]{:S(2)}) collective-permute-start(bf16[256,768]{1,0:T(8,128)(2,1)S(1)} %bitcast.292), channel_id=1, source_target_pairs={{0,16},{8,24},{16,0},{24,8},{1,17},{9,25},{17,1},{25,9},{2,18},{10... | collective-permute-start | bytes 1179656 | tf_op jit(solution)/shard_map/ppermute | solution.py:117
  126.4 28.3 %collective-permute-start.11 = (bf16[256,768]{1,0:T(8,128)(2,1)S(1)}, bf16[256,768]{1,0:T(8,128)(2,1)S(1)}, u32[]{:S(2)}, u32[]{:S(2)}) collective-permute-start(bf16[256,768]{1,0:T(8,128)(2,1)S(1)} %bitcast.290), channel_id=1, source_target_pairs={{0,24},{8,16},{16,8},{24,0},{1,25},{9,17},{17,9},{25,1},{2,26},{10... | collective-permute-start | bytes 1179656 | tf_op jit(solution)/shard_map/ppermute | solution.py:117
  127.6 30.5 %collective-permute-start.14 = (bf16[256,768]{1,0:T(8,128)(2,1)S(1)}, bf16[256,768]{1,0:T(8,128)(2,1)S(1)}, u32[]{:S(2)}, u32[]{:S(2)}) collective-permute-start(bf16[256,768]{1,0:T(8,128)(2,1)S(1)} %bitcast.284), channel_id=1, source_target_pairs={{0,24},{8,16},{16,8},{24,0},{1,25},{9,17},{17,9},{25,1},{2,26},{10... | collective-permute-start | bytes 1179656 | tf_op jit(solution)/shard_map/ppermute | solution.py:117
  129.6 33.0 %collective-permute-start.13 = (bf16[256,768]{1,0:T(8,128)(2,1)S(1)}, bf16[256,768]{1,0:T(8,128)(2,1)S(1)}, u32[]{:S(2)}, u32[]{:S(2)}) collective-permute-start(bf16[256,768]{1,0:T(8,128)(2,1)S(1)} %bitcast.279), channel_id=1, source_target_pairs={{0,16},{8,24},{16,0},{24,8},{1,17},{9,25},{17,1},{25,9},{2,18},{10... | collective-permute-start | bytes 1179656 | tf_op jit(solution)/shard_map/ppermute | solution.py:117
  135.7 26.9 %collective-permute-start.12 = (bf16[256,768]{1,0:T(8,128)(2,1)S(1)}, bf16[256,768]{1,0:T(8,128)(2,1)S(1)}, u32[]{:S(2)}, u32[]{:S(2)}) collective-permute-start(bf16[256,768]{1,0:T(8,128)(2,1)S(1)} %bitcast.285), channel_id=1, source_target_pairs={{0,8},{8,0},{16,24},{24,16},{1,9},{9,1},{17,25},{25,17},{2,10},{10... | collective-permute-start | bytes 1179656 | tf_op jit(solution)/shard_map/ppermute | solution.py:117
  154.1 15.3 %collective-permute-start.15 = (bf16[256,768]{1,0:T(8,128)(2,1)S(1)}, bf16[256,768]{1,0:T(8,128)(2,1)S(1)}, u32[]{:S(2)}, u32[]{:S(2)}) collective-permute-start(bf16[256,768]{1,0:T(8,128)(2,1)S(1)} %bitcast.294), channel_id=1, source_target_pairs={{0,8},{8,0},{16,24},{24,16},{1,9},{9,1},{17,25},{25,17},{2,10},{10... | collective-permute-start | bytes 1179656 | tf_op jit(solution)/shard_map/ppermute | solution.py:117
  154.7 24.0 %collective-permute-start.16 = (bf16[256,768]{1,0:T(8,128)(2,1)S(1)}, bf16[256,768]{1,0:T(8,128)(2,1)S(1)}, u32[]{:S(2)}, u32[]{:S(2)}) collective-permute-start(bf16[256,768]{1,0:T(8,128)(2,1)S(1)} %bitcast.293), channel_id=1, source_target_pairs={{0,16},{8,24},{16,0},{24,8},{1,17},{9,25},{17,1},{25,9},{2,18},{10... | collective-permute-start | bytes 1179656 | tf_op jit(solution)/shard_map/ppermute | solution.py:117
  158.0 20.7 %collective-permute-start.17 = (bf16[256,768]{1,0:T(8,128)(2,1)S(1)}, bf16[256,768]{1,0:T(8,128)(2,1)S(1)}, u32[]{:S(2)}, u32[]{:S(2)}) collective-permute-start(bf16[256,768]{1,0:T(8,128)(2,1)S(1)} %bitcast.286), channel_id=1, source_target_pairs={{0,24},{8,16},{16,8},{24,0},{1,25},{9,17},{17,9},{25,1},{2,26},{10... | collective-permute-start | bytes 1179656 | tf_op jit(solution)/shard_map/ppermute | solution.py:117
  181.6 31.5 %all-to-all-start.1 = ((bf16[8,64,1024]{2,1,0:T(8,128)(2,1)}), bf16[8,64,1024]{2,1,0:T(8,128)(2,1)S(1)}, u32[]{:S(2)}, u32[]{:S(2)}) async-start(bf16[8,64,1024]{2,1,0:T(8,128)(2,1)} %bitcast.17), calls=%async_computation.1 | async-start | bytes 2097152 | tf_op jit(solution)/shard_map/all_to_all | solution.py:166
  186.5 5.2 %collective-permute-start.4 = (f32[128,6]{0,1:T(8,128)S(1)}, f32[128,6]{0,1:T(8,128)S(1)}, u32[]{:S(2)}, u32[]{:S(2)}) collective-permute-start(f32[128,6]{0,1:T(8,128)S(1)} %copy-done.65), channel_id=1, source_target_pairs={{0,16},{8,24},{16,0},{24,8},{1,17},{9,25},{17,1},{25,9},{2,18},{10... | collective-permute-start | bytes 9224 | tf_op jit(solution)/shard_map/ppermute | solution.py:117
  187.6 6.1 %collective-permute-start.3 = (f32[128,6]{0,1:T(8,128)S(1)}, f32[128,6]{0,1:T(8,128)S(1)}, u32[]{:S(2)}, u32[]{:S(2)}) collective-permute-start(f32[128,6]{0,1:T(8,128)S(1)} %copy-done.65), channel_id=1, source_target_pairs={{0,8},{8,0},{16,24},{24,16},{1,9},{9,1},{17,25},{25,17},{2,10},{10... | collective-permute-start | bytes 9224 | tf_op jit(solution)/shard_map/ppermute | solution.py:117
  188.1 5.6 %collective-permute-start.5 = (f32[128,6]{0,1:T(8,128)S(1)}, f32[128,6]{0,1:T(8,128)S(1)}, u32[]{:S(2)}, u32[]{:S(2)}) collective-permute-start(f32[128,6]{0,1:T(8,128)S(1)} %copy-done.65), channel_id=1, source_target_pairs={{0,24},{8,16},{16,8},{24,0},{1,25},{9,17},{17,9},{25,1},{2,26},{10... | collective-permute-start | bytes 9224 | tf_op jit(solution)/shard_map/ppermute | solution.py:117
  190.0 10.3 %collective-permute-start.31 = (bf16[128,1024]{1,0:T(8,128)(2,1)S(1)}, bf16[128,1024]{1,0:T(8,128)(2,1)S(1)}, u32[]{:S(2)}, u32[]{:S(2)}) collective-permute-start(bf16[128,1024]{1,0:T(8,128)(2,1)S(1)} %copy-done.46), channel_id=1, source_target_pairs={{0,16},{8,24},{16,0},{24,8},{1,17},{9,25},{17,1},{25,9},{2,18},{10... | collective-permute-start | bytes 786440 | tf_op jit(solution)/shard_map/ppermute | solution.py:117
  191.1 9.2 %collective-permute-start.30 = (bf16[128,1024]{1,0:T(8,128)(2,1)S(1)}, bf16[128,1024]{1,0:T(8,128)(2,1)S(1)}, u32[]{:S(2)}, u32[]{:S(2)}) collective-permute-start(bf16[128,1024]{1,0:T(8,128)(2,1)S(1)} %copy-done.46), channel_id=1, source_target_pairs={{0,8},{8,0},{16,24},{24,16},{1,9},{9,1},{17,25},{25,17},{2,10},{10... | collective-permute-start | bytes 786440 | tf_op jit(solution)/shard_map/ppermute | solution.py:117
  191.7 13.0 %collective-permute-start.32 = (bf16[128,1024]{1,0:T(8,128)(2,1)S(1)}, bf16[128,1024]{1,0:T(8,128)(2,1)S(1)}, u32[]{:S(2)}, u32[]{:S(2)}) collective-permute-start(bf16[128,1024]{1,0:T(8,128)(2,1)S(1)} %copy-done.46), channel_id=1, source_target_pairs={{0,24},{8,16},{16,8},{24,0},{1,25},{9,17},{17,9},{25,1},{2,26},{10... | collective-permute-start | bytes 786440 | tf_op jit(solution)/shard_map/ppermute | solution.py:117
  217.7 30.1 %all-to-all-start.4 = ((bf16[8,64,1024]{2,1,0:T(8,128)(2,1)}), bf16[8,64,1024]{2,1,0:T(8,128)(2,1)S(1)}, u32[]{:S(2)}, u32[]{:S(2)}) async-start(bf16[8,64,1024]{2,1,0:T(8,128)(2,1)} %bitcast.256), calls=%async_computation.4 | async-start | bytes 2097152 | tf_op jit(solution)/shard_map/all_to_all | solution.py:166
  247.8 32.7 %all-to-all-start.6 = ((bf16[8,64,1024]{2,1,0:T(8,128)(2,1)}), bf16[8,64,1024]{2,1,0:T(8,128)(2,1)S(1)}, u32[]{:S(2)}, u32[]{:S(2)}) async-start(bf16[8,64,1024]{2,1,0:T(8,128)(2,1)} %bitcast.251), calls=%async_computation.6 | async-start | bytes 2097152 | tf_op jit(solution)/shard_map/all_to_all | solution.py:166
  256.5 18.9 %collective-permute-start.27 = (bf16[128,1024]{1,0:T(8,128)(2,1)}, bf16[128,1024]{1,0:T(8,128)(2,1)S(1)}, u32[]{:S(2)}, u32[]{:S(2)}) collective-permute-start(bf16[128,1024]{1,0:T(8,128)(2,1)} %get-tuple-element.103), channel_id=1, source_target_pairs={{0,8},{8,0},{16,24},{24,16},{1,9},{9,1},{17,25},{25,17},{2,10},{10... | collective-permute-start | bytes 786440 | tf_op jit(solution)/shard_map/ppermute | solution.py:117
  257.1 18.3 %collective-permute-start.29 = (bf16[128,1024]{1,0:T(8,128)(2,1)}, bf16[128,1024]{1,0:T(8,128)(2,1)}, u32[]{:S(2)}, u32[]{:S(2)}) collective-permute-start(bf16[128,1024]{1,0:T(8,128)(2,1)} %get-tuple-element.104), channel_id=1, source_target_pairs={{0,24},{8,16},{16,8},{24,0},{1,25},{9,17},{17,9},{25,1},{2,26},{10... | collective-permute-start | bytes 786440 | tf_op jit(solution)/shard_map/ppermute | solution.py:117
  259.0 16.4 %collective-permute-start.28 = (bf16[128,1024]{1,0:T(8,128)(2,1)}, bf16[128,1024]{1,0:T(8,128)(2,1)}, u32[]{:S(2)}, u32[]{:S(2)}) collective-permute-start(bf16[128,1024]{1,0:T(8,128)(2,1)} %get-tuple-element.105), channel_id=1, source_target_pairs={{0,16},{8,24},{16,0},{24,8},{1,17},{9,25},{17,1},{25,9},{2,18},{10... | collective-permute-start | bytes 786440 | tf_op jit(solution)/shard_map/ppermute | solution.py:117
  260.0 11.2 %collective-permute-start.36 = (f32[128,6]{0,1:T(8,128)S(1)}, f32[128,6]{0,1:T(8,128)S(1)}, u32[]{:S(2)}, u32[]{:S(2)}) collective-permute-start(f32[128,6]{0,1:T(8,128)S(1)} %get-tuple-element.118), channel_id=1, source_target_pairs={{0,8},{8,0},{16,24},{24,16},{1,9},{9,1},{17,25},{25,17},{2,10},{10... | collective-permute-start | bytes 9224 | tf_op jit(solution)/shard_map/ppermute | solution.py:117
  260.6 11.6 %collective-permute-start.38 = (f32[128,6]{0,1:T(8,128)S(1)}, f32[128,6]{0,1:T(8,128)S(1)}, u32[]{:S(2)}, u32[]{:S(2)}) collective-permute-start(f32[128,6]{0,1:T(8,128)S(1)} %get-tuple-element.119), channel_id=1, source_target_pairs={{0,24},{8,16},{16,8},{24,0},{1,25},{9,17},{17,9},{25,1},{2,26},{10... | collective-permute-start | bytes 9224 | tf_op jit(solution)/shard_map/ppermute | solution.py:117
  294.4 83.4 %all-to-all-start.5 = ((bf16[8,64,1024]{2,1,0:T(8,128)(2,1)}), bf16[8,64,1024]{2,1,0:T(8,128)(2,1)}, u32[]{:S(2)}, u32[]{:S(2)}) async-start(bf16[8,64,1024]{2,1,0:T(8,128)(2,1)} %bitcast.246), calls=%async_computation.5 | async-start | bytes 2097152 | tf_op jit(solution)/shard_map/all_to_all | solution.py:166
  299.5 18.5 %collective-permute-start.43 = (bf16[256,768]{1,0:T(8,128)(2,1)S(1)}, bf16[256,768]{1,0:T(8,128)(2,1)S(1)}, u32[]{:S(2)}, u32[]{:S(2)}) collective-permute-start(bf16[256,768]{1,0:T(8,128)(2,1)S(1)} %get-tuple-element.89), channel_id=1, source_target_pairs={{0,24},{8,16},{16,8},{24,0},{1,25},{9,17},{17,9},{25,1},{2,26},{10... | collective-permute-start | bytes 1179656 | tf_op jit(solution)/shard_map/ppermute | solution.py:117
  300.5 20.4 %collective-permute-start.41 = (bf16[256,768]{1,0:T(8,128)(2,1)S(1)}, bf16[256,768]{1,0:T(8,128)(2,1)S(1)}, u32[]{:S(2)}, u32[]{:S(2)}) collective-permute-start(bf16[256,768]{1,0:T(8,128)(2,1)S(1)} %get-tuple-element.90), channel_id=1, source_target_pairs={{0,16},{8,24},{16,0},{24,8},{1,17},{9,25},{17,1},{25,9},{2,18},{10... | collective-permute-start | bytes 1179656 | tf_op jit(solution)/shard_map/ppermute | solution.py:117
  301.5 28.8 %collective-permute-start.39 = (bf16[256,768]{1,0:T(8,128)(2,1)S(1)}, bf16[256,768]{1,0:T(8,128)(2,1)S(1)}, u32[]{:S(2)}, u32[]{:S(2)}) collective-permute-start(bf16[256,768]{1,0:T(8,128)(2,1)S(1)} %get-tuple-element.91), channel_id=1, source_target_pairs={{0,8},{8,0},{16,24},{24,16},{1,9},{9,1},{17,25},{25,17},{2,10},{10... | collective-permute-start | bytes 1179656 | tf_op jit(solution)/shard_map/ppermute | solution.py:117
  309.5 19.8 %collective-permute-start.44 = (bf16[256,768]{1,0:T(8,128)(2,1)S(1)}, bf16[256,768]{1,0:T(8,128)(2,1)S(1)}, u32[]{:S(2)}, u32[]{:S(2)}) collective-permute-start(bf16[256,768]{1,0:T(8,128)(2,1)S(1)} %get-tuple-element.93), channel_id=1, source_target_pairs={{0,24},{8,16},{16,8},{24,0},{1,25},{9,17},{17,9},{25,1},{2,26},{10... | collective-permute-start | bytes 1179656 | tf_op jit(solution)/shard_map/ppermute | solution.py:117
  310.6 35.6 %collective-permute-start.42 = (bf16[256,768]{1,0:T(8,128)(2,1)S(1)}, bf16[256,768]{1,0:T(8,128)(2,1)S(1)}, u32[]{:S(2)}, u32[]{:S(2)}) collective-permute-start(bf16[256,768]{1,0:T(8,128)(2,1)S(1)} %get-tuple-element.94), channel_id=1, source_target_pairs={{0,16},{8,24},{16,0},{24,8},{1,17},{9,25},{17,1},{25,9},{2,18},{10... | collective-permute-start | bytes 1179656 | tf_op jit(solution)/shard_map/ppermute | solution.py:117
  317.9 29.3 %collective-permute-start.49 = (bf16[256,768]{1,0:T(8,128)(2,1)S(1)}, bf16[256,768]{1,0:T(8,128)(2,1)S(1)}, u32[]{:S(2)}, u32[]{:S(2)}) collective-permute-start(bf16[256,768]{1,0:T(8,128)(2,1)S(1)} %get-tuple-element.81), channel_id=1, source_target_pairs={{0,24},{8,16},{16,8},{24,0},{1,25},{9,17},{17,9},{25,1},{2,26},{10... | collective-permute-start | bytes 1179656 | tf_op jit(solution)/shard_map/ppermute | solution.py:117
  320.9 26.9 %collective-permute-start.40 = (bf16[256,768]{1,0:T(8,128)(2,1)S(1)}, bf16[256,768]{1,0:T(8,128)(2,1)S(1)}, u32[]{:S(2)}, u32[]{:S(2)}) collective-permute-start(bf16[256,768]{1,0:T(8,128)(2,1)S(1)} %get-tuple-element.95), channel_id=1, source_target_pairs={{0,8},{8,0},{16,24},{24,16},{1,9},{9,1},{17,25},{25,17},{2,10},{10... | collective-permute-start | bytes 1179656 | tf_op jit(solution)/shard_map/ppermute | solution.py:117
  329.3 25.3 %collective-permute-start.50 = (bf16[256,768]{1,0:T(8,128)(2,1)S(1)}, bf16[256,768]{1,0:T(8,128)(2,1)S(1)}, u32[]{:S(2)}, u32[]{:S(2)}) collective-permute-start(bf16[256,768]{1,0:T(8,128)(2,1)S(1)} %get-tuple-element.85), channel_id=1, source_target_pairs={{0,24},{8,16},{16,8},{24,0},{1,25},{9,17},{17,9},{25,1},{2,26},{10... | collective-permute-start | bytes 1179656 | tf_op jit(solution)/shard_map/ppermute | solution.py:117
  330.4 32.2 %collective-permute-start.47 = (bf16[256,768]{1,0:T(8,128)(2,1)S(1)}, bf16[256,768]{1,0:T(8,128)(2,1)S(1)}, u32[]{:S(2)}, u32[]{:S(2)}) collective-permute-start(bf16[256,768]{1,0:T(8,128)(2,1)S(1)} %get-tuple-element.82), channel_id=1, source_target_pairs={{0,16},{8,24},{16,0},{24,8},{1,17},{9,25},{17,1},{25,9},{2,18},{10... | collective-permute-start | bytes 1179656 | tf_op jit(solution)/shard_map/ppermute | solution.py:117
  346.1 25.2 %collective-permute-start.48 = (bf16[256,768]{1,0:T(8,128)(2,1)S(1)}, bf16[256,768]{1,0:T(8,128)(2,1)S(1)}, u32[]{:S(2)}, u32[]{:S(2)}) collective-permute-start(bf16[256,768]{1,0:T(8,128)(2,1)S(1)} %get-tuple-element.86), channel_id=1, source_target_pairs={{0,16},{8,24},{16,0},{24,8},{1,17},{9,25},{17,1},{25,9},{2,18},{10... | collective-permute-start | bytes 1179656 | tf_op jit(solution)/shard_map/ppermute | solution.py:117
  347.3 24.7 %collective-permute-start.45 = (bf16[256,768]{1,0:T(8,128)(2,1)S(1)}, bf16[256,768]{1,0:T(8,128)(2,1)S(1)}, u32[]{:S(2)}, u32[]{:S(2)}) collective-permute-start(bf16[256,768]{1,0:T(8,128)(2,1)S(1)} %get-tuple-element.83), channel_id=1, source_target_pairs={{0,8},{8,0},{16,24},{24,16},{1,9},{9,1},{17,25},{25,17},{2,10},{10... | collective-permute-start | bytes 1179656 | tf_op jit(solution)/shard_map/ppermute | solution.py:117
  347.8 26.2 %collective-permute-start.46 = (bf16[256,768]{1,0:T(8,128)(2,1)S(1)}, bf16[256,768]{1,0:T(8,128)(2,1)S(1)}, u32[]{:S(2)}, u32[]{:S(2)}) collective-permute-start(bf16[256,768]{1,0:T(8,128)(2,1)S(1)} %get-tuple-element.87), channel_id=1, source_target_pairs={{0,8},{8,0},{16,24},{24,16},{1,9},{9,1},{17,25},{25,17},{2,10},{10... | collective-permute-start | bytes 1179656 | tf_op jit(solution)/shard_map/ppermute | solution.py:117
  354.6 31.0 %collective-permute-start.56 = (bf16[256,768]{1,0:T(8,128)(2,1)}, bf16[256,768]{1,0:T(8,128)(2,1)}, u32[]{:S(2)}, u32[]{:S(2)}) collective-permute-start(bf16[256,768]{1,0:T(8,128)(2,1)} %get-tuple-element.77), channel_id=1, source_target_pairs={{0,24},{8,16},{16,8},{24,0},{1,25},{9,17},{17,9},{25,1},{2,26},{10... | collective-permute-start | bytes 1179656 | tf_op jit(solution)/shard_map/ppermute | solution.py:117
  362.6 38.8 %collective-permute-start.54 = (bf16[256,768]{1,0:T(8,128)(2,1)}, bf16[256,768]{1,0:T(8,128)(2,1)}, u32[]{:S(2)}, u32[]{:S(2)}) collective-permute-start(bf16[256,768]{1,0:T(8,128)(2,1)} %get-tuple-element.78), channel_id=1, source_target_pairs={{0,16},{8,24},{16,0},{24,8},{1,17},{9,25},{17,1},{25,9},{2,18},{10... | collective-permute-start | bytes 1179656 | tf_op jit(solution)/shard_map/ppermute | solution.py:117
  371.4 34.3 %collective-permute-start.52 = (bf16[256,768]{1,0:T(8,128)(2,1)}, bf16[256,768]{1,0:T(8,128)(2,1)}, u32[]{:S(2)}, u32[]{:S(2)}) collective-permute-start(bf16[256,768]{1,0:T(8,128)(2,1)} %get-tuple-element.79), channel_id=1, source_target_pairs={{0,8},{8,0},{16,24},{24,16},{1,9},{9,1},{17,25},{25,17},{2,10},{10... | collective-permute-start | bytes 1179656 | tf_op jit(solution)/shard_map/ppermute | solution.py:117
  372.0 28.2 %collective-permute-start.55 = (bf16[256,768]{1,0:T(8,128)(2,1)}, bf16[256,768]{1,0:T(8,128)(2,1)}, u32[]{:S(2)}, u32[]{:S(2)}) collective-permute-start(bf16[256,768]{1,0:T(8,128)(2,1)} %get-tuple-element.73), channel_id=1, source_target_pairs={{0,24},{8,16},{16,8},{24,0},{1,25},{9,17},{17,9},{25,1},{2,26},{10... | collective-permute-start | bytes 1179656 | tf_op jit(solution)/shard_map/ppermute | solution.py:117
  374.0 30.5 %collective-permute-start.53 = (bf16[256,768]{1,0:T(8,128)(2,1)S(1)}, bf16[256,768]{1,0:T(8,128)(2,1)}, u32[]{:S(2)}, u32[]{:S(2)}) collective-permute-start(bf16[256,768]{1,0:T(8,128)(2,1)S(1)} %copy-done.22), channel_id=1, source_target_pairs={{0,16},{8,24},{16,0},{24,8},{1,17},{9,25},{17,1},{25,9},{2,18},{10... | collective-permute-start | bytes 1179656 | tf_op jit(solution)/shard_map/ppermute | solution.py:117
  377.8 33.6 %all-to-all-start.7 = ((bf16[8,64,1024]{2,1,0:T(8,128)(2,1)}), bf16[8,64,1024]{2,1,0:T(8,128)(2,1)}, u32[]{:S(2)}, u32[]{:S(2)}) async-start(bf16[8,64,1024]{2,1,0:T(8,128)(2,1)} %bitcast.244), calls=%async_computation.7 | async-start | bytes 2097152 | tf_op jit(solution)/shard_map/all_to_all | solution.py:166
  386.4 19.4 %collective-permute-start.51 = (bf16[256,768]{1,0:T(8,128)(2,1)S(1)}, bf16[256,768]{1,0:T(8,128)(2,1)S(1)}, u32[]{:S(2)}, u32[]{:S(2)}) collective-permute-start(bf16[256,768]{1,0:T(8,128)(2,1)S(1)} %copy-done.21), channel_id=1, source_target_pairs={{0,8},{8,0},{16,24},{24,16},{1,9},{9,1},{17,25},{25,17},{2,10},{10... | collective-permute-start | bytes 1179656 | tf_op jit(solution)/shard_map/ppermute | solution.py:117
  414.6 10.7 %collective-permute-start.33 = (bf16[128,1024]{1,0:T(8,128)(2,1)S(1)}, bf16[128,1024]{1,0:T(8,128)(2,1)S(1)}, u32[]{:S(2)}, u32[]{:S(2)}) collective-permute-start(bf16[128,1024]{1,0:T(8,128)(2,1)S(1)} %get-tuple-element.96), channel_id=1, source_target_pairs={{0,8},{8,0},{16,24},{24,16},{1,9},{9,1},{17,25},{25,17},{2,10},{10... | collective-permute-start | bytes 786440 | tf_op jit(solution)/shard_map/ppermute | solution.py:117
  415.4 13.5 %collective-permute-start.35 = (bf16[128,1024]{1,0:T(8,128)(2,1)S(1)}, bf16[128,1024]{1,0:T(8,128)(2,1)S(1)}, u32[]{:S(2)}, u32[]{:S(2)}) collective-permute-start(bf16[128,1024]{1,0:T(8,128)(2,1)S(1)} %get-tuple-element.97), channel_id=1, source_target_pairs={{0,24},{8,16},{16,8},{24,0},{1,25},{9,17},{17,9},{25,1},{2,26},{10... | collective-permute-start | bytes 786440 | tf_op jit(solution)/shard_map/ppermute | solution.py:117
  417.1 13.1 %collective-permute-start.34 = (bf16[128,1024]{1,0:T(8,128)(2,1)S(1)}, bf16[128,1024]{1,0:T(8,128)(2,1)S(1)}, u32[]{:S(2)}, u32[]{:S(2)}) collective-permute-start(bf16[128,1024]{1,0:T(8,128)(2,1)S(1)} %get-tuple-element.98), channel_id=1, source_target_pairs={{0,16},{8,24},{16,0},{24,8},{1,17},{9,25},{17,1},{25,9},{2,18},{10... | collective-permute-start | bytes 786440 | tf_op jit(solution)/shard_map/ppermute | solution.py:117
  (110 other events, 794.8 us)

commit v2 on v0

--- a/solution.py
+++ b/solution.py
@@ -1,10 +1,18 @@
 import jax
 import jax.numpy as jnp
 from jax import lax
+from jax.experimental import pallas as pl
+from jax.experimental.pallas import tpu as pltpu
 from jax.sharding import PartitionSpec as P
 
 EXPERTS = 64
 CAP = 16
+BF = jnp.bfloat16
+F32 = jnp.float32
+
+
+def dot(a, b, ca, cb):
+    return lax.dot_general(a, b, (((ca,), (cb,)), ((), ())), preferred_element_type=F32)
 
 
 def expand_rows(routed, weights):
@@ -19,7 +27,7 @@
     return jnp.einsum("erd,erf->def", routed, inner, preferred_element_type=jnp.float32)
 
 
-def body(tokens, expert_ids, route_weight, gate_weight, up_weight, down_weight, out_grad):
+def gathered_body(tokens, expert_ids, route_weight, gate_weight, up_weight, down_weight, out_grad):
     tok_count, model_width = tokens.shape
     top_count = expert_ids.shape[1]
     experts = EXPERTS
@@ -97,6 +105,341 @@
     return (layer_output, grad_tokens, grad_route, grad_gate, grad_up, down_summed)
 
 
+LIGHT, HEAVY = 1 << 10, 1 << 37
+
+
+def call(kernel, name, grid, in_specs, out_specs, out_shape, scratch=(), cost=LIGHT):
+    return pl.pallas_call(
+        kernel,
+        grid_spec=pltpu.PrefetchScalarGridSpec(
+            num_scalar_prefetch=1,
+            grid=grid,
+            in_specs=in_specs,
+            out_specs=out_specs,
+            scratch_shapes=scratch,
+        ),
+        out_shape=out_shape,
+        compiler_params=pltpu.CompilerParams(vmem_limit_bytes=48 << 20),
+        cost_estimate=pl.CostEstimate(flops=cost, transcendentals=0, bytes_accessed=1024),
+        name=name,
+    )
+
+
+def pick_kernel(me_ref, sel_ref, scale_ref, *refs):
+    pieces, out_ref = refs[:-1], refs[-1]
+    values = jnp.concatenate([p[...] for p in pieces], axis=0)
+    out_ref[...] = (dot(sel_ref[...], values, 1, 0) * scale_ref[...]).astype(BF)
+
+
+def forward_kernel(me_ref, x_ref, *refs):
+    nb = (len(refs) - 5) // 2
+    gates, ups = refs[:nb], refs[nb : 2 * nb]
+    a_ref, b_ref, h_ref, gate_acc, up_acc = refs[2 * nb :]
+    j = pl.program_id(1)
+    x = x_ref[...].reshape(gate_acc.shape[0], x_ref.shape[-1])
+    for s in range(nb):
+
+        @pl.when(j == s)
+        def _(s=s):
+            for acc, w in ((gate_acc, gates[s]), (up_acc, ups[s])):
+                part = dot(x, w[0], 1, 0)
+                acc[...] = part if s == 0 else acc[...] + part
+
+    @pl.when(j == nb - 1)
+    def _():
+        step = 64
+
+        @pl.loop(0, gate_acc.shape[0] // step)
+        def _(t):
+            at = pl.ds(pl.multiple_of(t * step, step), step)
+            gate, up = gate_acc[at, :], up_acc[at, :]
+            sig = jax.nn.sigmoid(gate)
+            act = gate * sig
+            h_ref[0, at, :] = (act * up).astype(BF)
+            a_ref[0, at, :] = up * sig * (1.0 + gate * (1.0 - sig))
+            b_ref[0, at, :] = act
+
+
+def outer_kernel(me_ref, x_ref, y_ref, *outs):
+    j = pl.program_id(1)
+    x = x_ref[...].reshape(y_ref.shape[1], x_ref.shape[-1])
+    for s in range(len(outs)):
+
+        @pl.when(j == s)
+        def _(s=s):
+            outs[s][0] = dot(x, y_ref[0], 0, 0).astype(BF)
+
+
+def middle_kernel(me_ref, sg_ref, h_ref, a_ref, b_ref, *refs):
+    nb = len(refs) - 4
+    downs = refs[:nb]
+    out_ref, gd_ref, ud_ref, acc = refs[nb:]
+    j = pl.program_id(1)
+    sg = sg_ref[...].reshape(acc.shape[0], sg_ref.shape[-1])
+    for s in range(nb):
+
+        @pl.when(j == s)
+        def _(s=s):
+            part = dot(sg, downs[s][0], 1, 0)
+            acc[...] = part if s == 0 else acc[...] + part
+            out_ref[...] = dot(h_ref[0], downs[s][0], 1, 1).astype(BF).reshape(out_ref.shape)
+
+    @pl.when(j == nb - 1)
+    def _():
+        step = 64
+
+        @pl.loop(0, acc.shape[0] // step)
+        def _(t):
+            at = pl.ds(pl.multiple_of(t * step, step), step)
+            gh = acc[at, :]
+            gd_ref[0, at, :] = (gh * a_ref[0, at, :]).astype(BF)
+            ud_ref[0, at, :] = (gh * b_ref[0, at, :]).astype(BF)
+
+
+def input_kernel(me_ref, gd_ref, ud_ref, *refs):
+    nb = (len(refs) - 1) // 2
+    gates, ups, out_ref = refs[:nb], refs[nb : 2 * nb], refs[-1]
+    j = pl.program_id(1)
+    for s in range(nb):
+
+        @pl.when(j == s)
+        def _(s=s):
+            total = dot(gd_ref[0], gates[s][0], 1, 1) + dot(ud_ref[0], ups[s][0], 1, 1)
+            out_ref[...] = total.astype(BF).reshape(out_ref.shape)
+
+
+def expert_body(tokens, expert_ids, route_weight, gate_weight, up_weight, down_weight, out_grad):
+    nb, ne = lax.axis_size("blk"), lax.axis_size("ep")
+    me = lax.axis_index("blk")
+    me_arr = me.reshape(1).astype(jnp.int32)
+    tok, width = tokens.shape
+    local_experts = gate_weight.shape[1]
+    own = local_experts // nb
+    chunk, inner = gate_weight.shape[0], gate_weight.shape[2]
+    per = nb * CAP
+    depth = ne * per
+    slots = own * depth
+    rows = nb * tok
+
+    def hop(x, j):
+        return lax.ppermute(x, "blk", [(i, i ^ j) for i in range(nb)])
+
+    def after(x, *deps):
+        return lax.optimization_barrier((x, deps))[0]
+
+    def spread(x, deps=None):
+        return [x] + [hop(x if deps is None else after(x, deps[j]), j) for j in range(1, nb)]
+
+    def prepare(w):
+        w = lax.optimization_barrier(jnp.swapaxes(w, 0, 1))
+        return w, [lax.dynamic_slice_in_dim(w, (me ^ j) * own, own, 0) for j in range(1, nb)]
+
+    def weight_pieces(prepared, deps):
+        w, parts = prepared
+        return [w] + [hop(after(parts[j - 1], deps[j]), j) for j in range(1, nb)]
+
+    high = lax.reduce_precision(route_weight, 8, 7)
+    mid = lax.reduce_precision(route_weight - high, 8, 7)
+    low = route_weight - high - mid
+    extra = jnp.concatenate([expert_ids.astype(F32), high, mid, low], axis=1).astype(BF)
+    extra = jnp.pad(extra, ((0, 0), (0, 128 - extra.shape[1])))
+    tok_p = spread(jnp.concatenate([tokens, extra], axis=1))
+    gate_ready = prepare(gate_weight)
+    tok_p, gate_ready = lax.optimization_barrier((tok_p, gate_ready))
+    og_p = spread(out_grad)
+    gate_p = weight_pieces(gate_ready, og_p)
+    up_ready, down_ready = prepare(up_weight), prepare(down_weight)
+    og_p, up_ready, down_ready = lax.optimization_barrier((og_p, up_ready, down_ready))
+    extra = jnp.concatenate([p[:, width:] for p in tok_p], axis=0).astype(F32)
+    top = expert_ids.shape[1]
+    ids_all = extra[:, :top].astype(jnp.int32)
+    rw_all = extra[:, top : 2 * top] + extra[:, 2 * top : 3 * top] + extra[:, 3 * top : 4 * top]
+
+    row = jnp.arange(rows)
+    before = ((row[:, None] > row[None, :]) & (row[:, None] // tok == row[None, :] // tok)).astype(BF)
+    slot = jnp.arange(slots)
+    slot_group, slot_rank = (slot // CAP) % nb, slot % CAP
+    experts = (jnp.arange(ne)[:, None] * local_experts + me * own + jnp.arange(own)[None, :]).reshape(-1)
+    eq = ids_all[:, :, None] == experts[None, None, :]
+    member = jnp.any(eq, axis=1)
+    weight = jnp.sum(jnp.where(eq, rw_all[:, :, None], 0.0), axis=1)
+    rank = dot(before, member.astype(BF), 1, 0)
+    rank = jnp.where(member, rank, -1.0).astype(jnp.int32)
+    rank_s = jnp.repeat(rank.T, per, axis=0)
+    weight_s = jnp.repeat(weight.T, per, axis=0)
+    hit = (rank_s == slot_rank[:, None]) & (slot_group[:, None] == row[None, :] // tok)
+    sel = hit.astype(BF)
+    sel_w = jnp.where(hit, weight_s, 0.0)
+
+    def pick(pieces, scale):
+        tile = slots // 4
+        return call(
+            pick_kernel,
+            "pick",
+            (slots // tile,),
+            [
+                pl.BlockSpec((tile, rows), lambda t, m: (t, 0)),
+                pl.BlockSpec((tile, 1), lambda t, m: (t, 0)),
+            ]
+            + [pl.BlockSpec((tok, width), lambda t, m: (0, 0))] * nb,
+            pl.BlockSpec((tile, width), lambda t, m: (t, 0)),
+            jax.ShapeDtypeStruct((slots, width), BF),
+        )(me_arr, sel, scale, *pieces)
+
+    previous = []
+
+    def exchange(x):
+        if previous:
+            x, _ = lax.optimization_barrier((x, previous[-1]))
+        x = x.reshape(ne, own * per, width)
+        previous.append(lax.all_to_all(x, "ep", split_axis=0, concat_axis=0, tiled=True))
+        return previous[-1].reshape(ne, own, per, width)
+
+    routed = exchange(pick(tok_p, jnp.ones((slots, 1), F32)))
+    slot_grad = pick(og_p, jnp.sum(sel_w, axis=1, keepdims=True))
+    up_ready = after(up_ready, slot_grad)
+    up_p = weight_pieces(up_ready, gate_p)
+    down_p = weight_pieces(down_ready, up_p)
+    graded = exchange(after(slot_grad, gate_p))
+
+    grid = (own, nb)
+    rows_spec = pl.BlockSpec((ne, None, per, chunk), lambda i, j, m: (0, i, 0, m[0] ^ j))
+    wide_spec = pl.BlockSpec((1, depth, inner), lambda i, j, m: (i, 0, 0))
+    piece_spec = pl.BlockSpec((1, chunk, inner), lambda i, j, m: (i, 0, 0))
+    first_spec = pl.BlockSpec((1, chunk, inner), lambda i, j, m: (m[0] * own + i, 0, 0))
+    weight_specs = [first_spec] + [piece_spec] * (nb - 1)
+    wide = lambda dt: jax.ShapeDtypeStruct((own, depth, inner), dt)
+    piece = jax.ShapeDtypeStruct((own, chunk, inner), BF)
+    full = jax.ShapeDtypeStruct((ne, own, per, width), BF)
+    acc = pltpu.VMEM((depth, inner), F32)
+
+    a, b, hidden = call(
+        forward_kernel,
+        "forward",
+        grid,
+        [rows_spec] + weight_specs * 2,
+        [wide_spec] * 3,
+        [wide(F32), wide(F32), wide(BF)],
+        [acc, acc],
+    )(me_arr, routed, *gate_p, *up_p)
+
+    def outer(x, y, cost):
+        return call(
+            outer_kernel,
+            "outer",
+            grid,
+            [rows_spec, wide_spec],
+            [piece_spec] * nb,
+            [piece] * nb,
+            (),
+            cost,
+        )(me_arr, x, y)
+
+    def send_back(parts, deps):
+        got = [parts[0]]
+        for j in range(1, nb):
+            got.append(hop(parts[j] if deps is None else after(parts[j], deps[j]), j))
+        return got
+
+    down_part = outer(graded, hidden, LIGHT)
+    down_got = send_back(down_part, None)
+    hidden = after(hidden, down_part)
+    outs, gate_delta, up_delta = call(
+        middle_kernel,
+        "middle",
+        grid,
+        [rows_spec] + [wide_spec] * 3 + weight_specs,
+        [rows_spec, wide_spec, wide_spec],
+        [full, wide(BF), wide(BF)],
+        [acc],
+    )(me_arr, graded, hidden, a, b, *down_p)
+    outs = exchange(outs).reshape(slots, width)
+    gate_part = outer(routed, after(gate_delta, down_got), LIGHT)
+    gate_part, up_delta = lax.optimization_barrier((gate_part, up_delta))
+    up_part = outer(routed, up_delta, HEAVY)
+    gate_got = send_back(gate_part, down_got)
+    gate_delta = after(gate_delta, up_part)
+    up_got = send_back(up_part, gate_got)
+    backs = call(
+        input_kernel,
+        "inputs",
+        grid,
+        [wide_spec] * 2 + weight_specs * 2,
+        rows_spec,
+        full,
+        (),
+        HEAVY,
+    )(me_arr, gate_delta, up_delta, *gate_p, *up_p)
+    down_got = after(down_got, backs)
+    backs = exchange(backs).reshape(slots, width)
+
+    grad_down = finish(down_got, me, HEAVY)
+    outs, grad_down = lax.optimization_barrier((outs, grad_down))
+    high = lax.reduce_precision(sel_w, 8, 7)
+    low = (sel_w - high).astype(BF)
+    high = high.astype(BF)
+    mixed = dot(high, outs, 0, 0) + dot(low, outs, 0, 0)
+    score = dot(outs, jnp.concatenate(og_p, 0), 1, 1)
+    score = jnp.where(hit, score, 0.0).reshape(ne * own, per, rows).sum(1)
+    route_grad = jnp.sum(jnp.where(eq, score.T[:, None, :], 0.0), axis=2)
+    grad_gate = finish(gate_got, me)
+    def gather_back(x, deps=None):
+        x = x.reshape((nb, tok) + x.shape[1:])
+        total = x[0].astype(F32)
+        for j in range(1, nb):
+            part = x[j] if deps is None else after(x[j], deps[j])
+            total += hop(part, j).astype(F32)
+        return total
+
+    mixed, grad_gate = lax.optimization_barrier((mixed, grad_gate))
+    layer_output = gather_back(mixed.astype(BF), up_got).astype(BF)
+    grad_route = gather_back(route_grad, up_got)
+    backs, grad_down, grad_gate, layer_output, grad_route = lax.optimization_barrier(
+        (backs, grad_down, grad_gate, layer_output, grad_route)
+    )
+    grad_tokens = gather_back(dot(sel, backs, 0, 0).astype(BF))
+    return (
+        layer_output,
+        grad_tokens,
+        grad_route,
+        grad_gate,
+        finish(up_got, me),
+        grad_down,
+    )
+
+
+def finish_kernel(me_ref, *refs):
+    nb = len(refs) - 3
+    pieces, out_ref, wide, sems = refs[:nb], refs[nb], refs[nb + 1], refs[nb + 2]
+    own = pieces[0].shape[0]
+    copies = []
+    for j in range(nb):
+        for i in range(own):
+            n = j * own + i
+            wide[n] = pieces[j][i].astype(F32)
+            place = (me_ref[0] ^ j) * own + i
+            copies.append(pltpu.make_async_copy(wide.at[n], out_ref.at[:, place, :], sems.at[n]))
+            copies[-1].start()
+    for copy in copies:
+        copy.wait()
+
+
+def finish(pieces, me, cost=LIGHT):
+    nb = len(pieces)
+    own, chunk, inner = pieces[0].shape
+    full = nb * own
+    return call(
+        finish_kernel,
+        "finish",
+        (1,),
+        [pl.BlockSpec((own, chunk, inner), lambda t, m: (0, 0, 0))] * nb,
+        pl.BlockSpec(memory_space=pl.ANY),
+        jax.ShapeDtypeStruct((chunk, full, inner), F32),
+        [pltpu.VMEM((full, chunk, inner), F32), pltpu.SemaphoreType.DMA((full,))],
+        cost,
+    )(me.reshape(1).astype(jnp.int32), *pieces)
+
+
 def solution(mesh):
     in_specs = (
         P(("blk", "ep"), None),
@@ -115,4 +458,7 @@
         P("blk", "ep", None),
         P("blk", "ep", None),
     )
+    nb, ne = mesh.shape["blk"], mesh.shape["ep"]
+    whole_experts = nb & (nb - 1) == 0 and (EXPERTS // ne) % nb == 0
+    body = expert_body if whole_experts else gathered_body
     return jax.shard_map(body, mesh=mesh, in_specs=in_specs, out_specs=out_specs, check_vma=False)

time: 797 us -> 314 us (0.39)
  waiting for transfers between devices: 529 us -> 128 us
  Pallas kernels: 0 us -> 71 us
  matrix products: 80.5 us -> 12.3 us
  local copies, waits for them, and re-layouts: 94.7 us -> 31.9 us
  other arithmetic: 50.8 us -> 9.54 us
  starting transfers between devices: 21 us -> 58.7 us
  between operations: 14.2 us -> 1.17 us
    all_gather x3 -> x0, waiting for transfers between devices: 222 us -> none  [the longest x1 116 us: body(): lax.all_gather(down_weight, 'blk', axis=0, tiled=True)]
    reduce_scatter x2 -> x0, waiting for transfers between devices: 163 us -> none  [the longest x1 163 us: body(): lax.psum_scatter(jnp.stack([outer_rows(received, gate_delta), outer_rows(...]
    all_to_all x4, waiting for transfers between devices: 144 us -> 5 us  [exchange(): lax.all_to_all(x, 'ep', split_axis=0, concat_axis=0, tiled=True)]
    ppermute x0 -> x33, waiting for transfers between devices: none -> 123 us  [hop(): return lax.ppermute(x, 'blk', [(i, i ^ j) for i in range(nb)])]
    pallas_call x0 -> x11, Pallas kernels: none -> 71 us  [the longest x3 21.2 us: outer(): call(outer_kernel, 'outer', grid, [rows_spec, wide_spec], [piece_spec] *...]
    dot_general x9 -> x5, matrix products: 80.5 us -> 12.3 us  [dot(): lax.dot_general(a, b, (((ca,), (cb,)), ((), ())), preferred_element_type=...]
    ppermute x0 -> x33, starting transfers between devices: none -> 39.1 us  [hop(): return lax.ppermute(x, 'blk', [(i, i ^ j) for i in range(nb)])]
    another operation x3 -> x2, other arithmetic: 22.8 us -> 1.38 us  [the longest x1 21 us: body(): jnp.stack([outer_rows(received, gate_delta), outer_rows(received, up_delt...]
  transfers between devices with their start and end apart: 9 -> 37, of which waited for: 7 -> 19; matrix products, arithmetic and copies ran while one was open for 21% -> 8% of each run, Pallas kernels for 0% -> 22%
where the time goes in v2:
time: 314 us; the launch traced here: 313 us
  waiting for transfers between devices  128 us (41%)
  Pallas kernels  71 us (23%)
  starting transfers between devices  58.7 us (19%)
  local copies, waits for them, and re-layouts  31.9 us (10%)
  matrix products  12.3 us (4%)
  other arithmetic  9.54 us (3%)
    ppermute x33, waiting for transfers between devices, hop(): return lax.ppermute(x, 'blk', [(i, i ^ j) for i in range(nb)])  123 us
    ppermute x33, starting transfers between devices, hop(): return lax.ppermute(x, 'blk', [(i, i ^ j) for i in range(nb)])  39.1 us
    unnamed x105, local copies, waits for them, and re-layouts  25.3 us
    pallas_call x3, Pallas kernels, outer(): call(outer_kernel, 'outer', grid, [rows_spec, wide_spec], [piece_spec] *...  21.2 us
    all_to_all x4, starting transfers between devices, exchange(): lax.all_to_all(x, 'ep', split_axis=0, concat_axis=0, tiled=True)  19.6 us
    dot_general x5, matrix products, dot(): lax.dot_general(a, b, (((ca,), (cb,)), ((), ())), preferred_element_type=...  12.3 us
    pallas_call x1, Pallas kernels, expert_body(): call(forward_kernel, 'forward', grid, [rows_spec] + weight_specs * 2, [wi...  11.8 us
    pallas_call x3, Pallas kernels, finish(): call(finish_kernel, 'finish', (1,), [pl.BlockSpec((own, chunk, inner), la...  11.7 us
  transfers between devices with their start and end apart: 37, of which 19 were waited for; matrix products, arithmetic and copies ran while one was open for 8% of the time, Pallas kernels for 22%

profile of v2, /device:TPU:0, one launch (start us, length us, event | category | flops | bytes accessed | tf_op | source)
XLA Modules:
  0.0 312.9 jit_solution(10086595226499181233)
XLA Ops:
  3.1 3.0 collective-permute-start
  6.1 1.5 collective-permute-start.1
  7.8 4.2 %copy.51 = bf16[256,8,768]{2,0,1:T(8,128)(2,1)} copy(bf16[256,8,768]{2,1,0:T(8,128)(2,1)} %param.10) | data formatting | bytes 6291456 | tf_op args[3]
  12.0 3.1 constant_dynamic-slice_fusion.6
  15.1 5.8 %collective-permute-done.1.refs_2_ = bf16[128,1152]{1,0:T(8,128)(2,1)S(1)} collective-permute-done((bf16[128,1152]{1,0:T(8,128)(2,1)S(1)}, bf16[128,1152]{1,0:T(8,128)(2,1)S(1)}, u32[]{:S(2)}, u32[]{:S(2)}) %collective-permute-start.1) | collective-permute-done | bytes 294944 | tf_op jit(solution)/shard_map/ppermute | solution.py:225
  22.1 1.7 fusion
  24.6 3.1 pick.3
  27.7 5.0 %all-to-all-start = ((bf16[8,128,1024]{2,1,0:T(8,128)(2,1)}), bf16[8,128,1024]{2,1,0:T(8,128)(2,1)}, u32[]{:S(2)}, u32[]{:S(2)}) async-start(bf16[8,128,1024]{2,1,0:T(8,128)(2,1)} %bitcast.7), calls=%async_computation | async-start | bytes 4194304 | tf_op jit(solution)/shard_map/all_to_all | solution.py:295
  32.7 1.6 collective-permute-start.5
  34.2 1.2 collective-permute-start.4
  36.2 6.6 %collective-permute-done.5.refs_3_ = bf16[128,1024]{1,0:T(8,128)(2,1)S(1)} collective-permute-done((bf16[128,1024]{1,0:T(8,128)(2,1)S(1)}, bf16[128,1024]{1,0:T(8,128)(2,1)S(1)}, u32[]{:S(2)}, u32[]{:S(2)}) %collective-permute-start.5) | collective-permute-done | bytes 262176 | tf_op jit(solution)/shard_map/ppermute | solution.py:225
  42.8 1.5 collective-permute-start.8
  44.3 4.0 %collective-permute-done.4.refs_2_ = bf16[128,1024]{1,0:T(8,128)(2,1)S(1)} collective-permute-done((bf16[128,1024]{1,0:T(8,128)(2,1)S(1)}, bf16[128,1024]{1,0:T(8,128)(2,1)S(1)}, u32[]{:S(2)}, u32[]{:S(2)}) %collective-permute-start.4) | collective-permute-done | bytes 262176 | tf_op jit(solution)/shard_map/ppermute | solution.py:225
  48.3 1.5 collective-permute-start.7
  51.1 2.5 copy.50
  55.3 2.5 constant_dynamic-slice_fusion
  61.7 3.0 pick.2
  65.3 16.4 %collective-permute-done.7.refs_2_ = bf16[2,256,768]{2,1,0:T(8,128)(2,1)S(1)} collective-permute-done((bf16[2,256,768]{2,1,0:T(8,128)(2,1)}, bf16[2,256,768]{2,1,0:T(8,128)(2,1)S(1)}, u32[]{:S(2)}, u32[]{:S(2)}) %collective-permute-start.7) | collective-permute-done | bytes 786464 | tf_op jit(solution)/shard_map/ppermute | solution.py:225
  82.6 4.7 %all-to-all-start.1 = ((bf16[8,128,1024]{2,1,0:T(8,128)(2,1)}), bf16[8,128,1024]{2,1,0:T(8,128)(2,1)}, u32[]{:S(2)}, u32[]{:S(2)}) async-start(bf16[8,128,1024]{2,1,0:T(8,128)(2,1)} %bitcast.8), calls=%async_computation.1 | async-start | bytes 4194304 | tf_op jit(solution)/shard_map/all_to_all | solution.py:295
  87.3 1.5 collective-permute-start.11
  88.8 1.2 collective-permute-start.10
  90.8 18.0 %collective-permute-done.11.refs_7_ = bf16[2,256,768]{2,1,0:T(8,128)(2,1)S(1)} collective-permute-done((bf16[2,256,768]{2,1,0:T(8,128)(2,1)}, bf16[2,256,768]{2,1,0:T(8,128)(2,1)S(1)}, u32[]{:S(2)}, u32[]{:S(2)}) %collective-permute-start.11) | collective-permute-done | bytes 786464 | tf_op jit(solution)/shard_map/ppermute | solution.py:225
  108.8 1.5 collective-permute-start.14
  110.3 15.3 %collective-permute-done.10.refs_6_ = bf16[2,256,768]{2,1,0:T(8,128)(2,1)S(1)} collective-permute-done((bf16[2,256,768]{2,1,0:T(8,128)(2,1)}, bf16[2,256,768]{2,1,0:T(8,128)(2,1)S(1)}, u32[]{:S(2)}, u32[]{:S(2)}) %collective-permute-start.10) | collective-permute-done | bytes 786464 | tf_op jit(solution)/shard_map/ppermute | solution.py:225
  125.6 1.5 collective-permute-start.13
  129.9 11.8 %forward.1 = (f32[2,512,768]{2,1,0:T(8,128)}, f32[2,512,768]{2,1,0:T(8,128)}, bf16[2,512,768]{2,1,0:T(8,128)(2,1)}) custom-call(s32[1]{0:T(128)} %bitcast.me_ref, bf16[8,2,64,1024]{3,2,1,0:T(8,128)(2,1)} %bitcast.10.x_ref, bf16[8,256,768]{2,1,0:T(8,128)(2,1)} %bitcast.49, bf16[2,256,768]{2,1,0:T(8,128)(2,1)} %collective-permute-done.6.refs_1_, ...), custom_call_target="tpu_custom_call" | custom-call | flops 1024 | bytes 1024 | tf_op jit(solution)/shard_map/forward/pallas_call | solution.py:316
  143.5 1.4 copy-done
  144.9 7.5 %outer.3 = (bf16[2,256,768]{2,1,0:T(8,128)(2,1)S(1)}, bf16[2,256,768]{2,1,0:T(8,128)(2,1)}, bf16[2,256,768]{2,1,0:T(8,128)(2,1)}, bf16[2,256,768]{2,1,0:T(8,128)(2,1)}) custom-call(s32[1]{0:T(128)} %bitcast.me_ref, bf16[8,2,64,1024]{3,2,1,0:T(8,128)(2,1)} %bitcast.9.x_ref.sg_ref, bf16[2,512,768]{2,1,0:T(8,128)(2,1)S(1)} %copy-done), custom_call_target="tpu_custom_call" | custom-call | flops 1024 | bytes 1024 | tf_op jit(solution)/shard_map/outer/pallas_call | solution.py:327
  152.4 1.5 collective-permute-start.15
  154.4 1.5 collective-permute-start.17
  155.9 1.3 reduce-precision_convert_fusion
  157.2 1.9 collective-permute-done.13.refs_2_
  161.6 11.1 %middle.1 = (bf16[8,2,64,1024]{3,2,1,0:T(8,128)(2,1)}, bf16[2,512,768]{2,1,0:T(8,128)(2,1)S(1)}, bf16[2,512,768]{2,1,0:T(8,128)(2,1)S(1)}) custom-call(s32[1]{0:T(128)} %bitcast.me_ref, bf16[8,2,64,1024]{3,2,1,0:T(8,128)(2,1)} %bitcast.9.x_ref.sg_ref, bf16[2,512,768]{2,1,0:T(8,128)(2,1)} %get-tuple-element.127.y_ref.h_ref, ...), custom_call_target="tpu_custom_call" | custom-call | flops 1024 | bytes 1024 | tf_op jit(solution)/shard_map/middle/pallas_call | solution.py:347
  172.7 1.2 copy-done.28
  173.9 5.1 %all-to-all-start.2 = ((bf16[8,128,1024]{2,1,0:T(8,128)(2,1)}), bf16[8,128,1024]{2,1,0:T(8,128)(2,1)}, u32[]{:S(2)}, u32[]{:S(2)}) async-start(bf16[8,128,1024]{2,1,0:T(8,128)(2,1)} %bitcast.52), calls=%async_computation.2 | async-start | bytes 4194304 | tf_op jit(solution)/shard_map/all_to_all | solution.py:295
  179.0 13.8 %collective-permute-done.17.refs_3_ = bf16[2,256,768]{2,1,0:T(8,128)(2,1)} collective-permute-done((bf16[2,256,768]{2,1,0:T(8,128)(2,1)}, bf16[2,256,768]{2,1,0:T(8,128)(2,1)}, u32[]{:S(2)}, u32[]{:S(2)}) %collective-permute-start.17) | collective-permute-done | bytes 786464 | tf_op jit(solution)/shard_map/ppermute | solution.py:225
  192.9 7.5 %outer.4 = (bf16[2,256,768]{2,1,0:T(8,128)(2,1)S(1)}, bf16[2,256,768]{2,1,0:T(8,128)(2,1)}, bf16[2,256,768]{2,1,0:T(8,128)(2,1)}, bf16[2,256,768]{2,1,0:T(8,128)(2,1)}) custom-call(s32[1]{0:T(128)} %bitcast.me_ref, bf16[8,2,64,1024]{3,2,1,0:T(8,128)(2,1)} %bitcast.10.x_ref, bf16[2,512,768]{2,1,0:T(8,128)(2,1)S(1)} %get-tuple-element.149.y_ref.gd_ref), custom_call_target="tpu_custom_call" | custom-call | flops 1024 | bytes 1024 | tf_op jit(solution)/shard_map/outer/pallas_call | solution.py:327
  201.3 1.3 collective-permute-start.18
  202.6 6.2 %outer.5 = (bf16[2,256,768]{2,1,0:T(8,128)(2,1)S(1)}, bf16[2,256,768]{2,1,0:T(8,128)(2,1)S(1)}, bf16[2,256,768]{2,1,0:T(8,128)(2,1)S(1)}, bf16[2,256,768]{2,1,0:T(8,128)(2,1)S(1)}) custom-call(s32[1]{0:T(128)} %bitcast.me_ref, bf16[8,2,64,1024]{3,2,1,0:T(8,128)(2,1)} %bitcast.10.x_ref, bf16[2,512,768]{2,1,0:T(8,128)(2,1)S(1)} %copy-done.29), custom_call_target="tpu_custom_call" | custom-call | flops 137438953472 | bytes 1024 | tf_op jit(solution)/shard_map/outer/pallas_call | solution.py:327
  212.6 1.4 collective-permute-start.20
  214.0 9.2 %inputs.1 = bf16[8,2,64,1024]{3,2,1,0:T(8,128)(2,1)} custom-call(s32[1]{0:T(128)} %bitcast.me_ref, bf16[2,512,768]{2,1,0:T(8,128)(2,1)} %copy-done.1, bf16[2,512,768]{2,1,0:T(8,128)(2,1)} %copy-done.28, bf16[8,256,768]{2,1,0:T(8,128)(2,1)} %bitcast.50, bf16[2,256,768]{2,1,0:T(8,128)(2,1)} %collective-permute-done.6.refs_1_, ...), custom_call_target="tpu_custom_call" | custom-call | flops 137438953472 | bytes 1024 | tf_op jit(solution)/shard_map/inputs/pallas_call | solution.py:363
  223.2 5.0 %all-to-all-done.2 = bf16[8,128,1024]{2,1,0:T(8,128)(2,1)} async-done(((bf16[8,128,1024]{2,1,0:T(8,128)(2,1)}), bf16[8,128,1024]{2,1,0:T(8,128)(2,1)}, u32[]{:S(2)}, u32[]{:S(2)}) %all-to-all-start.2) | async-done | bytes 2097184 | tf_op jit(solution)/shard_map/all_to_all | solution.py:295
  228.2 4.7 %all-to-all-start.3 = ((bf16[8,128,1024]{2,1,0:T(8,128)(2,1)}), bf16[8,128,1024]{2,1,0:T(8,128)(2,1)}, u32[]{:S(2)}, u32[]{:S(2)}) async-start(bf16[8,128,1024]{2,1,0:T(8,128)(2,1)} %bitcast.51), calls=%async_computation.3 | async-start | bytes 4194304 | tf_op jit(solution)/shard_map/all_to_all | solution.py:295
  233.0 4.5 %finish.3 = f32[256,8,768]{2,1,0:T(8,128)} custom-call(s32[1]{0:T(128)} %bitcast.me_ref, bf16[2,256,768]{2,1,0:T(8,128)(2,1)S(1)} %copy-done.31, bf16[2,256,768]{2,1,0:T(8,128)(2,1)} %collective-permute-done.15.refs_1_, bf16[2,256,768]{2,1,0:T(8,128)(2,1)} %collective-permute-done.16.refs_2_, bf16[2,256,768]{2,1,0:T(8,128)(2,1)} %collective-permute-done.17.refs_3_), custom_call_target="tpu_custom_call" | custom-call | flops 137438953472 | bytes 1024 | tf_op jit(solution)/shard_map/finish/pallas_call | solution.py:431
  238.1 9.5 %collective-permute-done.19.refs_2_ = bf16[2,256,768]{2,1,0:T(8,128)(2,1)} collective-permute-done((bf16[2,256,768]{2,1,0:T(8,128)(2,1)}, bf16[2,256,768]{2,1,0:T(8,128)(2,1)}, u32[]{:S(2)}, u32[]{:S(2)}) %collective-permute-start.19) | collective-permute-done | bytes 786464 | tf_op jit(solution)/shard_map/ppermute | solution.py:225
  248.5 1.6 collective-permute-start.25
  250.1 4.4 %finish.4 = f32[256,8,768]{2,1,0:T(8,128)} custom-call(s32[1]{0:T(128)} %bitcast.me_ref, bf16[2,256,768]{2,1,0:T(8,128)(2,1)S(1)} %copy-done.17, bf16[2,256,768]{2,1,0:T(8,128)(2,1)} %collective-permute-done.18.refs_1_, bf16[2,256,768]{2,1,0:T(8,128)(2,1)} %collective-permute-done.19.refs_2_, bf16[2,256,768]{2,1,0:T(8,128)(2,1)} %collective-permute-done.20.refs_3_), custom_call_target="tpu_custom_call" | custom-call | flops 1024 | bytes 1024 | tf_op jit(solution)/shard_map/finish/pallas_call | solution.py:431
  254.5 3.0 fusion.44
  257.5 3.0 convolution_add_fusion
  260.6 1.1 collective-permute-start.22
  261.7 20.9 %collective-permute-done.23.refs_2_ = bf16[2,256,768]{2,1,0:T(8,128)(2,1)S(1)} collective-permute-done((bf16[2,256,768]{2,1,0:T(8,128)(2,1)S(1)}, bf16[2,256,768]{2,1,0:T(8,128)(2,1)S(1)}, u32[]{:S(2)}, u32[]{:S(2)}) %collective-permute-start.23) | collective-permute-done | bytes 786464 | tf_op jit(solution)/shard_map/ppermute | solution.py:225
  283.2 1.7 collective-permute-start.26
  284.9 2.9 bitcast_reduce_fusion
  288.0 1.3 collective-permute-start.27
  289.8 1.8 collective-permute-done.27
  291.6 1.2 collective-permute-start.29
  292.9 1.5 collective-permute-done.28
  294.4 1.7 collective-permute-done.29
  297.6 3.1 convolution_convert_fusion
  300.8 1.3 collective-permute-start.30
  302.6 1.7 collective-permute-start.32
  304.3 2.8 finish.5
  307.1 2.0 collective-permute-done.30
  309.1 2.9 collective-permute-done.31
  (167 shorter events, 32.8 us)
Async XLA Ops:
  3.1 12.0 %collective-permute-start = (bf16[128,1152]{1,0:T(8,128)(2,1)S(1)}, bf16[128,1152]{1,0:T(8,128)(2,1)S(1)}, u32[]{:S(2)}, u32[]{:S(2)}) collective-permute-start(bf16[128,1152]{1,0:T(8,128)(2,1)S(1)} %fusion.18.refs_0_), channel_id=1, source_target_pairs={{0,8},{8,0},{16,24},{24,16},{1,9},{9,1},{17,25},{25,17},{2,10},{10... | collective-permute-start | bytes 884744 | tf_op jit(solution)/shard_map/ppermute | solution.py:225
  6.1 14.8 %collective-permute-start.1 = (bf16[128,1152]{1,0:T(8,128)(2,1)S(1)}, bf16[128,1152]{1,0:T(8,128)(2,1)S(1)}, u32[]{:S(2)}, u32[]{:S(2)}) collective-permute-start(bf16[128,1152]{1,0:T(8,128)(2,1)S(1)} %fusion.18.refs_0_), channel_id=1, source_target_pairs={{0,16},{8,24},{16,0},{24,8},{1,17},{9,25},{17,1},{25,9},{2,18},{10... | collective-permute-start | bytes 884744 | tf_op jit(solution)/shard_map/ppermute | solution.py:225
  7.7 13.3 %collective-permute-start.2 = (bf16[128,1152]{1,0:T(8,128)(2,1)S(1)}, bf16[128,1152]{1,0:T(8,128)(2,1)S(1)}, u32[]{:S(2)}, u32[]{:S(2)}) collective-permute-start(bf16[128,1152]{1,0:T(8,128)(2,1)S(1)} %fusion.18.refs_0_), channel_id=1, source_target_pairs={{0,24},{8,16},{16,8},{24,0},{1,25},{9,17},{17,9},{25,1},{2,26},{10... | collective-permute-start | bytes 884744 | tf_op jit(solution)/shard_map/ppermute | solution.py:225
  12.0 9.6 %copy-start.49 = (s32[16]{0:T(128)}, s32[16]{0:T(128)S(1)}, u32[]{:S(2)}) copy-start(s32[16]{0:T(128)S(1)} %add.138) | copy-start | bytes 196
  27.7 5.0 %copy-start.18 = (bf16[128,1024]{1,0:T(8,128)(2,1)S(1)}, bf16[128,1024]{1,0:T(8,128)(2,1)}, u32[]{:S(2)}) copy-start(bf16[128,1024]{1,0:T(8,128)(2,1)} %refs_0_) | copy-start | bytes 786436
  27.7 54.3 %all-to-all-start = ((bf16[8,128,1024]{2,1,0:T(8,128)(2,1)}), bf16[8,128,1024]{2,1,0:T(8,128)(2,1)}, u32[]{:S(2)}, u32[]{:S(2)}) async-start(bf16[8,128,1024]{2,1,0:T(8,128)(2,1)} %bitcast.7), calls=%async_computation | async-start | bytes 4194304 | tf_op jit(solution)/shard_map/all_to_all | solution.py:295
  32.7 20.9 %copy-start.44 = (bf16[256,8,768]{2,1,0:T(8,128)(2,1)S(1)}, bf16[256,8,768]{2,1,0:T(8,128)(2,1)}, u32[]{:S(2)}) copy-start(bf16[256,8,768]{2,1,0:T(8,128)(2,1)} %param.12) | copy-start | bytes 9437188
  32.7 10.1 %collective-permute-start.5 = (bf16[128,1024]{1,0:T(8,128)(2,1)S(1)}, bf16[128,1024]{1,0:T(8,128)(2,1)S(1)}, u32[]{:S(2)}, u32[]{:S(2)}) collective-permute-start(bf16[128,1024]{1,0:T(8,128)(2,1)S(1)} %copy-done.18), channel_id=1, source_target_pairs={{0,24},{8,16},{16,8},{24,0},{1,25},{9,17},{17,9},{25,1},{2,26},{10... | collective-permute-start | bytes 786440 | tf_op jit(solution)/shard_map/ppermute | solution.py:225
  34.2 14.1 %collective-permute-start.4 = (bf16[128,1024]{1,0:T(8,128)(2,1)S(1)}, bf16[128,1024]{1,0:T(8,128)(2,1)S(1)}, u32[]{:S(2)}, u32[]{:S(2)}) collective-permute-start(bf16[128,1024]{1,0:T(8,128)(2,1)S(1)} %copy-done.18), channel_id=1, source_target_pairs={{0,16},{8,24},{16,0},{24,8},{1,17},{9,25},{17,1},{25,9},{2,18},{10... | collective-permute-start | bytes 786440 | tf_op jit(solution)/shard_map/ppermute | solution.py:225
  35.4 14.4 %collective-permute-start.3 = (bf16[128,1024]{1,0:T(8,128)(2,1)S(1)}, bf16[128,1024]{1,0:T(8,128)(2,1)S(1)}, u32[]{:S(2)}, u32[]{:S(2)}) collective-permute-start(bf16[128,1024]{1,0:T(8,128)(2,1)S(1)} %copy-done.18), channel_id=1, source_target_pairs={{0,8},{8,0},{16,24},{24,16},{1,9},{9,1},{17,25},{25,17},{2,10},{10... | collective-permute-start | bytes 786440 | tf_op jit(solution)/shard_map/ppermute | solution.py:225
  42.8 10.8 %copy-start.19 = (bf16[128,1024]{1,0:T(8,128)(2,1)}, bf16[128,1024]{1,0:T(8,128)(2,1)S(1)}, u32[]{:S(2)}) copy-start(bf16[128,1024]{1,0:T(8,128)(2,1)S(1)} %collective-permute-done.5.refs_3_) | copy-start | bytes 786436
  42.8 22.5 %collective-permute-start.8 = (bf16[2,256,768]{2,1,0:T(8,128)(2,1)}, bf16[2,256,768]{2,1,0:T(8,128)(2,1)S(1)}, u32[]{:S(2)}, u32[]{:S(2)}) collective-permute-start(bf16[2,256,768]{2,1,0:T(8,128)(2,1)} %get-tuple-element.108), channel_id=1, source_target_pairs={{0,24},{8,16},{16,8},{24,0},{1,25},{9,17},{17,9},{25,1},{2,26},{10... | collective-permute-start | bytes 2359304 | tf_op jit(solution)/shard_map/ppermute | solution.py:225
  48.3 5.3 %copy-start.22 = (bf16[128,1024]{1,0:T(8,128)(2,1)}, bf16[128,1024]{1,0:T(8,128)(2,1)S(1)}, u32[]{:S(2)}) copy-start(bf16[128,1024]{1,0:T(8,128)(2,1)S(1)} %collective-permute-done.4.refs_2_) | copy-start | bytes 786436
  48.3 33.4 %collective-permute-start.7 = (bf16[2,256,768]{2,1,0:T(8,128)(2,1)}, bf16[2,256,768]{2,1,0:T(8,128)(2,1)S(1)}, u32[]{:S(2)}, u32[]{:S(2)}) collective-permute-start(bf16[2,256,768]{2,1,0:T(8,128)(2,1)} %get-tuple-element.106), channel_id=1, source_target_pairs={{0,16},{8,24},{16,0},{24,8},{1,17},{9,25},{17,1},{25,9},{2,18},{10... | collective-permute-start | bytes 2359304 | tf_op jit(solution)/shard_map/ppermute | solution.py:225
  50.5 31.4 %collective-permute-start.6 = (bf16[2,256,768]{2,1,0:T(8,128)(2,1)}, bf16[2,256,768]{2,1,0:T(8,128)(2,1)}, u32[]{:S(2)}, u32[]{:S(2)}) collective-permute-start(bf16[2,256,768]{2,1,0:T(8,128)(2,1)} %get-tuple-element.104), channel_id=1, source_target_pairs={{0,8},{8,0},{16,24},{24,16},{1,9},{9,1},{17,25},{25,17},{2,10},{10... | collective-permute-start | bytes 2359304 | tf_op jit(solution)/shard_map/ppermute | solution.py:225
  65.3 16.6 %copy-start.4 = (bf16[2,256,768]{2,1,0:T(8,128)(2,1)}, bf16[2,256,768]{2,1,0:T(8,128)(2,1)S(1)}, u32[]{:S(2)}) copy-start(bf16[2,256,768]{2,1,0:T(8,128)(2,1)S(1)} %collective-permute-done.8.refs_3_) | copy-start | bytes 2359300
  81.9 8.1 %copy-start.46 = (bf16[2,256,768]{2,1,0:T(8,128)(2,1)S(1)}, bf16[2,256,768]{2,1,0:T(8,128)(2,1)}, u32[]{:S(2)}) copy-start(bf16[2,256,768]{2,1,0:T(8,128)(2,1)} %get-tuple-element.117) | copy-start | bytes 2359300
  82.6 60.9 %all-to-all-start.1 = ((bf16[8,128,1024]{2,1,0:T(8,128)(2,1)}), bf16[8,128,1024]{2,1,0:T(8,128)(2,1)}, u32[]{:S(2)}, u32[]{:S(2)}) async-start(bf16[8,128,1024]{2,1,0:T(8,128)(2,1)} %bitcast.8), calls=%async_computation.1 | async-start | bytes 4194304 | tf_op jit(solution)/shard_map/all_to_all | solution.py:295
  87.3 21.5 %collective-permute-start.11 = (bf16[2,256,768]{2,1,0:T(8,128)(2,1)}, bf16[2,256,768]{2,1,0:T(8,128)(2,1)S(1)}, u32[]{:S(2)}, u32[]{:S(2)}) collective-permute-start(bf16[2,256,768]{2,1,0:T(8,128)(2,1)} %get-tuple-element.121), channel_id=1, source_target_pairs={{0,24},{8,16},{16,8},{24,0},{1,25},{9,17},{17,9},{25,1},{2,26},{10... | collective-permute-start | bytes 2359304 | tf_op jit(solution)/shard_map/ppermute | solution.py:225
  88.8 36.8 %collective-permute-start.10 = (bf16[2,256,768]{2,1,0:T(8,128)(2,1)}, bf16[2,256,768]{2,1,0:T(8,128)(2,1)S(1)}, u32[]{:S(2)}, u32[]{:S(2)}) collective-permute-start(bf16[2,256,768]{2,1,0:T(8,128)(2,1)} %get-tuple-element.119), channel_id=1, source_target_pairs={{0,16},{8,24},{16,0},{24,8},{1,17},{9,25},{17,1},{25,9},{2,18},{10... | collective-permute-start | bytes 2359304 | tf_op jit(solution)/shard_map/ppermute | solution.py:225
  90.0 37.1 %collective-permute-start.9 = (bf16[2,256,768]{2,1,0:T(8,128)(2,1)S(1)}, bf16[2,256,768]{2,1,0:T(8,128)(2,1)S(1)}, u32[]{:S(2)}, u32[]{:S(2)}) collective-permute-start(bf16[2,256,768]{2,1,0:T(8,128)(2,1)S(1)} %copy-done.46), channel_id=1, source_target_pairs={{0,8},{8,0},{16,24},{24,16},{1,9},{9,1},{17,25},{25,17},{2,10},{10... | collective-permute-start | bytes 2359304 | tf_op jit(solution)/shard_map/ppermute | solution.py:225
  108.8 32.8 %copy-start.10 = (bf16[2,256,768]{2,1,0:T(8,128)(2,1)}, bf16[2,256,768]{2,1,0:T(8,128)(2,1)S(1)}, u32[]{:S(2)}) copy-start(bf16[2,256,768]{2,1,0:T(8,128)(2,1)S(1)} %collective-permute-done.11.refs_7_) | copy-start | bytes 2359300
  108.8 45.6 %collective-permute-start.14 = (bf16[2,256,768]{2,1,0:T(8,128)(2,1)}, bf16[2,256,768]{2,1,0:T(8,128)(2,1)S(1)}, u32[]{:S(2)}, u32[]{:S(2)}) collective-permute-start(bf16[2,256,768]{2,1,0:T(8,128)(2,1)} %get-tuple-element.136), channel_id=1, source_target_pairs={{0,24},{8,16},{16,8},{24,0},{1,25},{9,17},{17,9},{25,1},{2,26},{10... | collective-permute-start | bytes 2359304 | tf_op jit(solution)/shard_map/ppermute | solution.py:225
  125.6 33.5 %collective-permute-start.13 = (bf16[2,256,768]{2,1,0:T(8,128)(2,1)}, bf16[2,256,768]{2,1,0:T(8,128)(2,1)S(1)}, u32[]{:S(2)}, u32[]{:S(2)}) collective-permute-start(bf16[2,256,768]{2,1,0:T(8,128)(2,1)} %get-tuple-element.134), channel_id=1, source_target_pairs={{0,16},{8,24},{16,0},{24,8},{1,17},{9,25},{17,1},{25,9},{2,18},{10... | collective-permute-start | bytes 2359304 | tf_op jit(solution)/shard_map/ppermute | solution.py:225
  127.1 32.4 %collective-permute-start.12 = (bf16[2,256,768]{2,1,0:T(8,128)(2,1)}, bf16[2,256,768]{2,1,0:T(8,128)(2,1)S(1)}, u32[]{:S(2)}, u32[]{:S(2)}) collective-permute-start(bf16[2,256,768]{2,1,0:T(8,128)(2,1)} %get-tuple-element.132), channel_id=1, source_target_pairs={{0,8},{8,0},{16,24},{24,16},{1,9},{9,1},{17,25},{25,17},{2,10},{10... | collective-permute-start | bytes 2359304 | tf_op jit(solution)/shard_map/ppermute | solution.py:225
  144.9 11.0 %copy-start.41 = (pred[1024,512]{1,0:T(32,128)(4,1)S(1)}, pred[1024,512]{1,0:T(32,128)(4,1)}, u32[]{:S(2)}) copy-start(pred[1024,512]{1,0:T(32,128)(4,1)} %copy-done.40) | copy-start | bytes 1572868
  152.4 8.1 %copy-start.30 = (bf16[2,256,768]{2,1,0:T(8,128)(2,1)}, bf16[2,256,768]{2,1,0:T(8,128)(2,1)S(1)}, u32[]{:S(2)}) copy-start(bf16[2,256,768]{2,1,0:T(8,128)(2,1)S(1)} %get-tuple-element.153.refs_0_) | copy-start | bytes 2359300
  152.4 26.6 %collective-permute-start.15 = (bf16[2,256,768]{2,1,0:T(8,128)(2,1)}, bf16[2,256,768]{2,1,0:T(8,128)(2,1)}, u32[]{:S(2)}, u32[]{:S(2)}) collective-permute-start(bf16[2,256,768]{2,1,0:T(8,128)(2,1)} %get-tuple-element.124), channel_id=1, source_target_pairs={{0,8},{8,0},{16,24},{24,16},{1,9},{9,1},{17,25},{25,17},{2,10},{10... | collective-permute-start | bytes 2359304 | tf_op jit(solution)/shard_map/ppermute | solution.py:225
  153.9 25.1 %collective-permute-start.16 = (bf16[2,256,768]{2,1,0:T(8,128)(2,1)}, bf16[2,256,768]{2,1,0:T(8,128)(2,1)}, u32[]{:S(2)}, u32[]{:S(2)}) collective-permute-start(bf16[2,256,768]{2,1,0:T(8,128)(2,1)} %get-tuple-element.125), channel_id=1, source_target_pairs={{0,16},{8,24},{16,0},{24,8},{1,17},{9,25},{17,1},{25,9},{2,18},{10... | collective-permute-start | bytes 2359304 | tf_op jit(solution)/shard_map/ppermute | solution.py:225
  154.4 38.4 %collective-permute-start.17 = (bf16[2,256,768]{2,1,0:T(8,128)(2,1)}, bf16[2,256,768]{2,1,0:T(8,128)(2,1)}, u32[]{:S(2)}, u32[]{:S(2)}) collective-permute-start(bf16[2,256,768]{2,1,0:T(8,128)(2,1)} %get-tuple-element.126), channel_id=1, source_target_pairs={{0,24},{8,16},{16,8},{24,0},{1,25},{9,17},{17,9},{25,1},{2,26},{10... | collective-permute-start | bytes 2359304 | tf_op jit(solution)/shard_map/ppermute | solution.py:225
  173.9 19.0 %copy-start.1 = (bf16[2,512,768]{2,1,0:T(8,128)(2,1)}, bf16[2,512,768]{2,1,0:T(8,128)(2,1)S(1)}, u32[]{:S(2)}) copy-start(bf16[2,512,768]{2,1,0:T(8,128)(2,1)S(1)} %get-tuple-element.149.y_ref.gd_ref) | copy-start | bytes 4718596
  173.9 54.3 %all-to-all-start.2 = ((bf16[8,128,1024]{2,1,0:T(8,128)(2,1)}), bf16[8,128,1024]{2,1,0:T(8,128)(2,1)}, u32[]{:S(2)}, u32[]{:S(2)}) async-start(bf16[8,128,1024]{2,1,0:T(8,128)(2,1)} %bitcast.52), calls=%async_computation.2 | async-start | bytes 4194304 | tf_op jit(solution)/shard_map/all_to_all | solution.py:295
  179.0 23.6 %copy-start.29 = (bf16[2,512,768]{2,1,0:T(8,128)(2,1)S(1)}, bf16[2,512,768]{2,1,0:T(8,128)(2,1)}, u32[]{:S(2)}) copy-start(bf16[2,512,768]{2,1,0:T(8,128)(2,1)} %copy-done.28) | copy-start | bytes 4718596
  201.3 12.7 %copy-start.6 = (bf16[2,256,768]{2,1,0:T(8,128)(2,1)S(1)}, bf16[2,256,768]{2,1,0:T(8,128)(2,1)}, u32[]{:S(2)}) copy-start(bf16[2,256,768]{2,1,0:T(8,128)(2,1)} %copy-done.4) | copy-start | bytes 2359300
  201.3 12.7 %copy-start.9 = (bf16[2,256,768]{2,1,0:T(8,128)(2,1)S(1)}, bf16[2,256,768]{2,1,0:T(8,128)(2,1)}, u32[]{:S(2)}) copy-start(bf16[2,256,768]{2,1,0:T(8,128)(2,1)} %copy-done.7) | copy-start | bytes 2359300
  201.3 12.7 %copy-start.11 = (bf16[2,256,768]{2,1,0:T(8,128)(2,1)S(1)}, bf16[2,256,768]{2,1,0:T(8,128)(2,1)}, u32[]{:S(2)}) copy-start(bf16[2,256,768]{2,1,0:T(8,128)(2,1)} %copy-done.10) | copy-start | bytes 2359300
  201.3 12.7 %copy-start.13 = (bf16[2,256,768]{2,1,0:T(8,128)(2,1)S(1)}, bf16[2,256,768]{2,1,0:T(8,128)(2,1)}, u32[]{:S(2)}) copy-start(bf16[2,256,768]{2,1,0:T(8,128)(2,1)} %copy-done.12) | copy-start | bytes 2359300
  201.3 12.7 %copy-start.15 = (bf16[2,256,768]{2,1,0:T(8,128)(2,1)S(1)}, bf16[2,256,768]{2,1,0:T(8,128)(2,1)}, u32[]{:S(2)}) copy-start(bf16[2,256,768]{2,1,0:T(8,128)(2,1)} %copy-done.14) | copy-start | bytes 2359300
  201.3 36.2 %collective-permute-start.18 = (bf16[2,256,768]{2,1,0:T(8,128)(2,1)}, bf16[2,256,768]{2,1,0:T(8,128)(2,1)}, u32[]{:S(2)}, u32[]{:S(2)}) collective-permute-start(bf16[2,256,768]{2,1,0:T(8,128)(2,1)} %get-tuple-element.161), channel_id=1, source_target_pairs={{0,8},{8,0},{16,24},{24,16},{1,9},{9,1},{17,25},{25,17},{2,10},{10... | collective-permute-start | bytes 2359304 | tf_op jit(solution)/shard_map/ppermute | solution.py:225
  211.4 36.2 %collective-permute-start.19 = (bf16[2,256,768]{2,1,0:T(8,128)(2,1)}, bf16[2,256,768]{2,1,0:T(8,128)(2,1)}, u32[]{:S(2)}, u32[]{:S(2)}) collective-permute-start(bf16[2,256,768]{2,1,0:T(8,128)(2,1)} %get-tuple-element.163), channel_id=1, source_target_pairs={{0,16},{8,24},{16,0},{24,8},{1,17},{9,25},{17,1},{25,9},{2,18},{10... | collective-permute-start | bytes 2359304 | tf_op jit(solution)/shard_map/ppermute | solution.py:225
  212.6 35.9 %collective-permute-start.20 = (bf16[2,256,768]{2,1,0:T(8,128)(2,1)}, bf16[2,256,768]{2,1,0:T(8,128)(2,1)}, u32[]{:S(2)}, u32[]{:S(2)}) collective-permute-start(bf16[2,256,768]{2,1,0:T(8,128)(2,1)} %get-tuple-element.165), channel_id=1, source_target_pairs={{0,24},{8,16},{16,8},{24,0},{1,25},{9,17},{17,9},{25,1},{2,26},{10... | collective-permute-start | bytes 2359304 | tf_op jit(solution)/shard_map/ppermute | solution.py:225
  228.2 4.7 %copy-start.31 = (bf16[2,256,768]{2,1,0:T(8,128)(2,1)S(1)}, bf16[2,256,768]{2,1,0:T(8,128)(2,1)}, u32[]{:S(2)}) copy-start(bf16[2,256,768]{2,1,0:T(8,128)(2,1)} %copy-done.30) | copy-start | bytes 2359300
  228.2 69.5 %all-to-all-start.3 = ((bf16[8,128,1024]{2,1,0:T(8,128)(2,1)}), bf16[8,128,1024]{2,1,0:T(8,128)(2,1)}, u32[]{:S(2)}, u32[]{:S(2)}) async-start(bf16[8,128,1024]{2,1,0:T(8,128)(2,1)} %bitcast.51), calls=%async_computation.3 | async-start | bytes 4194304 | tf_op jit(solution)/shard_map/all_to_all | solution.py:295
  232.9 14.7 %copy-start.35 = (bf16[2,256,768]{2,1,0:T(8,128)(2,1)S(1)}, bf16[2,256,768]{2,1,0:T(8,128)(2,1)}, u32[]{:S(2)}) copy-start(bf16[2,256,768]{2,1,0:T(8,128)(2,1)} %copy-done.34) | copy-start | bytes 2359300
  232.9 15.5 %copy-start.33 = (bf16[2,256,768]{2,1,0:T(8,128)(2,1)S(1)}, bf16[2,256,768]{2,1,0:T(8,128)(2,1)}, u32[]{:S(2)}) copy-start(bf16[2,256,768]{2,1,0:T(8,128)(2,1)} %copy-done.32) | copy-start | bytes 2359300
  233.0 17.1 %copy-start.17 = (bf16[2,256,768]{2,1,0:T(8,128)(2,1)S(1)}, bf16[2,256,768]{2,1,0:T(8,128)(2,1)}, u32[]{:S(2)}) copy-start(bf16[2,256,768]{2,1,0:T(8,128)(2,1)} %copy-done.16) | copy-start | bytes 2359300
  237.5 16.9 %copy-start.43 = (bf16[1024,512]{1,0:T(8,128)(2,1)S(1)}, bf16[1024,512]{1,0:T(8,128)(2,1)}, u32[]{:S(2)}) copy-start(bf16[1024,512]{1,0:T(8,128)(2,1)} %reduce-precision_convert_fusion) | copy-start | bytes 3145732
  237.5 23.0 %collective-permute-start.21 = (bf16[2,256,768]{2,1,0:T(8,128)(2,1)S(1)}, bf16[2,256,768]{2,1,0:T(8,128)(2,1)S(1)}, u32[]{:S(2)}, u32[]{:S(2)}) collective-permute-start(bf16[2,256,768]{2,1,0:T(8,128)(2,1)S(1)} %copy-done.37), channel_id=1, source_target_pairs={{0,8},{8,0},{16,24},{24,16},{1,9},{9,1},{17,25},{25,17},{2,10},{10... | collective-permute-start | bytes 2359304 | tf_op jit(solution)/shard_map/ppermute | solution.py:225
  247.6 35.0 %collective-permute-start.23 = (bf16[2,256,768]{2,1,0:T(8,128)(2,1)S(1)}, bf16[2,256,768]{2,1,0:T(8,128)(2,1)S(1)}, u32[]{:S(2)}, u32[]{:S(2)}) collective-permute-start(bf16[2,256,768]{2,1,0:T(8,128)(2,1)S(1)} %copy-done.35), channel_id=1, source_target_pairs={{0,16},{8,24},{16,0},{24,8},{1,17},{9,25},{17,1},{25,9},{2,18},{10... | collective-permute-start | bytes 2359304 | tf_op jit(solution)/shard_map/ppermute | solution.py:225
  248.5 34.7 %collective-permute-start.25 = (bf16[2,256,768]{2,1,0:T(8,128)(2,1)S(1)}, bf16[2,256,768]{2,1,0:T(8,128)(2,1)S(1)}, u32[]{:S(2)}, u32[]{:S(2)}) collective-permute-start(bf16[2,256,768]{2,1,0:T(8,128)(2,1)S(1)} %copy-done.33), channel_id=1, source_target_pairs={{0,24},{8,16},{16,8},{24,0},{1,25},{9,17},{17,9},{25,1},{2,26},{10... | collective-permute-start | bytes 2359304 | tf_op jit(solution)/shard_map/ppermute | solution.py:225
  257.5 27.4 %copy-start.21 = (bf16[128,1024]{1,0:T(8,128)(2,1)S(1)}, bf16[128,1024]{1,0:T(8,128)(2,1)}, u32[]{:S(2)}) copy-start(bf16[128,1024]{1,0:T(8,128)(2,1)} %copy-done.19) | copy-start | bytes 786436
  257.5 27.4 %copy-start.24 = (bf16[128,1024]{1,0:T(8,128)(2,1)S(1)}, bf16[128,1024]{1,0:T(8,128)(2,1)}, u32[]{:S(2)}) copy-start(bf16[128,1024]{1,0:T(8,128)(2,1)} %copy-done.22) | copy-start | bytes 786436
  257.5 27.4 %copy-start.27 = (bf16[128,1024]{1,0:T(8,128)(2,1)S(1)}, bf16[128,1024]{1,0:T(8,128)(2,1)}, u32[]{:S(2)}) copy-start(bf16[128,1024]{1,0:T(8,128)(2,1)} %copy-done.25) | copy-start | bytes 786436
  257.5 27.4 %copy-start.42 = (pred[1024,512]{1,0:T(32,128)(4,1)S(1)}, pred[1024,512]{1,0:T(32,128)(4,1)}, u32[]{:S(2)}) copy-start(pred[1024,512]{1,0:T(32,128)(4,1)} %copy-done.40) | copy-start | bytes 1572868
  260.6 36.2 %collective-permute-start.22 = (bf16[128,1024]{1,0:T(8,128)(2,1)S(1)}, bf16[128,1024]{1,0:T(8,128)(2,1)S(1)}, u32[]{:S(2)}, u32[]{:S(2)}) collective-permute-start(bf16[128,1024]{1,0:T(8,128)(2,1)S(1)} %get-tuple-element.169), channel_id=1, source_target_pairs={{0,8},{8,0},{16,24},{24,16},{1,9},{9,1},{17,25},{25,17},{2,10},{10... | collective-permute-start | bytes 786440 | tf_op jit(solution)/shard_map/ppermute | solution.py:225
  282.6 14.2 %collective-permute-start.24 = (bf16[128,1024]{1,0:T(8,128)(2,1)S(1)}, bf16[128,1024]{1,0:T(8,128)(2,1)S(1)}, u32[]{:S(2)}, u32[]{:S(2)}) collective-permute-start(bf16[128,1024]{1,0:T(8,128)(2,1)S(1)} %get-tuple-element.171), channel_id=1, source_target_pairs={{0,16},{8,24},{16,0},{24,8},{1,17},{9,25},{17,1},{25,9},{2,18},{10... | collective-permute-start | bytes 786440 | tf_op jit(solution)/shard_map/ppermute | solution.py:225
  283.2 4.7 %copy-start.50 = (s32[16]{0:T(128)S(1)}, s32[16]{0:T(128)}, u32[]{:S(2)}) copy-start(s32[16]{0:T(128)} %copy-done.49) | copy-start | bytes 196
  283.2 13.6 %collective-permute-start.26 = (bf16[128,1024]{1,0:T(8,128)(2,1)S(1)}, bf16[128,1024]{1,0:T(8,128)(2,1)S(1)}, u32[]{:S(2)}, u32[]{:S(2)}) collective-permute-start(bf16[128,1024]{1,0:T(8,128)(2,1)S(1)} %get-tuple-element.173), channel_id=1, source_target_pairs={{0,24},{8,16},{16,8},{24,0},{1,25},{9,17},{17,9},{25,1},{2,26},{10... | collective-permute-start | bytes 786440 | tf_op jit(solution)/shard_map/ppermute | solution.py:225
  288.0 3.7 %collective-permute-start.27 = (f32[128,6]{0,1:T(8,128)S(1)}, f32[128,6]{0,1:T(8,128)S(1)}, u32[]{:S(2)}, u32[]{:S(2)}) collective-permute-start(f32[128,6]{0,1:T(8,128)S(1)} %get-tuple-element.174), channel_id=1, source_target_pairs={{0,8},{8,0},{16,24},{24,16},{1,9},{9,1},{17,25},{25,17},{2,10},{10... | collective-permute-start | bytes 9224 | tf_op jit(solution)/shard_map/ppermute | solution.py:225
  289.3 5.1 %collective-permute-start.28 = (f32[128,6]{0,1:T(8,128)S(1)}, f32[128,6]{0,1:T(8,128)S(1)}, u32[]{:S(2)}, u32[]{:S(2)}) collective-permute-start(f32[128,6]{0,1:T(8,128)S(1)} %get-tuple-element.175), channel_id=1, source_target_pairs={{0,16},{8,24},{16,0},{24,8},{1,17},{9,25},{17,1},{25,9},{2,18},{10... | collective-permute-start | bytes 9224 | tf_op jit(solution)/shard_map/ppermute | solution.py:225
  291.6 4.5 %collective-permute-start.29 = (f32[128,6]{0,1:T(8,128)S(1)}, f32[128,6]{0,1:T(8,128)S(1)}, u32[]{:S(2)}, u32[]{:S(2)}) collective-permute-start(f32[128,6]{0,1:T(8,128)S(1)} %get-tuple-element.176), channel_id=1, source_target_pairs={{0,24},{8,16},{16,8},{24,0},{1,25},{9,17},{17,9},{25,1},{2,26},{10... | collective-permute-start | bytes 9224 | tf_op jit(solution)/shard_map/ppermute | solution.py:225
  300.8 8.3 %collective-permute-start.30 = (bf16[128,1024]{1,0:T(8,128)(2,1)S(1)}, bf16[128,1024]{1,0:T(8,128)(2,1)S(1)}, u32[]{:S(2)}, u32[]{:S(2)}) collective-permute-start(bf16[128,1024]{1,0:T(8,128)(2,1)S(1)} %get-tuple-element.193), channel_id=1, source_target_pairs={{0,8},{8,0},{16,24},{24,16},{1,9},{9,1},{17,25},{25,17},{2,10},{10... | collective-permute-start | bytes 786440 | tf_op jit(solution)/shard_map/ppermute | solution.py:225
  302.1 9.9 %collective-permute-start.31 = (bf16[128,1024]{1,0:T(8,128)(2,1)S(1)}, bf16[128,1024]{1,0:T(8,128)(2,1)S(1)}, u32[]{:S(2)}, u32[]{:S(2)}) collective-permute-start(bf16[128,1024]{1,0:T(8,128)(2,1)S(1)} %get-tuple-element.195), channel_id=1, source_target_pairs={{0,16},{8,24},{16,0},{24,8},{1,17},{9,25},{17,1},{25,9},{2,18},{10... | collective-permute-start | bytes 786440 | tf_op jit(solution)/shard_map/ppermute | solution.py:225
  302.6 9.3 %collective-permute-start.32 = (bf16[128,1024]{1,0:T(8,128)(2,1)S(1)}, bf16[128,1024]{1,0:T(8,128)(2,1)S(1)}, u32[]{:S(2)}, u32[]{:S(2)}) collective-permute-start(bf16[128,1024]{1,0:T(8,128)(2,1)S(1)} %get-tuple-element.194), channel_id=1, source_target_pairs={{0,24},{8,16},{16,8},{24,0},{1,25},{9,17},{17,9},{25,1},{2,26},{10... | collective-permute-start | bytes 786440 | tf_op jit(solution)/shard_map/ppermute | solution.py:225
  (24 other events, 37.3 us)

commit v3 on v2

--- a/solution.py
+++ b/solution.py
@@ -106,6 +106,7 @@
 
 
 LIGHT, HEAVY = 1 << 10, 1 << 37
+COSTS = (1 << 34, 1 << 34, LIGHT, 1 << 35, HEAVY, LIGHT, 1 << 35, HEAVY)
 
 
 def call(kernel, name, grid, in_specs, out_specs, out_shape, scratch=(), cost=LIGHT):
@@ -170,10 +171,20 @@
             outs[s][0] = dot(x, y_ref[0], 0, 0).astype(BF)
 
 
-def middle_kernel(me_ref, sg_ref, h_ref, a_ref, b_ref, *refs):
-    nb = len(refs) - 4
+def output_kernel(me_ref, h_ref, *refs):
+    downs, out_ref = refs[:-1], refs[-1]
+    j = pl.program_id(1)
+    for s in range(len(downs)):
+
+        @pl.when(j == s)
+        def _(s=s):
+            out_ref[...] = dot(h_ref[0], downs[s][0], 1, 1).astype(BF).reshape(out_ref.shape)
+
+
+def delta_kernel(me_ref, sg_ref, a_ref, b_ref, *refs):
+    nb = len(refs) - 3
     downs = refs[:nb]
-    out_ref, gd_ref, ud_ref, acc = refs[nb:]
+    gd_ref, ud_ref, acc = refs[nb:]
     j = pl.program_id(1)
     sg = sg_ref[...].reshape(acc.shape[0], sg_ref.shape[-1])
     for s in range(nb):
@@ -182,7 +193,6 @@
         def _(s=s):
             part = dot(sg, downs[s][0], 1, 0)
             acc[...] = part if s == 0 else acc[...] + part
-            out_ref[...] = dot(h_ref[0], downs[s][0], 1, 1).astype(BF).reshape(out_ref.shape)
 
     @pl.when(j == nb - 1)
     def _():
@@ -243,14 +253,12 @@
     low = route_weight - high - mid
     extra = jnp.concatenate([expert_ids.astype(F32), high, mid, low], axis=1).astype(BF)
     extra = jnp.pad(extra, ((0, 0), (0, 128 - extra.shape[1])))
-    tok_p = spread(jnp.concatenate([tokens, extra], axis=1))
+    tok_p = spread(jnp.concatenate([tokens, out_grad, extra], axis=1))
     gate_ready = prepare(gate_weight)
     tok_p, gate_ready = lax.optimization_barrier((tok_p, gate_ready))
-    og_p = spread(out_grad)
-    gate_p = weight_pieces(gate_ready, og_p)
+    gate_p = weight_pieces(gate_ready, tok_p)
     up_ready, down_ready = prepare(up_weight), prepare(down_weight)
-    og_p, up_ready, down_ready = lax.optimization_barrier((og_p, up_ready, down_ready))
-    extra = jnp.concatenate([p[:, width:] for p in tok_p], axis=0).astype(F32)
+    extra = jnp.concatenate([p[:, 2 * width :] for p in tok_p], axis=0).astype(F32)
     top = expert_ids.shape[1]
     ids_all = extra[:, :top].astype(jnp.int32)
     rw_all = extra[:, top : 2 * top] + extra[:, 2 * top : 3 * top] + extra[:, 3 * top : 4 * top]
@@ -271,7 +279,7 @@
     sel = hit.astype(BF)
     sel_w = jnp.where(hit, weight_s, 0.0)
 
-    def pick(pieces, scale):
+    def pick(pieces, scale, half, cost):
         tile = slots // 4
         return call(
             pick_kernel,
@@ -281,9 +289,11 @@
                 pl.BlockSpec((tile, rows), lambda t, m: (t, 0)),
                 pl.BlockSpec((tile, 1), lambda t, m: (t, 0)),
             ]
-            + [pl.BlockSpec((tok, width), lambda t, m: (0, 0))] * nb,
+            + [pl.BlockSpec((tok, width), lambda t, m: (0, half))] * nb,
             pl.BlockSpec((tile, width), lambda t, m: (t, 0)),
             jax.ShapeDtypeStruct((slots, width), BF),
+            (),
+            cost,
         )(me_arr, sel, scale, *pieces)
 
     previous = []
@@ -295,9 +305,10 @@
         previous.append(lax.all_to_all(x, "ep", split_axis=0, concat_axis=0, tiled=True))
         return previous[-1].reshape(ne, own, per, width)
 
-    routed = exchange(pick(tok_p, jnp.ones((slots, 1), F32)))
-    slot_grad = pick(og_p, jnp.sum(sel_w, axis=1, keepdims=True))
-    up_ready = after(up_ready, slot_grad)
+    routed = exchange(pick(tok_p, jnp.ones((slots, 1), F32), 0, LIGHT))
+    scale = jnp.sum(sel_w, axis=1, keepdims=True)
+    late_p, scale, up_ready, down_ready = lax.optimization_barrier((tok_p, scale, up_ready, down_ready))
+    slot_grad = pick(after(late_p, gate_p), scale, 1, COSTS[7])
     up_p = weight_pieces(up_ready, gate_p)
     down_p = weight_pieces(down_ready, up_p)
     graded = exchange(after(slot_grad, gate_p))
@@ -321,6 +332,7 @@
         [wide_spec] * 3,
         [wide(F32), wide(F32), wide(BF)],
         [acc, acc],
+        COSTS[6],
     )(me_arr, routed, *gate_p, *up_p)
 
     def outer(x, y, cost):
@@ -341,25 +353,27 @@
             got.append(hop(parts[j] if deps is None else after(parts[j], deps[j]), j))
         return got
 
+    outs = call(
+        output_kernel, "outputs", grid, [wide_spec] + weight_specs, rows_spec, full
+    )(me_arr, hidden, *down_p)
+    graded, outs = lax.optimization_barrier((graded, outs))
     down_part = outer(graded, hidden, LIGHT)
     down_got = send_back(down_part, None)
-    hidden = after(hidden, down_part)
-    outs, gate_delta, up_delta = call(
-        middle_kernel,
-        "middle",
+    graded = after(graded, down_part)
+    gate_delta, up_delta = call(
+        delta_kernel,
+        "deltas",
         grid,
-        [rows_spec] + [wide_spec] * 3 + weight_specs,
-        [rows_spec, wide_spec, wide_spec],
-        [full, wide(BF), wide(BF)],
+        [rows_spec] + [wide_spec] * 2 + weight_specs,
+        [wide_spec] * 2,
+        [wide(BF), wide(BF)],
         [acc],
-    )(me_arr, graded, hidden, a, b, *down_p)
-    outs = exchange(outs).reshape(slots, width)
-    gate_part = outer(routed, after(gate_delta, down_got), LIGHT)
-    gate_part, up_delta = lax.optimization_barrier((gate_part, up_delta))
-    up_part = outer(routed, up_delta, HEAVY)
+        COSTS[0],
+    )(me_arr, graded, a, b, *down_p)
+    outs = exchange(after(outs, down_part)).reshape(slots, width)
+    gate_part = outer(routed, gate_delta, COSTS[1])
     gate_got = send_back(gate_part, down_got)
-    gate_delta = after(gate_delta, up_part)
-    up_got = send_back(up_part, gate_got)
+    gate_delta = after(gate_delta, gate_part)
     backs = call(
         input_kernel,
         "inputs",
@@ -368,21 +382,23 @@
         rows_spec,
         full,
         (),
-        HEAVY,
+        COSTS[3],
     )(me_arr, gate_delta, up_delta, *gate_p, *up_p)
+    up_part = outer(routed, after(up_delta, backs), COSTS[2])
+    up_got = send_back(up_part, gate_got)
     down_got = after(down_got, backs)
     backs = exchange(backs).reshape(slots, width)
 
-    grad_down = finish(down_got, me, HEAVY)
+    grad_down = finish(down_got, me, COSTS[4])
     outs, grad_down = lax.optimization_barrier((outs, grad_down))
     high = lax.reduce_precision(sel_w, 8, 7)
     low = (sel_w - high).astype(BF)
     high = high.astype(BF)
     mixed = dot(high, outs, 0, 0) + dot(low, outs, 0, 0)
-    score = dot(outs, jnp.concatenate(og_p, 0), 1, 1)
+    score = dot(outs, jnp.concatenate([p[:, width : 2 * width] for p in tok_p], 0), 1, 1)
     score = jnp.where(hit, score, 0.0).reshape(ne * own, per, rows).sum(1)
     route_grad = jnp.sum(jnp.where(eq, score.T[:, None, :], 0.0), axis=2)
-    grad_gate = finish(gate_got, me)
+    grad_gate = finish(gate_got, me, COSTS[5])
     def gather_back(x, deps=None):
         x = x.reshape((nb, tok) + x.shape[1:])
         total = x[0].astype(F32)
@@ -391,12 +407,17 @@
             total += hop(part, j).astype(F32)
         return total
 
-    mixed, grad_gate = lax.optimization_barrier((mixed, grad_gate))
-    layer_output = gather_back(mixed.astype(BF), up_got).astype(BF)
-    grad_route = gather_back(route_grad, up_got)
-    backs, grad_down, grad_gate, layer_output, grad_route = lax.optimization_barrier(
-        (backs, grad_down, grad_gate, layer_output, grad_route)
-    )
+    route_high = lax.reduce_precision(route_grad, 8, 7)
+    route_mid = lax.reduce_precision(route_grad - route_high, 8, 7)
+    route_low = route_grad - route_high - route_mid
+    route_all = jnp.concatenate([route_high, route_mid, route_low], axis=1)
+    route_all = jnp.pad(route_all, ((0, 0), (0, 128 - route_all.shape[1])))
+    payload = jnp.concatenate([mixed, route_all], axis=1).astype(BF)
+    payload, grad_gate, grad_down, backs = lax.optimization_barrier((payload, grad_gate, grad_down, backs))
+    layer_sum = gather_back(payload, up_got)
+    layer_output = layer_sum[:, :width].astype(BF)
+    route_sum = layer_sum[:, width:]
+    grad_route = route_sum[:, :top] + route_sum[:, top : 2 * top] + route_sum[:, 2 * top : 3 * top]
     grad_tokens = gather_back(dot(sel, backs, 0, 0).astype(BF))
     return (
         layer_output,

time: 314 us -> 305 us (0.971)
  waiting for transfers between devices: 128 us -> 115 us
  starting transfers between devices: 58.7 us -> 52.5 us
  local copies, waits for them, and re-layouts: 31.9 us -> 37.6 us
  Pallas kernels: 71 us -> 75.5 us
    ppermute x33 -> x27, waiting for transfers between devices: 123 us -> 80.2 us  [hop(): return lax.ppermute(x, 'blk', [(i, i ^ j) for i in range(nb)])]
    all_to_all x4, waiting for transfers between devices: 5 us -> 34.6 us  [exchange(): lax.all_to_all(x, 'ep', split_axis=0, concat_axis=0, tiled=True)]
    ppermute x33 -> x27, starting transfers between devices: 39.1 us -> 33.9 us  [hop(): return lax.ppermute(x, 'blk', [(i, i ^ j) for i in range(nb)])]
    pallas_call x1 -> x2, Pallas kernels: 11.1 us -> 15.1 us  [the longest x1 8.49 us: expert_body(): call(delta_kernel, 'deltas', grid, [rows_spec] + [wide_spec] * 2 + weight...]
    unnamed x105 -> x84, local copies, waits for them, and re-layouts: 25.3 us -> 27.3 us
  transfers between devices with their start and end apart: 37 -> 31, of which waited for: 19 -> 18; matrix products, arithmetic and copies ran while one was open for 8% -> 12% of each run, Pallas kernels for 22% -> 22%
where the time goes in v3:
time: 305 us; the launch traced here: 303 us
  waiting for transfers between devices  115 us (38%)
  Pallas kernels  75.5 us (25%)
  starting transfers between devices  52.5 us (17%)
  local copies, waits for them, and re-layouts  37.6 us (12%)
  matrix products  12.5 us (4%)
  other arithmetic  9.51 us (3%)
    ppermute x27, waiting for transfers between devices, hop(): return lax.ppermute(x, 'blk', [(i, i ^ j) for i in range(nb)])  80.2 us
    all_to_all x4, waiting for transfers between devices, exchange(): lax.all_to_all(x, 'ep', split_axis=0, concat_axis=0, tiled=True)  34.6 us
    ppermute x27, starting transfers between devices, hop(): return lax.ppermute(x, 'blk', [(i, i ^ j) for i in range(nb)])  33.9 us
    unnamed x84, local copies, waits for them, and re-layouts  27.3 us
    pallas_call x3, Pallas kernels, outer(): call(outer_kernel, 'outer', grid, [rows_spec, wide_spec], [piece_spec] *...  22.7 us
    all_to_all x4, starting transfers between devices, exchange(): lax.all_to_all(x, 'ep', split_axis=0, concat_axis=0, tiled=True)  18.6 us
    dot_general x5, matrix products, dot(): lax.dot_general(a, b, (((ca,), (cb,)), ((), ())), preferred_element_type=...  12.5 us
    pallas_call x1, Pallas kernels, expert_body(): call(forward_kernel, 'forward', grid, [rows_spec] + weight_specs * 2, [wi...  12.5 us
  transfers between devices with their start and end apart: 31, of which 18 were waited for; matrix products, arithmetic and copies ran while one was open for 12% of the time, Pallas kernels for 22%

profile of v3, /device:TPU:0, one launch (start us, length us, event | category | flops | bytes accessed | tf_op | source)
XLA Modules:
  0.0 303.4 jit_solution(16183185923978449334)
XLA Ops:
  3.2 4.0 %collective-permute-start.2 = (bf16[128,2176]{1,0:T(8,128)(2,1)S(1)}, bf16[128,2176]{1,0:T(8,128)(2,1)S(1)}, u32[]{:S(2)}, u32[]{:S(2)}) collective-permute-start(bf16[128,2176]{1,0:T(8,128)(2,1)S(1)} %fusion.18.refs_0_), channel_id=1, source_target_pairs={{0,24},{8,16},{16,8},{24,0},{1,25},{9,17},{17,9},{25,1},{2,26},{10... | collective-permute-start | bytes 1671176 | tf_op jit(solution)/shard_map/ppermute | solution.py:235
  8.0 4.3 %copy.59 = bf16[256,8,768]{2,0,1:T(8,128)(2,1)} copy(bf16[256,8,768]{2,1,0:T(8,128)(2,1)} %param.10) | data formatting | bytes 6291456 | tf_op args[3]
  12.3 2.3 copy.58
  15.0 2.3 copy.57
  17.3 3.2 %constant_dynamic-slice_fusion.6 = (bf16[2,256,768]{2,1,0:T(8,128)(2,1)}, bf16[2,256,768]{2,1,0:T(8,128)(2,1)}, bf16[2,256,768]{2,1,0:T(8,128)(2,1)}) fusion(bf16[8,256,768]{2,1,0:T(8,128)(2,1)} %bitcast.50, s32[]{:T(128)S(6)} %select_n.100, s32[]{:T(128)S(6)} %select_n.99, s32[]{:T(128)S(6)} %select_n.98), kind=kLoop, calls=%fused_computation.99 | loop fusion | bytes 4718604 | tf_op jit(solution)/shard_map/dynamic_slice | solution.py:245
  20.6 3.8 %constant_dynamic-slice_fusion = (bf16[2,256,768]{2,1,0:T(8,128)(2,1)}, bf16[2,256,768]{2,1,0:T(8,128)(2,1)}, bf16[2,256,768]{2,1,0:T(8,128)(2,1)}, bf16[2,256,7...) fusion(bf16[8,256,768]{2,1,0:T(8,128)(2,1)S(1)} %bitcast.46, s32[]{:T(128)S(6)} %select_n.100, ...), kind=kLoop, calls=%fused_computation.93 | loop fusion | bytes 9437196 | tf_op jit(solution)/shard_map/dynamic_slice | solution.py:245
  24.3 7.4 %collective-permute-done.1.refs_2_ = bf16[128,2176]{1,0:T(8,128)(2,1)S(1)} collective-permute-done((bf16[128,2176]{1,0:T(8,128)(2,1)S(1)}, bf16[128,2176]{1,0:T(8,128)(2,1)S(1)}, u32[]{:S(2)}, u32[]{:S(2)}) %collective-permute-start.1) | collective-permute-done | bytes 557088 | tf_op jit(solution)/shard_map/ppermute | solution.py:235
  32.1 1.6 collective-permute-start.5
  33.7 1.4 collective-permute-start.4
  36.7 1.7 fusion.1
  39.2 3.0 pick.3
  43.0 4.9 %all-to-all-start = ((bf16[8,128,1024]{2,1,0:T(8,128)(2,1)}), bf16[8,128,1024]{2,1,0:T(8,128)(2,1)}, u32[]{:S(2)}, u32[]{:S(2)}) async-start(bf16[8,128,1024]{2,1,0:T(8,128)(2,1)} %bitcast.8), calls=%async_computation | async-start | bytes 4194304 | tf_op jit(solution)/shard_map/all_to_all | solution.py:305
  48.9 4.9 %collective-permute-done.5.refs_3_ = bf16[2,256,768]{2,1,0:T(8,128)(2,1)} collective-permute-done((bf16[2,256,768]{2,1,0:T(8,128)(2,1)}, bf16[2,256,768]{2,1,0:T(8,128)(2,1)}, u32[]{:S(2)}, u32[]{:S(2)}) %collective-permute-start.5) | collective-permute-done | bytes 786464 | tf_op jit(solution)/shard_map/ppermute | solution.py:235
  53.9 15.6 %collective-permute-done.4.refs_2_ = bf16[2,256,768]{2,1,0:T(8,128)(2,1)} collective-permute-done((bf16[2,256,768]{2,1,0:T(8,128)(2,1)}, bf16[2,256,768]{2,1,0:T(8,128)(2,1)}, u32[]{:S(2)}, u32[]{:S(2)}) %collective-permute-start.4) | collective-permute-done | bytes 786464 | tf_op jit(solution)/shard_map/ppermute | solution.py:235
  69.7 1.4 collective-permute-start.8
  71.1 1.4 collective-permute-start.7
  74.2 1.9 pick.2
  76.1 1.3 copy-done.2
  77.5 19.6 %all-to-all-done = bf16[8,128,1024]{2,1,0:T(8,128)(2,1)} async-done(((bf16[8,128,1024]{2,1,0:T(8,128)(2,1)}), bf16[8,128,1024]{2,1,0:T(8,128)(2,1)}, u32[]{:S(2)}, u32[]{:S(2)}) %all-to-all-start) | async-done | bytes 2097184 | tf_op jit(solution)/shard_map/all_to_all | solution.py:305
  97.1 4.7 %all-to-all-start.1 = ((bf16[8,128,1024]{2,1,0:T(8,128)(2,1)}), bf16[8,128,1024]{2,1,0:T(8,128)(2,1)}, u32[]{:S(2)}, u32[]{:S(2)}) async-start(bf16[8,128,1024]{2,1,0:T(8,128)(2,1)} %bitcast.43), calls=%async_computation.1 | async-start | bytes 4194304 | tf_op jit(solution)/shard_map/all_to_all | solution.py:305
  102.5 1.3 reduce-precision_convert_fusion
  103.8 1.7 collective-permute-start.11
  105.5 1.5 collective-permute-done.7.refs_6_
  106.9 1.7 collective-permute-start.10
  108.7 12.5 %forward.1 = (f32[2,512,768]{2,1,0:T(8,128)}, f32[2,512,768]{2,1,0:T(8,128)}, bf16[2,512,768]{2,1,0:T(8,128)(2,1)}) custom-call(s32[1]{0:T(128)} %bitcast.5.me_ref, bf16[8,2,64,1024]{3,2,1,0:T(8,128)(2,1)} %bitcast.11.x_ref, bf16[8,256,768]{2,1,0:T(8,128)(2,1)} %bitcast.51, bf16[2,256,768]{2,1,0:T(8,128)(2,1)} %collective-permute-done.3.refs_1_, ...), custom_call_target="tpu_custom_call" | custom-call | flops 34359738368 | bytes 1024 | tf_op jit(solution)/shard_map/forward/pallas_call | solution.py:327
  121.2 4.0 %collective-permute-done.11.refs_3_ = bf16[2,256,768]{2,1,0:T(8,128)(2,1)S(1)} collective-permute-done((bf16[2,256,768]{2,1,0:T(8,128)(2,1)S(1)}, bf16[2,256,768]{2,1,0:T(8,128)(2,1)S(1)}, u32[]{:S(2)}, u32[]{:S(2)}) %collective-permute-start.11) | collective-permute-done | bytes 786464 | tf_op jit(solution)/shard_map/ppermute | solution.py:235
  125.1 16.1 %collective-permute-done.10.refs_2_ = bf16[2,256,768]{2,1,0:T(8,128)(2,1)S(1)} collective-permute-done((bf16[2,256,768]{2,1,0:T(8,128)(2,1)S(1)}, bf16[2,256,768]{2,1,0:T(8,128)(2,1)S(1)}, u32[]{:S(2)}, u32[]{:S(2)}) %collective-permute-start.10) | collective-permute-done | bytes 786464 | tf_op jit(solution)/shard_map/ppermute | solution.py:235
  141.2 1.4 copy-done
  142.6 6.6 %outputs.1 = bf16[8,2,64,1024]{3,2,1,0:T(8,128)(2,1)} custom-call(s32[1]{0:T(128)} %bitcast.5.me_ref, bf16[2,512,768]{2,1,0:T(8,128)(2,1)S(1)} %copy-done, bf16[8,256,768]{2,1,0:T(8,128)(2,1)} %bitcast.44, bf16[2,256,768]{2,1,0:T(8,128)(2,1)S(1)} %collective-permute-done.9.refs_1_, bf16[2,256,768]{2,1,0:T(8,128)(2,1)S(1)} %collective-permute-done.10.refs_2_, ...), custom_call_target="tpu_custom_call" | custom-call | flops 1024 | bytes 1024 | tf_op jit(solution)/shard_map/outputs/pallas_call | solution.py:356
  150.6 7.4 %outer.3 = (bf16[2,256,768]{2,1,0:T(8,128)(2,1)S(1)}, bf16[2,256,768]{2,1,0:T(8,128)(2,1)}, bf16[2,256,768]{2,1,0:T(8,128)(2,1)}, bf16[2,256,768]{2,1,0:T(8,128)(2,1)}) custom-call(s32[1]{0:T(128)} %bitcast.5.me_ref, bf16[8,2,64,1024]{3,2,1,0:T(8,128)(2,1)} %bitcast.10.x_ref.sg_ref, bf16[2,512,768]{2,1,0:T(8,128)(2,1)S(1)} %copy-done.1), custom_call_target="tpu_custom_call" | custom-call | flops 1024 | bytes 1024 | tf_op jit(solution)/shard_map/outer/pallas_call | solution.py:339
  158.9 1.5 collective-permute-start.12
  161.2 1.3 collective-permute-start.14
  162.4 4.5 %all-to-all-start.2 = ((bf16[8,128,1024]{2,1,0:T(8,128)(2,1)}), bf16[8,128,1024]{2,1,0:T(8,128)(2,1)}, u32[]{:S(2)}, u32[]{:S(2)}) async-start(bf16[8,128,1024]{2,1,0:T(8,128)(2,1)} %bitcast.12), calls=%async_computation.2 | async-start | bytes 4194304 | tf_op jit(solution)/shard_map/all_to_all | solution.py:305
  166.9 8.5 %deltas.1 = (bf16[2,512,768]{2,1,0:T(8,128)(2,1)S(1)}, bf16[2,512,768]{2,1,0:T(8,128)(2,1)S(1)}) custom-call(s32[1]{0:T(128)} %bitcast.5.me_ref, bf16[8,2,64,1024]{3,2,1,0:T(8,128)(2,1)} %bitcast.10.x_ref.sg_ref, f32[2,512,768]{2,1,0:T(8,128)} %get-tuple-element.132.a_ref, f32[2,512,768]{2,1,0:T(8,128)} %get-tuple-element.133.b_ref, ...), custom_call_target="tpu_custom_call" | custom-call | flops 17179869184 | bytes 1024 | tf_op jit(solution)/shard_map/deltas/pallas_call | solution.py:363
  175.4 1.2 copy-done.3
  176.6 7.7 %outer.4 = (bf16[2,256,768]{2,1,0:T(8,128)(2,1)S(1)}, bf16[2,256,768]{2,1,0:T(8,128)(2,1)}, bf16[2,256,768]{2,1,0:T(8,128)(2,1)}, bf16[2,256,768]{2,1,0:T(8,128)(2,1)}) custom-call(s32[1]{0:T(128)} %bitcast.5.me_ref, bf16[8,2,64,1024]{3,2,1,0:T(8,128)(2,1)} %bitcast.11.x_ref, bf16[2,512,768]{2,1,0:T(8,128)(2,1)S(1)} %get-tuple-element.139.y_ref.gd_ref), custom_call_target="tpu_custom_call" | custom-call | flops 17179869184 | bytes 1024 | tf_op jit(solution)/shard_map/outer/pallas_call | solution.py:339
  185.2 10.5 %inputs.1 = bf16[8,2,64,1024]{3,2,1,0:T(8,128)(2,1)} custom-call(s32[1]{0:T(128)} %bitcast.5.me_ref, bf16[2,512,768]{2,1,0:T(8,128)(2,1)} %copy-done.23, bf16[2,512,768]{2,1,0:T(8,128)(2,1)} %copy-done.3, bf16[8,256,768]{2,1,0:T(8,128)(2,1)} %bitcast.52, bf16[2,256,768]{2,1,0:T(8,128)(2,1)} %collective-permute-done.3.refs_1_, ...), custom_call_target="tpu_custom_call" | custom-call | flops 34359738368 | bytes 1024 | tf_op jit(solution)/shard_map/inputs/pallas_call | solution.py:377
  195.7 7.5 %outer.5 = (bf16[2,256,768]{2,1,0:T(8,128)(2,1)S(1)}, bf16[2,256,768]{2,1,0:T(8,128)(2,1)}, bf16[2,256,768]{2,1,0:T(8,128)(2,1)}, bf16[2,256,768]{2,1,0:T(8,128)(2,1)}) custom-call(s32[1]{0:T(128)} %bitcast.5.me_ref, bf16[8,2,64,1024]{3,2,1,0:T(8,128)(2,1)} %bitcast.11.x_ref, bf16[2,512,768]{2,1,0:T(8,128)(2,1)S(1)} %copy-done.4), custom_call_target="tpu_custom_call" | custom-call | flops 1024 | bytes 1024 | tf_op jit(solution)/shard_map/outer/pallas_call | solution.py:339
  204.2 1.7 collective-permute-start.17
  205.9 1.3 collective-permute-start.16
  207.7 8.4 %all-to-all-done.2 = bf16[8,128,1024]{2,1,0:T(8,128)(2,1)} async-done(((bf16[8,128,1024]{2,1,0:T(8,128)(2,1)}), bf16[8,128,1024]{2,1,0:T(8,128)(2,1)}, u32[]{:S(2)}, u32[]{:S(2)}) %all-to-all-start.2) | async-done | bytes 2097184 | tf_op jit(solution)/shard_map/all_to_all | solution.py:305
  216.0 4.6 %all-to-all-start.3 = ((bf16[8,128,1024]{2,1,0:T(8,128)(2,1)}), bf16[8,128,1024]{2,1,0:T(8,128)(2,1)}, u32[]{:S(2)}, u32[]{:S(2)}) async-start(bf16[8,128,1024]{2,1,0:T(8,128)(2,1)} %bitcast.53), calls=%async_computation.3 | async-start | bytes 4194304 | tf_op jit(solution)/shard_map/all_to_all | solution.py:305
  221.7 1.1 copy-done.22
  222.9 4.2 %finish.3 = f32[256,8,768]{2,1,0:T(8,128)} custom-call(s32[1]{0:T(128)} %bitcast.5.me_ref, bf16[2,256,768]{2,1,0:T(8,128)(2,1)S(1)} %copy-done.20, bf16[2,256,768]{2,1,0:T(8,128)(2,1)S(1)} %copy-done.22, bf16[2,256,768]{2,1,0:T(8,128)(2,1)} %collective-permute-done.13.refs_2_, bf16[2,256,768]{2,1,0:T(8,128)(2,1)} %collective-permute-done.14.refs_3_), custom_call_target="tpu_custom_call" | custom-call | flops 137438953472 | bytes 1024 | tf_op jit(solution)/shard_map/finish/pallas_call | solution.py:452
  228.0 1.6 collective-permute-start.22
  229.6 12.8 %collective-permute-done.16.refs_2_ = bf16[2,256,768]{2,1,0:T(8,128)(2,1)S(1)} collective-permute-done((bf16[2,256,768]{2,1,0:T(8,128)(2,1)}, bf16[2,256,768]{2,1,0:T(8,128)(2,1)S(1)}, u32[]{:S(2)}, u32[]{:S(2)}) %collective-permute-start.16) | collective-permute-done | bytes 786464 | tf_op jit(solution)/shard_map/ppermute | solution.py:235
  243.3 1.4 collective-permute-start.20
  246.5 1.1 copy-done.13
  249.9 2.8 finish.4
  252.7 2.9 bitcast_reduce_fusion
  256.0 3.3 %fusion.44 = f32[512,1024]{1,0:T(8,128)S(1)} fusion(bf16[1024,512]{1,0:T(8,128)(2,1)} %reduce-precision_convert_fusion, bf16[1024,1024]{1,0:T(8,128)(2,1)} %bitcast.13), kind=kOutput, calls=%fused_computation.109 | convolution fusion | flops 1073741824 | bytes 5242880 | tf_op jit(solution)/shard_map/dot_general | solution.py:15
  259.3 2.9 add_convert_fusion
  263.3 6.1 %all-to-all-done.3 = bf16[8,128,1024]{2,1,0:T(8,128)(2,1)} async-done(((bf16[8,128,1024]{2,1,0:T(8,128)(2,1)}), bf16[8,128,1024]{2,1,0:T(8,128)(2,1)}, u32[]{:S(2)}, u32[]{:S(2)}) %all-to-all-start.3) | async-done | bytes 2097184 | tf_op jit(solution)/shard_map/all_to_all | solution.py:305
  269.4 3.1 %convolution_convert_fusion = bf16[512,1024]{1,0:T(8,128)(2,1)S(1)} fusion(pred[1024,512]{1,0:T(32,128)(4,1)} %copy-done.25, bf16[1024,1024]{1,0:T(8,128)(2,1)} %bitcast.17), kind=kOutput, calls=%fused_computation.15 | convolution fusion | flops 1074266112 | bytes 3670016 | tf_op jit(solution)/shard_map/dot_general | solution.py:15
  272.6 1.5 collective-permute-start.24
  274.1 1.4 collective-permute-start.26
  276.5 2.0 collective-permute-start.21
  278.5 1.5 collective-permute-start.23
  280.0 1.9 collective-permute-done.24
  281.9 1.4 collective-permute-start.19
  283.3 2.8 finish.5
  286.1 2.3 collective-permute-done.26
  288.4 9.0 %collective-permute-done.25 = bf16[128,1024]{1,0:T(8,128)(2,1)S(1)} collective-permute-done((bf16[128,1024]{1,0:T(8,128)(2,1)S(1)}, bf16[128,1024]{1,0:T(8,128)(2,1)S(1)}, u32[]{:S(2)}, u32[]{:S(2)}) %collective-permute-start.25) | collective-permute-done | bytes 262176 | tf_op jit(solution)/shard_map/ppermute | solution.py:235
  298.4 3.3 %collective-permute-done.21 = bf16[128,1152]{1,0:T(8,128)(2,1)S(1)} collective-permute-done((bf16[128,1152]{1,0:T(8,128)(2,1)S(1)}, bf16[128,1152]{1,0:T(8,128)(2,1)S(1)}, u32[]{:S(2)}, u32[]{:S(2)}) %collective-permute-start.21) | collective-permute-done | bytes 294944 | tf_op jit(solution)/shard_map/ppermute | solution.py:235
  (147 shorter events, 28.5 us)
Async XLA Ops:
  3.2 21.1 %collective-permute-start.2 = (bf16[128,2176]{1,0:T(8,128)(2,1)S(1)}, bf16[128,2176]{1,0:T(8,128)(2,1)S(1)}, u32[]{:S(2)}, u32[]{:S(2)}) collective-permute-start(bf16[128,2176]{1,0:T(8,128)(2,1)S(1)} %fusion.18.refs_0_), channel_id=1, source_target_pairs={{0,24},{8,16},{16,8},{24,0},{1,25},{9,17},{17,9},{25,1},{2,26},{10... | collective-permute-start | bytes 1671176 | tf_op jit(solution)/shard_map/ppermute | solution.py:235
  7.2 24.6 %collective-permute-start.1 = (bf16[128,2176]{1,0:T(8,128)(2,1)S(1)}, bf16[128,2176]{1,0:T(8,128)(2,1)S(1)}, u32[]{:S(2)}, u32[]{:S(2)}) collective-permute-start(bf16[128,2176]{1,0:T(8,128)(2,1)S(1)} %fusion.18.refs_0_), channel_id=1, source_target_pairs={{0,16},{8,24},{16,0},{24,8},{1,17},{9,25},{17,1},{25,9},{2,18},{10... | collective-permute-start | bytes 1671176 | tf_op jit(solution)/shard_map/ppermute | solution.py:235
  7.7 24.3 %collective-permute-start = (bf16[128,2176]{1,0:T(8,128)(2,1)S(1)}, bf16[128,2176]{1,0:T(8,128)(2,1)S(1)}, u32[]{:S(2)}, u32[]{:S(2)}) collective-permute-start(bf16[128,2176]{1,0:T(8,128)(2,1)S(1)} %fusion.18.refs_0_), channel_id=1, source_target_pairs={{0,8},{8,0},{16,24},{24,16},{1,9},{9,1},{17,25},{25,17},{2,10},{10... | collective-permute-start | bytes 1671176 | tf_op jit(solution)/shard_map/ppermute | solution.py:235
  8.0 28.3 %copy-start.38 = (s32[16]{0:T(128)}, s32[16]{0:T(128)S(1)}, u32[]{:S(2)}) copy-start(s32[16]{0:T(128)S(1)} %add.137) | copy-start | bytes 196
  8.0 4.3 %copy-start.29 = (bf16[256,8,768]{2,1,0:T(8,128)(2,1)S(1)}, bf16[256,8,768]{2,1,0:T(8,128)(2,1)}, u32[]{:S(2)}) copy-start(bf16[256,8,768]{2,1,0:T(8,128)(2,1)} %param.11) | copy-start | bytes 9437188
  12.3 2.7 copy-start.30
  17.3 3.2 %copy-start.24 = (bf16[256,8,768]{2,0,1:T(8,128)(2,1)S(1)}, bf16[256,8,768]{2,0,1:T(8,128)(2,1)}, u32[]{:S(2)}) copy-start(bf16[256,8,768]{2,0,1:T(8,128)(2,1)} %copy.57) | copy-start | bytes 9437188
  24.3 78.2 %copy-start.5 = (bf16[128,2176]{1,0:T(8,128)(2,1)}, bf16[128,2176]{1,0:T(8,128)(2,1)S(1)}, u32[]{:S(2)}) copy-start(bf16[128,2176]{1,0:T(8,128)(2,1)S(1)} %collective-permute-done.2.refs_3_) | copy-start | bytes 1671172
  31.8 70.7 %copy-start.6 = (bf16[128,2176]{1,0:T(8,128)(2,1)}, bf16[128,2176]{1,0:T(8,128)(2,1)S(1)}, u32[]{:S(2)}) copy-start(bf16[128,2176]{1,0:T(8,128)(2,1)S(1)} %collective-permute-done.1.refs_2_) | copy-start | bytes 1671172
  32.0 70.4 %copy-start.7 = (bf16[128,2176]{1,0:T(8,128)(2,1)}, bf16[128,2176]{1,0:T(8,128)(2,1)S(1)}, u32[]{:S(2)}) copy-start(bf16[128,2176]{1,0:T(8,128)(2,1)S(1)} %collective-permute-done.refs_1_) | copy-start | bytes 1671172
  32.1 21.8 %collective-permute-start.5 = (bf16[2,256,768]{2,1,0:T(8,128)(2,1)}, bf16[2,256,768]{2,1,0:T(8,128)(2,1)}, u32[]{:S(2)}, u32[]{:S(2)}) collective-permute-start(bf16[2,256,768]{2,1,0:T(8,128)(2,1)} %get-tuple-element.101), channel_id=1, source_target_pairs={{0,24},{8,16},{16,8},{24,0},{1,25},{9,17},{17,9},{25,1},{2,26},{10... | collective-permute-start | bytes 2359304 | tf_op jit(solution)/shard_map/ppermute | solution.py:235
  33.7 35.7 %collective-permute-start.4 = (bf16[2,256,768]{2,1,0:T(8,128)(2,1)}, bf16[2,256,768]{2,1,0:T(8,128)(2,1)}, u32[]{:S(2)}, u32[]{:S(2)}) collective-permute-start(bf16[2,256,768]{2,1,0:T(8,128)(2,1)} %get-tuple-element.99), channel_id=1, source_target_pairs={{0,16},{8,24},{16,0},{24,8},{1,17},{9,25},{17,1},{25,9},{2,18},{10... | collective-permute-start | bytes 2359304 | tf_op jit(solution)/shard_map/ppermute | solution.py:235
  35.1 34.6 %collective-permute-start.3 = (bf16[2,256,768]{2,1,0:T(8,128)(2,1)}, bf16[2,256,768]{2,1,0:T(8,128)(2,1)}, u32[]{:S(2)}, u32[]{:S(2)}) collective-permute-start(bf16[2,256,768]{2,1,0:T(8,128)(2,1)} %get-tuple-element.97), channel_id=1, source_target_pairs={{0,8},{8,0},{16,24},{24,16},{1,9},{9,1},{17,25},{25,17},{2,10},{10... | collective-permute-start | bytes 2359304 | tf_op jit(solution)/shard_map/ppermute | solution.py:235
  36.0 2.3 copy-start.36
  43.0 54.0 %all-to-all-start = ((bf16[8,128,1024]{2,1,0:T(8,128)(2,1)}), bf16[8,128,1024]{2,1,0:T(8,128)(2,1)}, u32[]{:S(2)}, u32[]{:S(2)}) async-start(bf16[8,128,1024]{2,1,0:T(8,128)(2,1)} %bitcast.8), calls=%async_computation | async-start | bytes 4194304 | tf_op jit(solution)/shard_map/all_to_all | solution.py:305
  69.7 34.1 %collective-permute-start.8 = (bf16[2,256,768]{2,1,0:T(8,128)(2,1)}, bf16[2,256,768]{2,1,0:T(8,128)(2,1)}, u32[]{:S(2)}, u32[]{:S(2)}) collective-permute-start(bf16[2,256,768]{2,1,0:T(8,128)(2,1)} %get-tuple-element.114), channel_id=1, source_target_pairs={{0,24},{8,16},{16,8},{24,0},{1,25},{9,17},{17,9},{25,1},{2,26},{10... | collective-permute-start | bytes 2359304 | tf_op jit(solution)/shard_map/ppermute | solution.py:235
  71.1 35.8 %collective-permute-start.7 = (bf16[2,256,768]{2,1,0:T(8,128)(2,1)}, bf16[2,256,768]{2,1,0:T(8,128)(2,1)}, u32[]{:S(2)}, u32[]{:S(2)}) collective-permute-start(bf16[2,256,768]{2,1,0:T(8,128)(2,1)} %get-tuple-element.112), channel_id=1, source_target_pairs={{0,16},{8,24},{16,0},{24,8},{1,17},{9,25},{17,1},{25,9},{2,18},{10... | collective-permute-start | bytes 2359304 | tf_op jit(solution)/shard_map/ppermute | solution.py:235
  72.6 36.1 %collective-permute-start.6 = (bf16[2,256,768]{2,1,0:T(8,128)(2,1)}, bf16[2,256,768]{2,1,0:T(8,128)(2,1)}, u32[]{:S(2)}, u32[]{:S(2)}) collective-permute-start(bf16[2,256,768]{2,1,0:T(8,128)(2,1)} %get-tuple-element.110), channel_id=1, source_target_pairs={{0,8},{8,0},{16,24},{24,16},{1,9},{9,1},{17,25},{25,17},{2,10},{10... | collective-permute-start | bytes 2359304 | tf_op jit(solution)/shard_map/ppermute | solution.py:235
  76.1 1.3 copy-start.2
  97.0 5.4 %copy-start.26 = (pred[1024,512]{1,0:T(32,128)(4,1)S(1)}, pred[1024,512]{1,0:T(32,128)(4,1)}, u32[]{:S(2)}) copy-start(pred[1024,512]{1,0:T(32,128)(4,1)} %copy-done.25) | copy-start | bytes 1572868
  97.1 53.6 %all-to-all-start.1 = ((bf16[8,128,1024]{2,1,0:T(8,128)(2,1)}), bf16[8,128,1024]{2,1,0:T(8,128)(2,1)}, u32[]{:S(2)}, u32[]{:S(2)}) async-start(bf16[8,128,1024]{2,1,0:T(8,128)(2,1)} %bitcast.43), calls=%async_computation.1 | async-start | bytes 4194304 | tf_op jit(solution)/shard_map/all_to_all | solution.py:305
  101.7 2.1 copy-start.34
  101.7 5.2 %copy-start.33 = (bf16[2,256,768]{2,1,0:T(8,128)(2,1)S(1)}, bf16[2,256,768]{2,1,0:T(8,128)(2,1)}, u32[]{:S(2)}) copy-start(bf16[2,256,768]{2,1,0:T(8,128)(2,1)} %get-tuple-element.120) | copy-start | bytes 2359300
  101.7 6.9 %copy-start.32 = (bf16[2,256,768]{2,1,0:T(8,128)(2,1)S(1)}, bf16[2,256,768]{2,1,0:T(8,128)(2,1)}, u32[]{:S(2)}) copy-start(bf16[2,256,768]{2,1,0:T(8,128)(2,1)} %get-tuple-element.118) | copy-start | bytes 2359300
  103.8 21.3 %collective-permute-start.11 = (bf16[2,256,768]{2,1,0:T(8,128)(2,1)S(1)}, bf16[2,256,768]{2,1,0:T(8,128)(2,1)S(1)}, u32[]{:S(2)}, u32[]{:S(2)}) collective-permute-start(bf16[2,256,768]{2,1,0:T(8,128)(2,1)S(1)} %copy-done.34), channel_id=1, source_target_pairs={{0,24},{8,16},{16,8},{24,0},{1,25},{9,17},{17,9},{25,1},{2,26},{10... | collective-permute-start | bytes 2359304 | tf_op jit(solution)/shard_map/ppermute | solution.py:235
  106.9 34.2 %collective-permute-start.10 = (bf16[2,256,768]{2,1,0:T(8,128)(2,1)S(1)}, bf16[2,256,768]{2,1,0:T(8,128)(2,1)S(1)}, u32[]{:S(2)}, u32[]{:S(2)}) collective-permute-start(bf16[2,256,768]{2,1,0:T(8,128)(2,1)S(1)} %copy-done.33), channel_id=1, source_target_pairs={{0,16},{8,24},{16,0},{24,8},{1,17},{9,25},{17,1},{25,9},{2,18},{10... | collective-permute-start | bytes 2359304 | tf_op jit(solution)/shard_map/ppermute | solution.py:235
  108.7 32.5 %collective-permute-start.9 = (bf16[2,256,768]{2,1,0:T(8,128)(2,1)S(1)}, bf16[2,256,768]{2,1,0:T(8,128)(2,1)S(1)}, u32[]{:S(2)}, u32[]{:S(2)}) collective-permute-start(bf16[2,256,768]{2,1,0:T(8,128)(2,1)S(1)} %copy-done.32), channel_id=1, source_target_pairs={{0,8},{8,0},{16,24},{24,16},{1,9},{9,1},{17,25},{25,17},{2,10},{10... | collective-permute-start | bytes 2359304 | tf_op jit(solution)/shard_map/ppermute | solution.py:235
  141.2 1.4 copy-start
  142.6 8.0 %copy-start.1 = (bf16[2,512,768]{2,1,0:T(8,128)(2,1)S(1)}, bf16[2,512,768]{2,1,0:T(8,128)(2,1)}, u32[]{:S(2)}) copy-start(bf16[2,512,768]{2,1,0:T(8,128)(2,1)} %get-tuple-element.115.h_ref.y_ref) | copy-start | bytes 4718596
  158.9 44.3 %collective-permute-start.12 = (bf16[2,256,768]{2,1,0:T(8,128)(2,1)}, bf16[2,256,768]{2,1,0:T(8,128)(2,1)S(1)}, u32[]{:S(2)}, u32[]{:S(2)}) collective-permute-start(bf16[2,256,768]{2,1,0:T(8,128)(2,1)} %get-tuple-element.126), channel_id=1, source_target_pairs={{0,8},{8,0},{16,24},{24,16},{1,9},{9,1},{17,25},{25,17},{2,10},{10... | collective-permute-start | bytes 2359304 | tf_op jit(solution)/shard_map/ppermute | solution.py:235
  160.4 43.7 %collective-permute-start.13 = (bf16[2,256,768]{2,1,0:T(8,128)(2,1)}, bf16[2,256,768]{2,1,0:T(8,128)(2,1)}, u32[]{:S(2)}, u32[]{:S(2)}) collective-permute-start(bf16[2,256,768]{2,1,0:T(8,128)(2,1)} %get-tuple-element.127), channel_id=1, source_target_pairs={{0,16},{8,24},{16,0},{24,8},{1,17},{9,25},{17,1},{25,9},{2,18},{10... | collective-permute-start | bytes 2359304 | tf_op jit(solution)/shard_map/ppermute | solution.py:235
  161.2 43.0 %collective-permute-start.14 = (bf16[2,256,768]{2,1,0:T(8,128)(2,1)}, bf16[2,256,768]{2,1,0:T(8,128)(2,1)}, u32[]{:S(2)}, u32[]{:S(2)}) collective-permute-start(bf16[2,256,768]{2,1,0:T(8,128)(2,1)} %get-tuple-element.128), channel_id=1, source_target_pairs={{0,24},{8,16},{16,8},{24,0},{1,25},{9,17},{17,9},{25,1},{2,26},{10... | collective-permute-start | bytes 2359304 | tf_op jit(solution)/shard_map/ppermute | solution.py:235
  162.4 4.5 %copy-start.11 = (bf16[2,256,768]{2,1,0:T(8,128)(2,1)S(1)}, bf16[2,256,768]{2,1,0:T(8,128)(2,1)}, u32[]{:S(2)}) copy-start(bf16[2,256,768]{2,1,0:T(8,128)(2,1)} %copy-done.10) | copy-start | bytes 2359300
  162.4 53.6 %all-to-all-start.2 = ((bf16[8,128,1024]{2,1,0:T(8,128)(2,1)}), bf16[8,128,1024]{2,1,0:T(8,128)(2,1)}, u32[]{:S(2)}, u32[]{:S(2)}) async-start(bf16[8,128,1024]{2,1,0:T(8,128)(2,1)} %bitcast.12), calls=%async_computation.2 | async-start | bytes 4194304 | tf_op jit(solution)/shard_map/all_to_all | solution.py:305
  175.4 1.2 copy-start.3
  176.6 7.7 %copy-start.23 = (bf16[2,512,768]{2,1,0:T(8,128)(2,1)}, bf16[2,512,768]{2,1,0:T(8,128)(2,1)S(1)}, u32[]{:S(2)}) copy-start(bf16[2,512,768]{2,1,0:T(8,128)(2,1)S(1)} %get-tuple-element.139.y_ref.gd_ref) | copy-start | bytes 4718596
  185.2 10.5 %copy-start.4 = (bf16[2,512,768]{2,1,0:T(8,128)(2,1)S(1)}, bf16[2,512,768]{2,1,0:T(8,128)(2,1)}, u32[]{:S(2)}) copy-start(bf16[2,512,768]{2,1,0:T(8,128)(2,1)} %copy-done.3) | copy-start | bytes 4718596
  204.2 22.9 %collective-permute-start.17 = (bf16[2,256,768]{2,1,0:T(8,128)(2,1)}, bf16[2,256,768]{2,1,0:T(8,128)(2,1)S(1)}, u32[]{:S(2)}, u32[]{:S(2)}) collective-permute-start(bf16[2,256,768]{2,1,0:T(8,128)(2,1)} %get-tuple-element.148), channel_id=1, source_target_pairs={{0,24},{8,16},{16,8},{24,0},{1,25},{9,17},{17,9},{25,1},{2,26},{10... | collective-permute-start | bytes 2359304 | tf_op jit(solution)/shard_map/ppermute | solution.py:235
  205.9 36.6 %collective-permute-start.16 = (bf16[2,256,768]{2,1,0:T(8,128)(2,1)}, bf16[2,256,768]{2,1,0:T(8,128)(2,1)S(1)}, u32[]{:S(2)}, u32[]{:S(2)}) collective-permute-start(bf16[2,256,768]{2,1,0:T(8,128)(2,1)} %get-tuple-element.147), channel_id=1, source_target_pairs={{0,16},{8,24},{16,0},{24,8},{1,17},{9,25},{17,1},{25,9},{2,18},{10... | collective-permute-start | bytes 2359304 | tf_op jit(solution)/shard_map/ppermute | solution.py:235
  207.1 37.6 %collective-permute-start.15 = (bf16[2,256,768]{2,1,0:T(8,128)(2,1)}, bf16[2,256,768]{2,1,0:T(8,128)(2,1)S(1)}, u32[]{:S(2)}, u32[]{:S(2)}) collective-permute-start(bf16[2,256,768]{2,1,0:T(8,128)(2,1)} %get-tuple-element.146), channel_id=1, source_target_pairs={{0,8},{8,0},{16,24},{24,16},{1,9},{9,1},{17,25},{25,17},{2,10},{10... | collective-permute-start | bytes 2359304 | tf_op jit(solution)/shard_map/ppermute | solution.py:235
  216.0 53.4 %all-to-all-start.3 = ((bf16[8,128,1024]{2,1,0:T(8,128)(2,1)}), bf16[8,128,1024]{2,1,0:T(8,128)(2,1)}, u32[]{:S(2)}, u32[]{:S(2)}) async-start(bf16[8,128,1024]{2,1,0:T(8,128)(2,1)} %bitcast.53), calls=%async_computation.3 | async-start | bytes 4194304 | tf_op jit(solution)/shard_map/all_to_all | solution.py:305
  220.6 1.1 copy-start.20
  221.7 1.1 copy-start.22
  222.9 23.6 %copy-start.9 = (bf16[2,256,768]{2,1,0:T(8,128)(2,1)S(1)}, bf16[2,256,768]{2,1,0:T(8,128)(2,1)}, u32[]{:S(2)}) copy-start(bf16[2,256,768]{2,1,0:T(8,128)(2,1)} %copy-done.8) | copy-start | bytes 2359300
  228.0 48.5 %collective-permute-start.22 = (bf16[2,256,768]{2,1,0:T(8,128)(2,1)}, bf16[2,256,768]{2,1,0:T(8,128)(2,1)S(1)}, u32[]{:S(2)}, u32[]{:S(2)}) collective-permute-start(bf16[2,256,768]{2,1,0:T(8,128)(2,1)} %get-tuple-element.160), channel_id=1, source_target_pairs={{0,24},{8,16},{16,8},{24,0},{1,25},{9,17},{17,9},{25,1},{2,26},{10... | collective-permute-start | bytes 2359304 | tf_op jit(solution)/shard_map/ppermute | solution.py:235
  243.3 33.2 %collective-permute-start.20 = (bf16[2,256,768]{2,1,0:T(8,128)(2,1)}, bf16[2,256,768]{2,1,0:T(8,128)(2,1)S(1)}, u32[]{:S(2)}, u32[]{:S(2)}) collective-permute-start(bf16[2,256,768]{2,1,0:T(8,128)(2,1)} %get-tuple-element.157), channel_id=1, source_target_pairs={{0,16},{8,24},{16,0},{24,8},{1,17},{9,25},{17,1},{25,9},{2,18},{10... | collective-permute-start | bytes 2359304 | tf_op jit(solution)/shard_map/ppermute | solution.py:235
  245.7 7.0 %slice-start = ((bf16[128,2176]{1,0:T(8,128)(2,1)}), bf16[128,1024]{1,0:T(8,128)(2,1)S(1)}, s32[]{:S(2)}) async-start(bf16[128,2176]{1,0:T(8,128)(2,1)} %copy-done.5), calls=%async_computation.4 | async-start | bytes 524288 | tf_op jit(solution)/shard_map/slice | solution.py:398
  245.7 7.0 %slice-start.1 = ((bf16[128,2176]{1,0:T(8,128)(2,1)}), bf16[128,1024]{1,0:T(8,128)(2,1)S(1)}, s32[]{:S(2)}) async-start(bf16[128,2176]{1,0:T(8,128)(2,1)} %copy-done.6), calls=%async_computation.5 | async-start | bytes 524288 | tf_op jit(solution)/shard_map/slice | solution.py:398
  245.7 7.0 %slice-start.2 = ((bf16[128,2176]{1,0:T(8,128)(2,1)}), bf16[128,1024]{1,0:T(8,128)(2,1)S(1)}, s32[]{:S(2)}) async-start(bf16[128,2176]{1,0:T(8,128)(2,1)} %copy-done.7), calls=%async_computation.6 | async-start | bytes 524288 | tf_op jit(solution)/shard_map/slice | solution.py:398
  245.7 30.6 %collective-permute-start.18 = (bf16[2,256,768]{2,1,0:T(8,128)(2,1)}, bf16[2,256,768]{2,1,0:T(8,128)(2,1)S(1)}, u32[]{:S(2)}, u32[]{:S(2)}) collective-permute-start(bf16[2,256,768]{2,1,0:T(8,128)(2,1)} %get-tuple-element.154), channel_id=1, source_target_pairs={{0,8},{8,0},{16,24},{24,16},{1,9},{9,1},{17,25},{25,17},{2,10},{10... | collective-permute-start | bytes 2359304 | tf_op jit(solution)/shard_map/ppermute | solution.py:235
  246.5 1.1 copy-start.13
  247.6 1.1 copy-start.15
  249.9 2.8 copy-start.27
  249.9 2.8 copy-start.35
  252.7 3.0 copy-start.37
  252.7 3.0 copy-start.39
  256.0 3.3 %copy-start.31 = (bf16[1024,512]{1,0:T(8,128)(2,1)S(1)}, bf16[1024,512]{1,0:T(8,128)(2,1)}, u32[]{:S(2)}) copy-start(bf16[1024,512]{1,0:T(8,128)(2,1)} %get-tuple-element.196) | copy-start | bytes 3145732
  272.5 3.9 %copy-start.28 = (bf16[512,1152]{1,0:T(8,128)(2,1)S(1)}, bf16[512,1152]{1,0:T(8,128)(2,1)}, u32[]{:S(2)}) copy-start(bf16[512,1152]{1,0:T(8,128)(2,1)} %fusion.3) | copy-start | bytes 3538948
  272.6 9.3 %collective-permute-start.24 = (bf16[128,1024]{1,0:T(8,128)(2,1)S(1)}, bf16[128,1024]{1,0:T(8,128)(2,1)S(1)}, u32[]{:S(2)}, u32[]{:S(2)}) collective-permute-start(bf16[128,1024]{1,0:T(8,128)(2,1)S(1)} %get-tuple-element.210), channel_id=1, source_target_pairs={{0,8},{8,0},{16,24},{24,16},{1,9},{9,1},{17,25},{25,17},{2,10},{10... | collective-permute-start | bytes 786440 | tf_op jit(solution)/shard_map/ppermute | solution.py:235
  274.1 14.3 %collective-permute-start.26 = (bf16[128,1024]{1,0:T(8,128)(2,1)S(1)}, bf16[128,1024]{1,0:T(8,128)(2,1)S(1)}, u32[]{:S(2)}, u32[]{:S(2)}) collective-permute-start(bf16[128,1024]{1,0:T(8,128)(2,1)S(1)} %get-tuple-element.211), channel_id=1, source_target_pairs={{0,24},{8,16},{16,8},{24,0},{1,25},{9,17},{17,9},{25,1},{2,26},{10... | collective-permute-start | bytes 786440 | tf_op jit(solution)/shard_map/ppermute | solution.py:235
  276.3 21.2 %collective-permute-start.25 = (bf16[128,1024]{1,0:T(8,128)(2,1)S(1)}, bf16[128,1024]{1,0:T(8,128)(2,1)S(1)}, u32[]{:S(2)}, u32[]{:S(2)}) collective-permute-start(bf16[128,1024]{1,0:T(8,128)(2,1)S(1)} %get-tuple-element.212), channel_id=1, source_target_pairs={{0,16},{8,24},{16,0},{24,8},{1,17},{9,25},{17,1},{25,9},{2,18},{10... | collective-permute-start | bytes 786440 | tf_op jit(solution)/shard_map/ppermute | solution.py:235
  276.5 25.2 %collective-permute-start.21 = (bf16[128,1152]{1,0:T(8,128)(2,1)S(1)}, bf16[128,1152]{1,0:T(8,128)(2,1)S(1)}, u32[]{:S(2)}, u32[]{:S(2)}) collective-permute-start(bf16[128,1152]{1,0:T(8,128)(2,1)S(1)} %get-tuple-element.158), channel_id=1, source_target_pairs={{0,16},{8,24},{16,0},{24,8},{1,17},{9,25},{17,1},{25,9},{2,18},{10... | collective-permute-start | bytes 884744 | tf_op jit(solution)/shard_map/ppermute | solution.py:235
  278.5 23.3 %collective-permute-start.23 = (bf16[128,1152]{1,0:T(8,128)(2,1)S(1)}, bf16[128,1152]{1,0:T(8,128)(2,1)S(1)}, u32[]{:S(2)}, u32[]{:S(2)}) collective-permute-start(bf16[128,1152]{1,0:T(8,128)(2,1)S(1)} %get-tuple-element.161), channel_id=1, source_target_pairs={{0,24},{8,16},{16,8},{24,0},{1,25},{9,17},{17,9},{25,1},{2,26},{10... | collective-permute-start | bytes 884744 | tf_op jit(solution)/shard_map/ppermute | solution.py:235
  281.9 19.8 %collective-permute-start.19 = (bf16[128,1152]{1,0:T(8,128)(2,1)S(1)}, bf16[128,1152]{1,0:T(8,128)(2,1)S(1)}, u32[]{:S(2)}, u32[]{:S(2)}) collective-permute-start(bf16[128,1152]{1,0:T(8,128)(2,1)S(1)} %get-tuple-element.155), channel_id=1, source_target_pairs={{0,8},{8,0},{16,24},{24,16},{1,9},{9,1},{17,25},{25,17},{2,10},{10... | collective-permute-start | bytes 884744 | tf_op jit(solution)/shard_map/ppermute | solution.py:235
  (10 other events, 9.2 us)

commit v4 on v3

--- a/solution.py
+++ b/solution.py
@@ -1,3 +1,5 @@
+import functools
+
 import jax
 import jax.numpy as jnp
 from jax import lax
@@ -161,14 +163,17 @@
             b_ref[0, at, :] = act
 
 
-def outer_kernel(me_ref, x_ref, y_ref, *outs):
+def outer_kernel(count, me_ref, x_ref, *refs):
+    ys, outs = refs[:count], refs[count:]
+    nb = len(outs) // count
     j = pl.program_id(1)
-    x = x_ref[...].reshape(y_ref.shape[1], x_ref.shape[-1])
-    for s in range(len(outs)):
+    x = x_ref[...].reshape(ys[0].shape[1], x_ref.shape[-1])
+    for s in range(nb):
 
         @pl.when(j == s)
         def _(s=s):
-            outs[s][0] = dot(x, y_ref[0], 0, 0).astype(BF)
+            for n in range(count):
+                outs[n * nb + s][0] = dot(x, ys[n][0], 0, 0).astype(BF)
 
 
 def output_kernel(me_ref, h_ref, *refs):
@@ -335,17 +340,19 @@
         COSTS[6],
     )(me_arr, routed, *gate_p, *up_p)
 
-    def outer(x, y, cost):
-        return call(
-            outer_kernel,
+    def outer(x, ys, cost):
+        count = len(ys)
+        got = call(
+            functools.partial(outer_kernel, count),
             "outer",
             grid,
-            [rows_spec, wide_spec],
-            [piece_spec] * nb,
-            [piece] * nb,
+            [rows_spec] + [wide_spec] * count,
+            [piece_spec] * (nb * count),
+            [piece] * (nb * count),
             (),
             cost,
-        )(me_arr, x, y)
+        )(me_arr, x, *ys)
+        return [got[n * nb : (n + 1) * nb] for n in range(count)]
 
     def send_back(parts, deps):
         got = [parts[0]]
@@ -357,7 +364,7 @@
         output_kernel, "outputs", grid, [wide_spec] + weight_specs, rows_spec, full
     )(me_arr, hidden, *down_p)
     graded, outs = lax.optimization_barrier((graded, outs))
-    down_part = outer(graded, hidden, LIGHT)
+    (down_part,) = outer(graded, [hidden], LIGHT)
     down_got = send_back(down_part, None)
     graded = after(graded, down_part)
     gate_delta, up_delta = call(
@@ -371,7 +378,7 @@
         COSTS[0],
     )(me_arr, graded, a, b, *down_p)
     outs = exchange(after(outs, down_part)).reshape(slots, width)
-    gate_part = outer(routed, gate_delta, COSTS[1])
+    gate_part, up_part = outer(routed, [gate_delta, up_delta], COSTS[1])
     gate_got = send_back(gate_part, down_got)
     gate_delta = after(gate_delta, gate_part)
     backs = call(
@@ -384,7 +391,6 @@
         (),
         COSTS[3],
     )(me_arr, gate_delta, up_delta, *gate_p, *up_p)
-    up_part = outer(routed, after(up_delta, backs), COSTS[2])
     up_got = send_back(up_part, gate_got)
     down_got = after(down_got, backs)
     backs = exchange(backs).reshape(slots, width)

time: 305 us -> 304 us (level)
  Pallas kernels: 75.5 us -> 69.7 us
  waiting for transfers between devices: 115 us -> 119 us
    all_to_all x4, waiting for transfers between devices: 34.6 us -> 44 us  [exchange(): lax.all_to_all(x, 'ep', split_axis=0, concat_axis=0, tiled=True)]
    pallas_call x3 -> x2, Pallas kernels: 22.7 us -> 17.1 us  [outer(): call(functools.partial(outer_kernel, count), 'outer', grid, [rows_spec] +...]
    ppermute x27, waiting for transfers between devices: 80.2 us -> 74.8 us  [hop(): return lax.ppermute(x, 'blk', [(i, i ^ j) for i in range(nb)])]
    unnamed x84 -> x82, local copies, waits for them, and re-layouts: 27.3 us -> 28.4 us
  transfers between devices with their start and end apart: 31 -> 31, of which waited for: 18 -> 17; matrix products, arithmetic and copies ran while one was open for 12% -> 12% of each run, Pallas kernels for 22% -> 21%
where the time goes in v4:
time: 304 us; the launch traced here: 303 us
  waiting for transfers between devices  119 us (39%)
  Pallas kernels  69.7 us (23%)
  starting transfers between devices  52.5 us (17%)
  local copies, waits for them, and re-layouts  38.6 us (13%)
  matrix products  12.5 us (4%)
  other arithmetic  9.57 us (3%)
    ppermute x27, waiting for transfers between devices, hop(): return lax.ppermute(x, 'blk', [(i, i ^ j) for i in range(nb)])  74.8 us
    all_to_all x4, waiting for transfers between devices, exchange(): lax.all_to_all(x, 'ep', split_axis=0, concat_axis=0, tiled=True)  44 us
    ppermute x27, starting transfers between devices, hop(): return lax.ppermute(x, 'blk', [(i, i ^ j) for i in range(nb)])  33.9 us
    unnamed x82, local copies, waits for them, and re-layouts  28.4 us
    all_to_all x4, starting transfers between devices, exchange(): lax.all_to_all(x, 'ep', split_axis=0, concat_axis=0, tiled=True)  18.6 us
    pallas_call x2, Pallas kernels, outer(): call(functools.partial(outer_kernel, count), 'outer', grid, [rows_spec] +...  17.1 us
    dot_general x5, matrix products, dot(): lax.dot_general(a, b, (((ca,), (cb,)), ((), ())), preferred_element_type=...  12.5 us
    pallas_call x1, Pallas kernels, expert_body(): call(forward_kernel, 'forward', grid, [rows_spec] + weight_specs * 2, [wi...  12.3 us
  transfers between devices with their start and end apart: 31, of which 17 were waited for; matrix products, arithmetic and copies ran while one was open for 12% of the time, Pallas kernels for 21%

profile of v4, /device:TPU:0, one launch (start us, length us, event | category | flops | bytes accessed | tf_op | source)
XLA Modules:
  0.0 302.9 jit_solution(17809135350323466616)
XLA Ops:
  3.2 4.0 %collective-permute-start.2 = (bf16[128,2176]{1,0:T(8,128)(2,1)S(1)}, bf16[128,2176]{1,0:T(8,128)(2,1)S(1)}, u32[]{:S(2)}, u32[]{:S(2)}) collective-permute-start(bf16[128,2176]{1,0:T(8,128)(2,1)S(1)} %fusion.18.refs_0_), channel_id=1, source_target_pairs={{0,24},{8,16},{16,8},{24,0},{1,25},{9,17},{17,9},{25,1},{2,26},{10... | collective-permute-start | bytes 1671176 | tf_op jit(solution)/shard_map/ppermute | solution.py:240
  8.0 4.3 %copy.59 = bf16[256,8,768]{2,0,1:T(8,128)(2,1)} copy(bf16[256,8,768]{2,1,0:T(8,128)(2,1)} %param.10) | data formatting | bytes 6291456 | tf_op args[3]
  12.3 2.3 copy.58
  15.0 2.3 copy.57
  17.3 3.2 %constant_dynamic-slice_fusion.6 = (bf16[2,256,768]{2,1,0:T(8,128)(2,1)}, bf16[2,256,768]{2,1,0:T(8,128)(2,1)}, bf16[2,256,768]{2,1,0:T(8,128)(2,1)}) fusion(bf16[8,256,768]{2,1,0:T(8,128)(2,1)} %bitcast.50, s32[]{:T(128)S(6)} %select_n.100, s32[]{:T(128)S(6)} %select_n.99, s32[]{:T(128)S(6)} %select_n.98), kind=kLoop, calls=%fused_computation.99 | loop fusion | bytes 4718604 | tf_op jit(solution)/shard_map/dynamic_slice | solution.py:250
  20.5 3.8 %constant_dynamic-slice_fusion = (bf16[2,256,768]{2,1,0:T(8,128)(2,1)}, bf16[2,256,768]{2,1,0:T(8,128)(2,1)}, bf16[2,256,768]{2,1,0:T(8,128)(2,1)}, bf16[2,256,7...) fusion(bf16[8,256,768]{2,1,0:T(8,128)(2,1)S(1)} %bitcast.46, s32[]{:T(128)S(6)} %select_n.100, ...), kind=kLoop, calls=%fused_computation.93 | loop fusion | bytes 9437196 | tf_op jit(solution)/shard_map/dynamic_slice | solution.py:250
  24.3 7.5 %collective-permute-done.1.refs_2_ = bf16[128,2176]{1,0:T(8,128)(2,1)S(1)} collective-permute-done((bf16[128,2176]{1,0:T(8,128)(2,1)S(1)}, bf16[128,2176]{1,0:T(8,128)(2,1)S(1)}, u32[]{:S(2)}, u32[]{:S(2)}) %collective-permute-start.1) | collective-permute-done | bytes 557088 | tf_op jit(solution)/shard_map/ppermute | solution.py:240
  32.1 1.6 collective-permute-start.5
  33.7 1.4 collective-permute-start.4
  36.7 1.7 fusion.1
  39.2 3.1 %pick.3 = bf16[1024,1024]{1,0:T(8,128)(2,1)} custom-call(s32[1]{0:T(128)} %bitcast.5.me_ref, bf16[1024,512]{1,0:T(8,128)(2,1)S(1)} %convert_element_type.63.sel_ref, f32[1024,1]{1,0:T(8,128)S(1)} %broadcast_in_dim.65.scale_ref, bf16[128,2176]{1,0:T(8,128)(2,1)S(1)} %fusion.18.refs_0_, bf16[128,2176]{1,0:T(8,128)(2,1)S(1)} %collective-permute-done.refs_1_, ...), custom_call_target="tpu_custom_call" | custom-call | flops 1024 | bytes 1024 | tf_op jit(solution)/shard_map/pick/pallas_call | solution.py:289
  43.1 4.9 %all-to-all-start = ((bf16[8,128,1024]{2,1,0:T(8,128)(2,1)}), bf16[8,128,1024]{2,1,0:T(8,128)(2,1)}, u32[]{:S(2)}, u32[]{:S(2)}) async-start(bf16[8,128,1024]{2,1,0:T(8,128)(2,1)} %bitcast.8), calls=%async_computation | async-start | bytes 4194304 | tf_op jit(solution)/shard_map/all_to_all | solution.py:310
  49.0 4.8 %collective-permute-done.5.refs_3_ = bf16[2,256,768]{2,1,0:T(8,128)(2,1)} collective-permute-done((bf16[2,256,768]{2,1,0:T(8,128)(2,1)}, bf16[2,256,768]{2,1,0:T(8,128)(2,1)}, u32[]{:S(2)}, u32[]{:S(2)}) %collective-permute-start.5) | collective-permute-done | bytes 786464 | tf_op jit(solution)/shard_map/ppermute | solution.py:240
  53.9 15.6 %collective-permute-done.4.refs_2_ = bf16[2,256,768]{2,1,0:T(8,128)(2,1)} collective-permute-done((bf16[2,256,768]{2,1,0:T(8,128)(2,1)}, bf16[2,256,768]{2,1,0:T(8,128)(2,1)}, u32[]{:S(2)}, u32[]{:S(2)}) %collective-permute-start.4) | collective-permute-done | bytes 786464 | tf_op jit(solution)/shard_map/ppermute | solution.py:240
  69.7 1.4 collective-permute-start.8
  71.1 1.4 collective-permute-start.7
  74.2 1.9 pick.2
  76.1 1.3 copy-done.2
  77.5 19.7 %all-to-all-done = bf16[8,128,1024]{2,1,0:T(8,128)(2,1)} async-done(((bf16[8,128,1024]{2,1,0:T(8,128)(2,1)}), bf16[8,128,1024]{2,1,0:T(8,128)(2,1)}, u32[]{:S(2)}, u32[]{:S(2)}) %all-to-all-start) | async-done | bytes 2097184 | tf_op jit(solution)/shard_map/all_to_all | solution.py:310
  97.2 4.6 %all-to-all-start.1 = ((bf16[8,128,1024]{2,1,0:T(8,128)(2,1)}), bf16[8,128,1024]{2,1,0:T(8,128)(2,1)}, u32[]{:S(2)}, u32[]{:S(2)}) async-start(bf16[8,128,1024]{2,1,0:T(8,128)(2,1)} %bitcast.43), calls=%async_computation.1 | async-start | bytes 4194304 | tf_op jit(solution)/shard_map/all_to_all | solution.py:310
  102.6 1.3 reduce-precision_convert_fusion
  103.9 1.7 collective-permute-start.11
  105.6 1.4 collective-permute-done.7.refs_6_
  106.9 1.7 collective-permute-start.10
  108.7 12.3 %forward.1 = (f32[2,512,768]{2,1,0:T(8,128)}, f32[2,512,768]{2,1,0:T(8,128)}, bf16[2,512,768]{2,1,0:T(8,128)(2,1)}) custom-call(s32[1]{0:T(128)} %bitcast.5.me_ref, bf16[8,2,64,1024]{3,2,1,0:T(8,128)(2,1)} %bitcast.11.x_ref, bf16[8,256,768]{2,1,0:T(8,128)(2,1)} %bitcast.51, bf16[2,256,768]{2,1,0:T(8,128)(2,1)} %collective-permute-done.3.refs_1_, ...), custom_call_target="tpu_custom_call" | custom-call | flops 34359738368 | bytes 1024 | tf_op jit(solution)/shard_map/forward/pallas_call | solution.py:332
  121.0 4.2 %collective-permute-done.11.refs_3_ = bf16[2,256,768]{2,1,0:T(8,128)(2,1)S(1)} collective-permute-done((bf16[2,256,768]{2,1,0:T(8,128)(2,1)S(1)}, bf16[2,256,768]{2,1,0:T(8,128)(2,1)S(1)}, u32[]{:S(2)}, u32[]{:S(2)}) %collective-permute-start.11) | collective-permute-done | bytes 786464 | tf_op jit(solution)/shard_map/ppermute | solution.py:240
  125.2 16.1 %collective-permute-done.10.refs_2_ = bf16[2,256,768]{2,1,0:T(8,128)(2,1)S(1)} collective-permute-done((bf16[2,256,768]{2,1,0:T(8,128)(2,1)S(1)}, bf16[2,256,768]{2,1,0:T(8,128)(2,1)S(1)}, u32[]{:S(2)}, u32[]{:S(2)}) %collective-permute-start.10) | collective-permute-done | bytes 786464 | tf_op jit(solution)/shard_map/ppermute | solution.py:240
  141.3 1.4 copy-done
  142.7 6.6 %outputs.1 = bf16[8,2,64,1024]{3,2,1,0:T(8,128)(2,1)} custom-call(s32[1]{0:T(128)} %bitcast.5.me_ref, bf16[2,512,768]{2,1,0:T(8,128)(2,1)S(1)} %copy-done, bf16[8,256,768]{2,1,0:T(8,128)(2,1)} %bitcast.44, bf16[2,256,768]{2,1,0:T(8,128)(2,1)S(1)} %collective-permute-done.9.refs_1_, bf16[2,256,768]{2,1,0:T(8,128)(2,1)S(1)} %collective-permute-done.10.refs_2_, ...), custom_call_target="tpu_custom_call" | custom-call | flops 1024 | bytes 1024 | tf_op jit(solution)/shard_map/outputs/pallas_call | solution.py:363
  150.7 7.5 %outer.2 = (bf16[2,256,768]{2,1,0:T(8,128)(2,1)S(1)}, bf16[2,256,768]{2,1,0:T(8,128)(2,1)}, bf16[2,256,768]{2,1,0:T(8,128)(2,1)}, bf16[2,256,768]{2,1,0:T(8,128)(2,1)}) custom-call(s32[1]{0:T(128)} %bitcast.5.me_ref, bf16[8,2,64,1024]{3,2,1,0:T(8,128)(2,1)} %bitcast.10.x_ref.sg_ref, bf16[2,512,768]{2,1,0:T(8,128)(2,1)S(1)} %copy-done.1), custom_call_target="tpu_custom_call" | custom-call | flops 1024 | bytes 1024 | tf_op jit(solution)/shard_map/outer/pallas_call | solution.py:345
  159.1 1.5 collective-permute-start.12
  161.3 1.3 collective-permute-start.14
  162.6 4.5 %all-to-all-start.2 = ((bf16[8,128,1024]{2,1,0:T(8,128)(2,1)}), bf16[8,128,1024]{2,1,0:T(8,128)(2,1)}, u32[]{:S(2)}, u32[]{:S(2)}) async-start(bf16[8,128,1024]{2,1,0:T(8,128)(2,1)} %bitcast.12), calls=%async_computation.2 | async-start | bytes 4194304 | tf_op jit(solution)/shard_map/all_to_all | solution.py:310
  167.1 8.5 %deltas.1 = (bf16[2,512,768]{2,1,0:T(8,128)(2,1)S(1)}, bf16[2,512,768]{2,1,0:T(8,128)(2,1)S(1)}) custom-call(s32[1]{0:T(128)} %bitcast.5.me_ref, bf16[8,2,64,1024]{3,2,1,0:T(8,128)(2,1)} %bitcast.10.x_ref.sg_ref, f32[2,512,768]{2,1,0:T(8,128)} %get-tuple-element.131.a_ref, f32[2,512,768]{2,1,0:T(8,128)} %get-tuple-element.132.b_ref, ...), custom_call_target="tpu_custom_call" | custom-call | flops 17179869184 | bytes 1024 | tf_op jit(solution)/shard_map/deltas/pallas_call | solution.py:370
  175.6 1.1 copy-done.21
  176.7 1.1 copy-done.22
  177.9 9.6 %outer.3 = (bf16[2,256,768]{2,1,0:T(8,128)(2,1)S(1)}, bf16[2,256,768]{2,1,0:T(8,128)(2,1)}, bf16[2,256,768]{2,1,0:T(8,128)(2,1)}, bf16[2,256,768]{2,1,0:T(8,128)...) custom-call(s32[1]{0:T(128)} %bitcast.5.me_ref, ...), custom_call_target="tpu_custom_call" | custom-call | flops 17179869184 | bytes 1024 | tf_op jit(solution)/shard_map/outer/pallas_call | solution.py:345
  188.4 10.4 %inputs.1 = bf16[8,2,64,1024]{3,2,1,0:T(8,128)(2,1)} custom-call(s32[1]{0:T(128)} %bitcast.5.me_ref, bf16[2,512,768]{2,1,0:T(8,128)(2,1)} %copy-done.21, bf16[2,512,768]{2,1,0:T(8,128)(2,1)} %copy-done.22, bf16[8,256,768]{2,1,0:T(8,128)(2,1)} %bitcast.52, bf16[2,256,768]{2,1,0:T(8,128)(2,1)} %collective-permute-done.3.refs_1_, ...), custom_call_target="tpu_custom_call" | custom-call | flops 34359738368 | bytes 1024 | tf_op jit(solution)/shard_map/inputs/pallas_call | solution.py:384
  199.7 1.7 collective-permute-start.17
  201.3 1.3 collective-permute-start.16
  203.2 13.0 %all-to-all-done.2 = bf16[8,128,1024]{2,1,0:T(8,128)(2,1)} async-done(((bf16[8,128,1024]{2,1,0:T(8,128)(2,1)}), bf16[8,128,1024]{2,1,0:T(8,128)(2,1)}, u32[]{:S(2)}, u32[]{:S(2)}) %all-to-all-start.2) | async-done | bytes 2097184 | tf_op jit(solution)/shard_map/all_to_all | solution.py:310
  216.2 4.6 %all-to-all-start.3 = ((bf16[8,128,1024]{2,1,0:T(8,128)(2,1)}), bf16[8,128,1024]{2,1,0:T(8,128)(2,1)}, u32[]{:S(2)}, u32[]{:S(2)}) async-start(bf16[8,128,1024]{2,1,0:T(8,128)(2,1)} %bitcast.53), calls=%async_computation.3 | async-start | bytes 4194304 | tf_op jit(solution)/shard_map/all_to_all | solution.py:310
  223.1 4.2 %finish.3 = f32[256,8,768]{2,1,0:T(8,128)} custom-call(s32[1]{0:T(128)} %bitcast.5.me_ref, bf16[2,256,768]{2,1,0:T(8,128)(2,1)S(1)} %copy-done.18, bf16[2,256,768]{2,1,0:T(8,128)(2,1)S(1)} %copy-done.20, bf16[2,256,768]{2,1,0:T(8,128)(2,1)} %collective-permute-done.13.refs_2_, bf16[2,256,768]{2,1,0:T(8,128)(2,1)} %collective-permute-done.14.refs_3_), custom_call_target="tpu_custom_call" | custom-call | flops 137438953472 | bytes 1024 | tf_op jit(solution)/shard_map/finish/pallas_call | solution.py:458
  228.2 1.6 collective-permute-start.22
  229.9 8.1 %collective-permute-done.16.refs_2_ = bf16[2,256,768]{2,1,0:T(8,128)(2,1)S(1)} collective-permute-done((bf16[2,256,768]{2,1,0:T(8,128)(2,1)}, bf16[2,256,768]{2,1,0:T(8,128)(2,1)S(1)}, u32[]{:S(2)}, u32[]{:S(2)}) %collective-permute-start.16) | collective-permute-done | bytes 786464 | tf_op jit(solution)/shard_map/ppermute | solution.py:240
  238.8 1.4 collective-permute-start.20
  242.0 1.1 copy-done.11
  243.1 1.1 copy-done.13
  245.4 2.8 finish.4
  248.2 2.9 bitcast_reduce_fusion
  251.5 3.3 %fusion.44 = f32[512,1024]{1,0:T(8,128)S(1)} fusion(bf16[1024,512]{1,0:T(8,128)(2,1)} %reduce-precision_convert_fusion, bf16[1024,1024]{1,0:T(8,128)(2,1)} %bitcast.13), kind=kOutput, calls=%fused_computation.109 | convolution fusion | flops 1073741824 | bytes 5242880 | tf_op jit(solution)/shard_map/dot_general | solution.py:17
  254.8 2.9 add_convert_fusion
  258.8 10.9 %all-to-all-done.3 = bf16[8,128,1024]{2,1,0:T(8,128)(2,1)} async-done(((bf16[8,128,1024]{2,1,0:T(8,128)(2,1)}), bf16[8,128,1024]{2,1,0:T(8,128)(2,1)}, u32[]{:S(2)}, u32[]{:S(2)}) %all-to-all-start.3) | async-done | bytes 2097184 | tf_op jit(solution)/shard_map/all_to_all | solution.py:310
  269.6 3.1 %convolution_convert_fusion = bf16[512,1024]{1,0:T(8,128)(2,1)S(1)} fusion(pred[1024,512]{1,0:T(32,128)(4,1)} %copy-done.24, bf16[1024,1024]{1,0:T(8,128)(2,1)} %bitcast.17), kind=kOutput, calls=%fused_computation.15 | convolution fusion | flops 1074266112 | bytes 3670016 | tf_op jit(solution)/shard_map/dot_general | solution.py:17
  272.8 1.5 collective-permute-start.24
  274.3 1.4 collective-permute-start.26
  276.4 1.5 collective-permute-start.21
  277.9 1.5 collective-permute-start.23
  279.4 2.6 collective-permute-done.24
  282.1 1.5 collective-permute-start.19
  283.5 2.8 finish.5
  286.3 2.3 collective-permute-done.26
  288.6 8.3 %collective-permute-done.25 = bf16[128,1024]{1,0:T(8,128)(2,1)S(1)} collective-permute-done((bf16[128,1024]{1,0:T(8,128)(2,1)S(1)}, bf16[128,1024]{1,0:T(8,128)(2,1)S(1)}, u32[]{:S(2)}, u32[]{:S(2)}) %collective-permute-start.25) | collective-permute-done | bytes 262176 | tf_op jit(solution)/shard_map/ppermute | solution.py:240
  297.8 3.4 %collective-permute-done.21 = bf16[128,1152]{1,0:T(8,128)(2,1)S(1)} collective-permute-done((bf16[128,1152]{1,0:T(8,128)(2,1)S(1)}, bf16[128,1152]{1,0:T(8,128)(2,1)S(1)}, u32[]{:S(2)}, u32[]{:S(2)}) %collective-permute-start.21) | collective-permute-done | bytes 294944 | tf_op jit(solution)/shard_map/ppermute | solution.py:240
  (144 shorter events, 28.2 us)
Async XLA Ops:
  3.2 21.0 %collective-permute-start.2 = (bf16[128,2176]{1,0:T(8,128)(2,1)S(1)}, bf16[128,2176]{1,0:T(8,128)(2,1)S(1)}, u32[]{:S(2)}, u32[]{:S(2)}) collective-permute-start(bf16[128,2176]{1,0:T(8,128)(2,1)S(1)} %fusion.18.refs_0_), channel_id=1, source_target_pairs={{0,24},{8,16},{16,8},{24,0},{1,25},{9,17},{17,9},{25,1},{2,26},{10... | collective-permute-start | bytes 1671176 | tf_op jit(solution)/shard_map/ppermute | solution.py:240
  7.2 24.6 %collective-permute-start.1 = (bf16[128,2176]{1,0:T(8,128)(2,1)S(1)}, bf16[128,2176]{1,0:T(8,128)(2,1)S(1)}, u32[]{:S(2)}, u32[]{:S(2)}) collective-permute-start(bf16[128,2176]{1,0:T(8,128)(2,1)S(1)} %fusion.18.refs_0_), channel_id=1, source_target_pairs={{0,16},{8,24},{16,0},{24,8},{1,17},{9,25},{17,1},{25,9},{2,18},{10... | collective-permute-start | bytes 1671176 | tf_op jit(solution)/shard_map/ppermute | solution.py:240
  7.7 24.3 %collective-permute-start = (bf16[128,2176]{1,0:T(8,128)(2,1)S(1)}, bf16[128,2176]{1,0:T(8,128)(2,1)S(1)}, u32[]{:S(2)}, u32[]{:S(2)}) collective-permute-start(bf16[128,2176]{1,0:T(8,128)(2,1)S(1)} %fusion.18.refs_0_), channel_id=1, source_target_pairs={{0,8},{8,0},{16,24},{24,16},{1,9},{9,1},{17,25},{25,17},{2,10},{10... | collective-permute-start | bytes 1671176 | tf_op jit(solution)/shard_map/ppermute | solution.py:240
  8.0 28.3 %copy-start.37 = (s32[16]{0:T(128)}, s32[16]{0:T(128)S(1)}, u32[]{:S(2)}) copy-start(s32[16]{0:T(128)S(1)} %add.137) | copy-start | bytes 196
  8.0 4.3 %copy-start.28 = (bf16[256,8,768]{2,1,0:T(8,128)(2,1)S(1)}, bf16[256,8,768]{2,1,0:T(8,128)(2,1)}, u32[]{:S(2)}) copy-start(bf16[256,8,768]{2,1,0:T(8,128)(2,1)} %param.11) | copy-start | bytes 9437188
  12.3 2.7 copy-start.29
  17.3 3.2 %copy-start.23 = (bf16[256,8,768]{2,0,1:T(8,128)(2,1)S(1)}, bf16[256,8,768]{2,0,1:T(8,128)(2,1)}, u32[]{:S(2)}) copy-start(bf16[256,8,768]{2,0,1:T(8,128)(2,1)} %copy.57) | copy-start | bytes 9437188
  24.3 78.3 %copy-start.3 = (bf16[128,2176]{1,0:T(8,128)(2,1)}, bf16[128,2176]{1,0:T(8,128)(2,1)S(1)}, u32[]{:S(2)}) copy-start(bf16[128,2176]{1,0:T(8,128)(2,1)S(1)} %collective-permute-done.2.refs_3_) | copy-start | bytes 1671172
  31.8 70.8 %copy-start.4 = (bf16[128,2176]{1,0:T(8,128)(2,1)}, bf16[128,2176]{1,0:T(8,128)(2,1)S(1)}, u32[]{:S(2)}) copy-start(bf16[128,2176]{1,0:T(8,128)(2,1)S(1)} %collective-permute-done.1.refs_2_) | copy-start | bytes 1671172
  32.0 70.5 %copy-start.5 = (bf16[128,2176]{1,0:T(8,128)(2,1)}, bf16[128,2176]{1,0:T(8,128)(2,1)S(1)}, u32[]{:S(2)}) copy-start(bf16[128,2176]{1,0:T(8,128)(2,1)S(1)} %collective-permute-done.refs_1_) | copy-start | bytes 1671172
  32.1 21.8 %collective-permute-start.5 = (bf16[2,256,768]{2,1,0:T(8,128)(2,1)}, bf16[2,256,768]{2,1,0:T(8,128)(2,1)}, u32[]{:S(2)}, u32[]{:S(2)}) collective-permute-start(bf16[2,256,768]{2,1,0:T(8,128)(2,1)} %get-tuple-element.100), channel_id=1, source_target_pairs={{0,24},{8,16},{16,8},{24,0},{1,25},{9,17},{17,9},{25,1},{2,26},{10... | collective-permute-start | bytes 2359304 | tf_op jit(solution)/shard_map/ppermute | solution.py:240
  33.7 35.7 %collective-permute-start.4 = (bf16[2,256,768]{2,1,0:T(8,128)(2,1)}, bf16[2,256,768]{2,1,0:T(8,128)(2,1)}, u32[]{:S(2)}, u32[]{:S(2)}) collective-permute-start(bf16[2,256,768]{2,1,0:T(8,128)(2,1)} %get-tuple-element.98), channel_id=1, source_target_pairs={{0,16},{8,24},{16,0},{24,8},{1,17},{9,25},{17,1},{25,9},{2,18},{10... | collective-permute-start | bytes 2359304 | tf_op jit(solution)/shard_map/ppermute | solution.py:240
  35.1 34.6 %collective-permute-start.3 = (bf16[2,256,768]{2,1,0:T(8,128)(2,1)}, bf16[2,256,768]{2,1,0:T(8,128)(2,1)}, u32[]{:S(2)}, u32[]{:S(2)}) collective-permute-start(bf16[2,256,768]{2,1,0:T(8,128)(2,1)} %get-tuple-element.96), channel_id=1, source_target_pairs={{0,8},{8,0},{16,24},{24,16},{1,9},{9,1},{17,25},{25,17},{2,10},{10... | collective-permute-start | bytes 2359304 | tf_op jit(solution)/shard_map/ppermute | solution.py:240
  36.0 2.4 copy-start.35
  43.1 54.1 %all-to-all-start = ((bf16[8,128,1024]{2,1,0:T(8,128)(2,1)}), bf16[8,128,1024]{2,1,0:T(8,128)(2,1)}, u32[]{:S(2)}, u32[]{:S(2)}) async-start(bf16[8,128,1024]{2,1,0:T(8,128)(2,1)} %bitcast.8), calls=%async_computation | async-start | bytes 4194304 | tf_op jit(solution)/shard_map/all_to_all | solution.py:310
  69.7 34.2 %collective-permute-start.8 = (bf16[2,256,768]{2,1,0:T(8,128)(2,1)}, bf16[2,256,768]{2,1,0:T(8,128)(2,1)}, u32[]{:S(2)}, u32[]{:S(2)}) collective-permute-start(bf16[2,256,768]{2,1,0:T(8,128)(2,1)} %get-tuple-element.113), channel_id=1, source_target_pairs={{0,24},{8,16},{16,8},{24,0},{1,25},{9,17},{17,9},{25,1},{2,26},{10... | collective-permute-start | bytes 2359304 | tf_op jit(solution)/shard_map/ppermute | solution.py:240
  71.1 35.8 %collective-permute-start.7 = (bf16[2,256,768]{2,1,0:T(8,128)(2,1)}, bf16[2,256,768]{2,1,0:T(8,128)(2,1)}, u32[]{:S(2)}, u32[]{:S(2)}) collective-permute-start(bf16[2,256,768]{2,1,0:T(8,128)(2,1)} %get-tuple-element.111), channel_id=1, source_target_pairs={{0,16},{8,24},{16,0},{24,8},{1,17},{9,25},{17,1},{25,9},{2,18},{10... | collective-permute-start | bytes 2359304 | tf_op jit(solution)/shard_map/ppermute | solution.py:240
  72.6 36.1 %collective-permute-start.6 = (bf16[2,256,768]{2,1,0:T(8,128)(2,1)}, bf16[2,256,768]{2,1,0:T(8,128)(2,1)}, u32[]{:S(2)}, u32[]{:S(2)}) collective-permute-start(bf16[2,256,768]{2,1,0:T(8,128)(2,1)} %get-tuple-element.109), channel_id=1, source_target_pairs={{0,8},{8,0},{16,24},{24,16},{1,9},{9,1},{17,25},{25,17},{2,10},{10... | collective-permute-start | bytes 2359304 | tf_op jit(solution)/shard_map/ppermute | solution.py:240
  76.1 1.3 copy-start.2
  97.1 5.4 %copy-start.25 = (pred[1024,512]{1,0:T(32,128)(4,1)S(1)}, pred[1024,512]{1,0:T(32,128)(4,1)}, u32[]{:S(2)}) copy-start(pred[1024,512]{1,0:T(32,128)(4,1)} %copy-done.24) | copy-start | bytes 1572868
  97.2 53.5 %all-to-all-start.1 = ((bf16[8,128,1024]{2,1,0:T(8,128)(2,1)}), bf16[8,128,1024]{2,1,0:T(8,128)(2,1)}, u32[]{:S(2)}, u32[]{:S(2)}) async-start(bf16[8,128,1024]{2,1,0:T(8,128)(2,1)} %bitcast.43), calls=%async_computation.1 | async-start | bytes 4194304 | tf_op jit(solution)/shard_map/all_to_all | solution.py:310
  101.8 2.1 copy-start.33
  101.8 5.1 %copy-start.32 = (bf16[2,256,768]{2,1,0:T(8,128)(2,1)S(1)}, bf16[2,256,768]{2,1,0:T(8,128)(2,1)}, u32[]{:S(2)}) copy-start(bf16[2,256,768]{2,1,0:T(8,128)(2,1)} %get-tuple-element.119) | copy-start | bytes 2359300
  101.8 6.8 %copy-start.31 = (bf16[2,256,768]{2,1,0:T(8,128)(2,1)S(1)}, bf16[2,256,768]{2,1,0:T(8,128)(2,1)}, u32[]{:S(2)}) copy-start(bf16[2,256,768]{2,1,0:T(8,128)(2,1)} %get-tuple-element.117) | copy-start | bytes 2359300
  103.9 21.3 %collective-permute-start.11 = (bf16[2,256,768]{2,1,0:T(8,128)(2,1)S(1)}, bf16[2,256,768]{2,1,0:T(8,128)(2,1)S(1)}, u32[]{:S(2)}, u32[]{:S(2)}) collective-permute-start(bf16[2,256,768]{2,1,0:T(8,128)(2,1)S(1)} %copy-done.33), channel_id=1, source_target_pairs={{0,24},{8,16},{16,8},{24,0},{1,25},{9,17},{17,9},{25,1},{2,26},{10... | collective-permute-start | bytes 2359304 | tf_op jit(solution)/shard_map/ppermute | solution.py:240
  106.9 34.3 %collective-permute-start.10 = (bf16[2,256,768]{2,1,0:T(8,128)(2,1)S(1)}, bf16[2,256,768]{2,1,0:T(8,128)(2,1)S(1)}, u32[]{:S(2)}, u32[]{:S(2)}) collective-permute-start(bf16[2,256,768]{2,1,0:T(8,128)(2,1)S(1)} %copy-done.32), channel_id=1, source_target_pairs={{0,16},{8,24},{16,0},{24,8},{1,17},{9,25},{17,1},{25,9},{2,18},{10... | collective-permute-start | bytes 2359304 | tf_op jit(solution)/shard_map/ppermute | solution.py:240
  108.7 32.6 %collective-permute-start.9 = (bf16[2,256,768]{2,1,0:T(8,128)(2,1)S(1)}, bf16[2,256,768]{2,1,0:T(8,128)(2,1)S(1)}, u32[]{:S(2)}, u32[]{:S(2)}) collective-permute-start(bf16[2,256,768]{2,1,0:T(8,128)(2,1)S(1)} %copy-done.31), channel_id=1, source_target_pairs={{0,8},{8,0},{16,24},{24,16},{1,9},{9,1},{17,25},{25,17},{2,10},{10... | collective-permute-start | bytes 2359304 | tf_op jit(solution)/shard_map/ppermute | solution.py:240
  141.3 1.4 copy-start
  142.7 8.0 %copy-start.1 = (bf16[2,512,768]{2,1,0:T(8,128)(2,1)S(1)}, bf16[2,512,768]{2,1,0:T(8,128)(2,1)}, u32[]{:S(2)}) copy-start(bf16[2,512,768]{2,1,0:T(8,128)(2,1)} %get-tuple-element.114.h_ref.refs_0_) | copy-start | bytes 4718596
  159.1 39.7 %collective-permute-start.12 = (bf16[2,256,768]{2,1,0:T(8,128)(2,1)}, bf16[2,256,768]{2,1,0:T(8,128)(2,1)S(1)}, u32[]{:S(2)}, u32[]{:S(2)}) collective-permute-start(bf16[2,256,768]{2,1,0:T(8,128)(2,1)} %get-tuple-element.125), channel_id=1, source_target_pairs={{0,8},{8,0},{16,24},{24,16},{1,9},{9,1},{17,25},{25,17},{2,10},{10... | collective-permute-start | bytes 2359304 | tf_op jit(solution)/shard_map/ppermute | solution.py:240
  160.6 39.1 %collective-permute-start.13 = (bf16[2,256,768]{2,1,0:T(8,128)(2,1)}, bf16[2,256,768]{2,1,0:T(8,128)(2,1)}, u32[]{:S(2)}, u32[]{:S(2)}) collective-permute-start(bf16[2,256,768]{2,1,0:T(8,128)(2,1)} %get-tuple-element.126), channel_id=1, source_target_pairs={{0,16},{8,24},{16,0},{24,8},{1,17},{9,25},{17,1},{25,9},{2,18},{10... | collective-permute-start | bytes 2359304 | tf_op jit(solution)/shard_map/ppermute | solution.py:240
  161.3 38.4 %collective-permute-start.14 = (bf16[2,256,768]{2,1,0:T(8,128)(2,1)}, bf16[2,256,768]{2,1,0:T(8,128)(2,1)}, u32[]{:S(2)}, u32[]{:S(2)}) collective-permute-start(bf16[2,256,768]{2,1,0:T(8,128)(2,1)} %get-tuple-element.127), channel_id=1, source_target_pairs={{0,24},{8,16},{16,8},{24,0},{1,25},{9,17},{17,9},{25,1},{2,26},{10... | collective-permute-start | bytes 2359304 | tf_op jit(solution)/shard_map/ppermute | solution.py:240
  162.6 4.5 %copy-start.9 = (bf16[2,256,768]{2,1,0:T(8,128)(2,1)S(1)}, bf16[2,256,768]{2,1,0:T(8,128)(2,1)}, u32[]{:S(2)}) copy-start(bf16[2,256,768]{2,1,0:T(8,128)(2,1)} %copy-done.8) | copy-start | bytes 2359300
  162.6 53.6 %all-to-all-start.2 = ((bf16[8,128,1024]{2,1,0:T(8,128)(2,1)}), bf16[8,128,1024]{2,1,0:T(8,128)(2,1)}, u32[]{:S(2)}, u32[]{:S(2)}) async-start(bf16[8,128,1024]{2,1,0:T(8,128)(2,1)} %bitcast.12), calls=%async_computation.2 | async-start | bytes 4194304 | tf_op jit(solution)/shard_map/all_to_all | solution.py:310
  175.6 1.1 copy-start.21
  176.7 1.1 copy-start.22
  199.7 27.6 %collective-permute-start.17 = (bf16[2,256,768]{2,1,0:T(8,128)(2,1)}, bf16[2,256,768]{2,1,0:T(8,128)(2,1)S(1)}, u32[]{:S(2)}, u32[]{:S(2)}) collective-permute-start(bf16[2,256,768]{2,1,0:T(8,128)(2,1)} %get-tuple-element.147), channel_id=1, source_target_pairs={{0,24},{8,16},{16,8},{24,0},{1,25},{9,17},{17,9},{25,1},{2,26},{10... | collective-permute-start | bytes 2359304 | tf_op jit(solution)/shard_map/ppermute | solution.py:240
  201.3 36.6 %collective-permute-start.16 = (bf16[2,256,768]{2,1,0:T(8,128)(2,1)}, bf16[2,256,768]{2,1,0:T(8,128)(2,1)S(1)}, u32[]{:S(2)}, u32[]{:S(2)}) collective-permute-start(bf16[2,256,768]{2,1,0:T(8,128)(2,1)} %get-tuple-element.146), channel_id=1, source_target_pairs={{0,16},{8,24},{16,0},{24,8},{1,17},{9,25},{17,1},{25,9},{2,18},{10... | collective-permute-start | bytes 2359304 | tf_op jit(solution)/shard_map/ppermute | solution.py:240
  202.6 37.7 %collective-permute-start.15 = (bf16[2,256,768]{2,1,0:T(8,128)(2,1)}, bf16[2,256,768]{2,1,0:T(8,128)(2,1)S(1)}, u32[]{:S(2)}, u32[]{:S(2)}) collective-permute-start(bf16[2,256,768]{2,1,0:T(8,128)(2,1)} %get-tuple-element.145), channel_id=1, source_target_pairs={{0,8},{8,0},{16,24},{24,16},{1,9},{9,1},{17,25},{25,17},{2,10},{10... | collective-permute-start | bytes 2359304 | tf_op jit(solution)/shard_map/ppermute | solution.py:240
  216.2 53.4 %all-to-all-start.3 = ((bf16[8,128,1024]{2,1,0:T(8,128)(2,1)}), bf16[8,128,1024]{2,1,0:T(8,128)(2,1)}, u32[]{:S(2)}, u32[]{:S(2)}) async-start(bf16[8,128,1024]{2,1,0:T(8,128)(2,1)} %bitcast.53), calls=%async_computation.3 | async-start | bytes 4194304 | tf_op jit(solution)/shard_map/all_to_all | solution.py:310
  220.8 1.1 copy-start.18
  221.9 1.1 copy-start.20
  223.1 18.9 %copy-start.7 = (bf16[2,256,768]{2,1,0:T(8,128)(2,1)S(1)}, bf16[2,256,768]{2,1,0:T(8,128)(2,1)}, u32[]{:S(2)}) copy-start(bf16[2,256,768]{2,1,0:T(8,128)(2,1)} %copy-done.6) | copy-start | bytes 2359300
  228.2 48.2 %collective-permute-start.22 = (bf16[2,256,768]{2,1,0:T(8,128)(2,1)}, bf16[2,256,768]{2,1,0:T(8,128)(2,1)S(1)}, u32[]{:S(2)}, u32[]{:S(2)}) collective-permute-start(bf16[2,256,768]{2,1,0:T(8,128)(2,1)} %get-tuple-element.158), channel_id=1, source_target_pairs={{0,24},{8,16},{16,8},{24,0},{1,25},{9,17},{17,9},{25,1},{2,26},{10... | collective-permute-start | bytes 2359304 | tf_op jit(solution)/shard_map/ppermute | solution.py:240
  238.8 37.6 %collective-permute-start.20 = (bf16[2,256,768]{2,1,0:T(8,128)(2,1)}, bf16[2,256,768]{2,1,0:T(8,128)(2,1)S(1)}, u32[]{:S(2)}, u32[]{:S(2)}) collective-permute-start(bf16[2,256,768]{2,1,0:T(8,128)(2,1)} %get-tuple-element.155), channel_id=1, source_target_pairs={{0,16},{8,24},{16,0},{24,8},{1,17},{9,25},{17,1},{25,9},{2,18},{10... | collective-permute-start | bytes 2359304 | tf_op jit(solution)/shard_map/ppermute | solution.py:240
  241.2 7.0 %slice-start = ((bf16[128,2176]{1,0:T(8,128)(2,1)}), bf16[128,1024]{1,0:T(8,128)(2,1)S(1)}, s32[]{:S(2)}) async-start(bf16[128,2176]{1,0:T(8,128)(2,1)} %copy-done.3), calls=%async_computation.4 | async-start | bytes 524288 | tf_op jit(solution)/shard_map/slice | solution.py:404
  241.2 7.0 %slice-start.1 = ((bf16[128,2176]{1,0:T(8,128)(2,1)}), bf16[128,1024]{1,0:T(8,128)(2,1)S(1)}, s32[]{:S(2)}) async-start(bf16[128,2176]{1,0:T(8,128)(2,1)} %copy-done.4), calls=%async_computation.5 | async-start | bytes 524288 | tf_op jit(solution)/shard_map/slice | solution.py:404
  241.2 7.0 %slice-start.2 = ((bf16[128,2176]{1,0:T(8,128)(2,1)}), bf16[128,1024]{1,0:T(8,128)(2,1)S(1)}, s32[]{:S(2)}) async-start(bf16[128,2176]{1,0:T(8,128)(2,1)} %copy-done.5), calls=%async_computation.6 | async-start | bytes 524288 | tf_op jit(solution)/shard_map/slice | solution.py:404
  241.2 34.5 %collective-permute-start.18 = (bf16[2,256,768]{2,1,0:T(8,128)(2,1)}, bf16[2,256,768]{2,1,0:T(8,128)(2,1)S(1)}, u32[]{:S(2)}, u32[]{:S(2)}) collective-permute-start(bf16[2,256,768]{2,1,0:T(8,128)(2,1)} %get-tuple-element.152), channel_id=1, source_target_pairs={{0,8},{8,0},{16,24},{24,16},{1,9},{9,1},{17,25},{25,17},{2,10},{10... | collective-permute-start | bytes 2359304 | tf_op jit(solution)/shard_map/ppermute | solution.py:240
  242.0 1.1 copy-start.11
  243.1 1.1 copy-start.13
  244.2 1.1 copy-start.15
  245.4 2.8 copy-start.26
  245.4 2.8 copy-start.34
  248.2 3.0 copy-start.36
  248.2 3.0 copy-start.38
  251.5 3.3 %copy-start.30 = (bf16[1024,512]{1,0:T(8,128)(2,1)S(1)}, bf16[1024,512]{1,0:T(8,128)(2,1)}, u32[]{:S(2)}) copy-start(bf16[1024,512]{1,0:T(8,128)(2,1)} %get-tuple-element.194) | copy-start | bytes 3145732
  272.7 3.6 %copy-start.27 = (bf16[512,1152]{1,0:T(8,128)(2,1)S(1)}, bf16[512,1152]{1,0:T(8,128)(2,1)}, u32[]{:S(2)}) copy-start(bf16[512,1152]{1,0:T(8,128)(2,1)} %fusion.3) | copy-start | bytes 3538948
  272.8 9.3 %collective-permute-start.24 = (bf16[128,1024]{1,0:T(8,128)(2,1)S(1)}, bf16[128,1024]{1,0:T(8,128)(2,1)S(1)}, u32[]{:S(2)}, u32[]{:S(2)}) collective-permute-start(bf16[128,1024]{1,0:T(8,128)(2,1)S(1)} %get-tuple-element.208), channel_id=1, source_target_pairs={{0,8},{8,0},{16,24},{24,16},{1,9},{9,1},{17,25},{25,17},{2,10},{10... | collective-permute-start | bytes 786440 | tf_op jit(solution)/shard_map/ppermute | solution.py:240
  274.3 14.3 %collective-permute-start.26 = (bf16[128,1024]{1,0:T(8,128)(2,1)S(1)}, bf16[128,1024]{1,0:T(8,128)(2,1)S(1)}, u32[]{:S(2)}, u32[]{:S(2)}) collective-permute-start(bf16[128,1024]{1,0:T(8,128)(2,1)S(1)} %get-tuple-element.209), channel_id=1, source_target_pairs={{0,24},{8,16},{16,8},{24,0},{1,25},{9,17},{17,9},{25,1},{2,26},{10... | collective-permute-start | bytes 786440 | tf_op jit(solution)/shard_map/ppermute | solution.py:240
  275.7 21.2 %collective-permute-start.25 = (bf16[128,1024]{1,0:T(8,128)(2,1)S(1)}, bf16[128,1024]{1,0:T(8,128)(2,1)S(1)}, u32[]{:S(2)}, u32[]{:S(2)}) collective-permute-start(bf16[128,1024]{1,0:T(8,128)(2,1)S(1)} %get-tuple-element.210), channel_id=1, source_target_pairs={{0,16},{8,24},{16,0},{24,8},{1,17},{9,25},{17,1},{25,9},{2,18},{10... | collective-permute-start | bytes 786440 | tf_op jit(solution)/shard_map/ppermute | solution.py:240
  276.4 24.8 %collective-permute-start.21 = (bf16[128,1152]{1,0:T(8,128)(2,1)S(1)}, bf16[128,1152]{1,0:T(8,128)(2,1)S(1)}, u32[]{:S(2)}, u32[]{:S(2)}) collective-permute-start(bf16[128,1152]{1,0:T(8,128)(2,1)S(1)} %get-tuple-element.156), channel_id=1, source_target_pairs={{0,16},{8,24},{16,0},{24,8},{1,17},{9,25},{17,1},{25,9},{2,18},{10... | collective-permute-start | bytes 884744 | tf_op jit(solution)/shard_map/ppermute | solution.py:240
  277.9 23.4 %collective-permute-start.23 = (bf16[128,1152]{1,0:T(8,128)(2,1)S(1)}, bf16[128,1152]{1,0:T(8,128)(2,1)S(1)}, u32[]{:S(2)}, u32[]{:S(2)}) collective-permute-start(bf16[128,1152]{1,0:T(8,128)(2,1)S(1)} %get-tuple-element.159), channel_id=1, source_target_pairs={{0,24},{8,16},{16,8},{24,0},{1,25},{9,17},{17,9},{25,1},{2,26},{10... | collective-permute-start | bytes 884744 | tf_op jit(solution)/shard_map/ppermute | solution.py:240
  282.1 19.2 %collective-permute-start.19 = (bf16[128,1152]{1,0:T(8,128)(2,1)S(1)}, bf16[128,1152]{1,0:T(8,128)(2,1)S(1)}, u32[]{:S(2)}, u32[]{:S(2)}) collective-permute-start(bf16[128,1152]{1,0:T(8,128)(2,1)S(1)} %get-tuple-element.153), channel_id=1, source_target_pairs={{0,8},{8,0},{16,24},{24,16},{1,9},{9,1},{17,25},{25,17},{2,10},{10... | collective-permute-start | bytes 884744 | tf_op jit(solution)/shard_map/ppermute | solution.py:240
  (9 other events, 8.1 us)
